TPU v7x, 32 devices: a whole 2x2x4 slice. The times are simulated.
32 devices in a mesh: outer: 1, inner: 32 (over z, y, x, core).
Axes of the slice: x: 2, y: 2, z: 4, core: 2. Of those that a mesh axis runs over, the one named last changes fastest.
Arguments:
- b_leaf: float32 [8192, 64], P(('outer', 'inner')), may hold values from -6 to 6
- b_sep: float32 [256, 64], P(('outer', 'inner')), may hold values from -6 to 6
- b_root: float32 [256, 64], P(('outer', 'inner')), may hold values from -6 to 6
- leaf_linv: float32 [8192, 256], P(('outer', 'inner')), as said below
- leaf_uinv: float32 [8192, 256], P(('outer', 'inner')), as said below
- leaf_lower: float32 [8192, 256], P(('outer', 'inner')), as said below
- leaf_upper: float32 [8192, 256], P(('outer', 'inner')), as said below
- sep_rows: int32 [32, 256], P(('outer', 'inner')), may hold values from 0 to 255, as said below
- sep_linv: float32 [256, 256], P(('outer', 'inner')), as said below
- sep_uinv: float32 [256, 256], P(('outer', 'inner')), as said below
- sep_lower: float32 [256, 256], P(None, ('outer', 'inner')), as said below
- sep_upper: float32 [256, 256], P(('outer', 'inner')), as said below
- root_linv: float32 [256, 256], P(('outer', 'inner')), as said below
- root_uinv: float32 [256, 256], P(('outer', 'inner')), as said below
- basis_leaf: float32 [8192, 512], P(('outer', 'inner')), as said below
- basis_sep: float32 [256, 512], P(('outer', 'inner')), as said below
- basis_root: float32 [256, 512], P(('outer', 'inner')), as said below
- g_blocks: float32 [32768, 128], P(('outer', 'inner')), may hold values from -0.25 to 0.25
- c_blocks: float32 [32768, 128], P(('outer', 'inner')), may hold values from -0.25 to 0.25
- block_cols: int32 [64, 4], P(('outer', 'inner')), may hold values from 0 to 1
Outputs:
- v_leaf: float32 [8192, 64], P(('outer', 'inner'))
- v_sep: float32 [256, 64], P(('outer', 'inner'))
- v_root: float32 [256, 64], P(('outer', 'inner'))
- coefficients: float32 [512, 64], replicated
- reduced_g: float32 [64, 64], replicated
- reduced_c: float32 [64, 64], replicated
Inputs may be any that keep to these rules, and one draw needn't show every extreme that they name: `sep_rows`: each row holds 256 distinct numbers; every row names 0 and 255. `leaf_linv`: lower triangular in each diagonal block of the stack, nonzero diagonal. `leaf_uinv`: upper triangular in each diagonal block of the stack, nonzero diagonal. `sep_linv`: lower triangular in each block of 256 rows, nonzero diagonal. `sep_uinv`: upper triangular in each block of 256 rows, nonzero diagonal. `root_linv`: lower triangular, nonzero diagonal. `root_uinv`: upper triangular, nonzero diagonal. `leaf_lower`: entries of order one over the square root of 256. `leaf_upper`: entries of order one over the square root of 256. `sep_lower`: entries of order one over the square root of the number of its columns. `sep_upper`: entries of order one over the square root of 256. basis_leaf, basis_sep and basis_root stacked by rows form Q with Q^T Q = 8704 I up to float32 rounding. `basis_sep`: part of the stacked Q described with basis_leaf. `basis_root`: part of the stacked Q described with basis_leaf.
All inputs are finite; a program needn't handle non-finite values.
Results may differ from a plain program's by a relative error of at most 0.0003.
Values sent between devices are 32-bit elements; how exact they have to be, the bound alone decides.
No kernel may reach another device: no remote copies, remote signals or barrier semaphores. Data moves between devices by JAX's collectives and lax.ppermute only.
A program may use at most 64 MiB of HBM per device.

v0:
```python
import jax
import jax.numpy as jnp
from jax import lax
from jax.sharding import PartitionSpec as P


def matmul_exact(left, right):
    return jnp.dot(left, right, precision=lax.Precision.HIGHEST, preferred_element_type=jnp.float32)


def contract_rows(left, right):
    return lax.dot_general(
        left,
        right,
        (((0,), (0,)), ((), ())),
        precision=lax.Precision.HIGHEST,
        preferred_element_type=jnp.float32,
    )


def shards(
    b_leaf,
    b_sep,
    b_root,
    leaf_linv,
    leaf_uinv,
    leaf_lower,
    leaf_upper,
    sep_rows,
    sep_linv,
    sep_uinv,
    sep_lower,
    sep_upper,
    root_linv,
    root_uinv,
    basis_leaf,
    basis_sep,
    basis_root,
    g_blocks,
    c_blocks,
    block_cols,
):
    ports = b_leaf.shape[1]
    sep_local = b_sep.shape[0]
    root_local = b_root.shape[0]
    sep_width = sep_linv.shape[1]
    selector = (sep_rows[0][:, None] == jnp.arange(sep_width, dtype=jnp.int32)[None, :]).astype(
        jnp.float32
    )
    y_leaf = matmul_exact(leaf_linv, b_leaf)
    contrib = matmul_exact(leaf_lower, y_leaf)
    t_sep = lax.psum_scatter(
        contract_rows(selector, contrib), "inner", scatter_dimension=0, tiled=True
    )
    sep_whole = lax.all_gather(b_sep - t_sep, "inner", axis=0, tiled=True)
    y_sep = matmul_exact(sep_linv, sep_whole)
    summed = lax.psum(matmul_exact(sep_lower, y_sep), ("outer", "inner"))
    sources = lax.all_gather(b_root, ("outer", "inner"), axis=0, tiled=True)
    y_root = matmul_exact(root_linv, sources - summed)
    y_root_all = lax.all_gather(y_root, ("outer", "inner"), axis=0, tiled=True)
    x_root = matmul_exact(root_uinv, y_root_all)
    x_root_all = lax.all_gather(x_root, ("outer", "inner"), axis=0, tiled=True)
    z_sep = y_sep - matmul_exact(sep_upper, x_root_all)
    z_sep_all = lax.all_gather(z_sep, "inner", axis=0, tiled=True)
    x_sep = matmul_exact(sep_uinv, z_sep_all)
    x_sep_all = lax.all_gather(x_sep, "inner", axis=0, tiled=True)
    coupled = matmul_exact(selector, x_sep_all)
    x_leaf = matmul_exact(leaf_uinv, y_leaf - matmul_exact(leaf_upper, coupled))
    node_count = float(
        lax.axis_size("outer") * lax.axis_size("inner") * (b_leaf.shape[0] + sep_local + root_local)
    )
    pieces_x = (x_leaf, x_sep, x_root)
    pieces_q = (basis_leaf, basis_sep, basis_root)
    projected = (
        contract_rows(basis_leaf, x_leaf)
        + contract_rows(basis_sep, x_sep)
        + contract_rows(basis_root, x_root)
    )
    coefficients = lax.psum(projected, ("outer", "inner")) / node_count
    cleaned = [
        values - matmul_exact(basis, coefficients) for basis, values in zip(pieces_q, pieces_x)
    ]
    local_gram = (
        contract_rows(cleaned[0], cleaned[0])
        + contract_rows(cleaned[1], cleaned[1])
        + contract_rows(cleaned[2], cleaned[2])
    )
    gram_matrix = lax.psum(local_gram, ("outer", "inner")) / node_count
    chol_lower = jnp.linalg.cholesky(gram_matrix)
    inverse_lower = lax.linalg.triangular_solve(
        chol_lower, jnp.eye(ports, dtype=jnp.float32), left_side=True, lower=True
    )
    v_leaf = matmul_exact(cleaned[0], inverse_lower.T)
    v_sep = matmul_exact(cleaned[1], inverse_lower.T)
    v_root = matmul_exact(cleaned[2], inverse_lower.T)
    block_rows = block_cols.shape[0]
    stored = block_cols.shape[1]
    block_size = g_blocks.shape[1]
    blocked = v_leaf.reshape(block_rows, block_size, ports)
    picked = blocked[block_cols]
    g_tiles = g_blocks.reshape(block_rows, stored, block_size, block_size)
    c_tiles = c_blocks.reshape(block_rows, stored, block_size, block_size)
    g_image = jnp.einsum("rwij,rwjp->rip", g_tiles, picked, precision=lax.Precision.HIGHEST)
    c_image = jnp.einsum("rwij,rwjp->rip", c_tiles, picked, precision=lax.Precision.HIGHEST)
    g_local = jnp.einsum("rip,riq->pq", blocked, g_image, precision=lax.Precision.HIGHEST)
    c_local = jnp.einsum("rip,riq->pq", blocked, c_image, precision=lax.Precision.HIGHEST)
    g_summed, c_summed = lax.psum((g_local, c_local), ("outer", "inner"))
    return (v_leaf, v_sep, v_root, coefficients, g_summed / node_count, c_summed / node_count)


def solution(mesh):
    return jax.shard_map(
        shards,
        mesh=mesh,
        in_specs=(
            P(("outer", "inner"), None),
            P(("outer", "inner"), None),
            P(("outer", "inner"), None),
            P(("outer", "inner"), None),
            P(("outer", "inner"), None),
            P(("outer", "inner"), None),
            P(("outer", "inner"), None),
            P(("outer", "inner"), None),
            P(("outer", "inner"), None),
            P(("outer", "inner"), None),
            P(None, ("outer", "inner")),
            P(("outer", "inner"), None),
            P(("outer", "inner"), None),
            P(("outer", "inner"), None),
            P(("outer", "inner"), None),
            P(("outer", "inner"), None),
            P(("outer", "inner"), None),
            P(("outer", "inner"), None),
            P(("outer", "inner"), None),
            P(("outer", "inner"), None),
        ),
        out_specs=(
            P(("outer", "inner"), None),
            P(("outer", "inner"), None),
            P(("outer", "inner"), None),
            P(),
            P(),
            P(),
        ),
        check_vma=False,
    )
```

profile of v0, /device:TPU:0, one launch (start us, length us, event | category | flops | bytes accessed | tf_op | source)
XLA Modules:
  0.0 685.7 jit_solution(16916968704119471954)
XLA Ops:
  7.2 1.4 fusion.17
  8.6 0.4 fusion.18
  9.0 0.7 copy-done.16
  9.7 1.0 fusion.8
  10.8 130.4 %all-reduce.10.cloned.1.call-done = f32[256,64]{1,0:T(8,128)} async-done(((f32[256,64]{1,0:T(8,128)}), f32[256,64]{1,0:T(8,128)}) %all-reduce.10.cloned.1.call-update) | async-done | bytes 65552
  141.3 0.7 dynamic-slice_subtract_fusion
  142.0 40.0 %all_gather.18 = f32[256,64]{1,0:T(8,128)S(1)} all-gather(f32[8,64]{1,0:T(8,128)S(1)} %dynamic-slice_subtract_fusion), channel_id=1, replica_groups=mesh['outer'=1,'inner'=32] {'inner'}, dimensions={0}, use_global_device_ids=true | all-gather | bytes 67584 | tf_op jit(solution)/shard_map/all_gather | solution.py:55
  182.2 0.5 copy-done.11
  182.7 0.9 convolution_bitcast_fusion.3
  183.7 0.6 copy-done.19
  184.3 37.0 %all_gather.19 = f32[256,64]{1,0:T(8,128)S(1)} all-gather(f32[8,64]{1,0:T(8,128)S(1)} %copy-done.18), channel_id=1, replica_groups=mesh['outer'=1,'inner'=32] {'outer','inner'}, dimensions={0}, use_global_device_ids=true | all-gather | bytes 67584 | tf_op jit(solution)/shard_map/all_gather | solution.py:58
  221.4 77.8 %all-reduce.6.cloned.1.call-done = f32[256,64]{0,1:T(8,128)} async-done(((f32[256,64]{0,1:T(8,128)}), f32[256,64]{0,1:T(8,128)}) %all-reduce.6.cloned.1.call-update) | async-done | bytes 65552 | tf_op jit(solution)/shard_map/psum | solution.py:57
  299.2 1.0 convolution_bitcast_fusion.8
  300.2 40.4 %all_gather.20 = f32[256,64]{1,0:T(8,128)S(1)} all-gather(f32[8,64]{1,0:T(8,128)S(1)} %convolution_bitcast_fusion.8), channel_id=1, replica_groups=mesh['outer'=1,'inner'=32] {'outer','inner'}, dimensions={0}, use_global_device_ids=true | all-gather | bytes 67584 | tf_op jit(solution)/shard_map/all_gather | solution.py:60
  340.8 37.0 %all_gather.21 = f32[256,64]{1,0:T(8,128)S(1)} all-gather(f32[8,64]{1,0:T(8,128)S(1)} %bitcast.119), channel_id=1, replica_groups=mesh['outer'=1,'inner'=32] {'outer','inner'}, dimensions={0}, use_global_device_ids=true | all-gather | bytes 67584 | tf_op jit(solution)/shard_map/all_gather | solution.py:62
  377.9 38.3 %all_gather.22 = f32[256,64]{1,0:T(8,128)S(1)} all-gather(f32[8,64]{1,0:T(8,128)S(1)} %fusion.5), channel_id=1, replica_groups=mesh['outer'=1,'inner'=32] {'inner'}, dimensions={0}, use_global_device_ids=true | all-gather | bytes 67584 | tf_op jit(solution)/shard_map/all_gather | solution.py:64
  416.4 37.0 %all_gather.23 = f32[256,64]{1,0:T(8,128)S(1)} all-gather(f32[8,64]{1,0:T(8,128)S(1)} %bitcast.120), channel_id=1, replica_groups=mesh['outer'=1,'inner'=32] {'inner'}, dimensions={0}, use_global_device_ids=true | all-gather | bytes 67584 | tf_op jit(solution)/shard_map/all_gather | solution.py:66
  453.4 0.3 fusion.6
  453.8 0.3 fusion.24
  454.2 0.3 fusion.23
  454.5 0.4 fusion.2
  454.9 0.4 fusion.22
  455.2 1.1 fusion.1
  456.4 122.1 %all-reduce.8.cloned.1.call-done = f32[512,64]{0,1:T(8,128)} async-done(((f32[512,64]{0,1:T(8,128)}), f32[512,64]{0,1:T(8,128)}) %all-reduce.8.cloned.1.call-update) | async-done | bytes 131088 | tf_op jit(solution)/shard_map/psum | solution.py:79
  578.5 0.9 broadcast_multiply_fusion
  579.4 0.6 convolution_subtract_fusion
  580.0 0.2 fusion.4
  580.2 0.2 fusion.3
  580.4 0.2 fusion.25
  580.7 0.2 convolution_add_fusion.2
  580.9 0.2 convolution_add_fusion.1
  581.2 39.4 %psum.37 = f32[64,64]{0,1:T(8,128)S(1)} all-reduce(f32[64,64]{0,1:T(8,128)S(1)} %convolution_add_fusion.1), channel_id=1, replica_groups=mesh['outer'=1,'inner'=32] {'outer','inner'}, use_global_device_ids=true, to_apply=%region_3.0 | all-reduce | flops 4096 | bytes 32768 | tf_op jit(solution)/shard_map/psum | solution.py:88
  620.7 5.8 cholesky.17
  626.6 0.6 compare_reduce_fusion
  627.2 0.7 fusion.13
  627.9 4.9 custom-call.6
  632.8 0.2 fusion.14
  633.0 0.2 fusion.26
  633.3 0.8 fusion.27
  634.0 0.8 fusion.28
  634.8 0.6 gather_fusion
  635.4 0.7 convolution_bitcast_fusion.1
  636.0 0.2 convolution_bitcast_fusion.5
  636.4 0.7 convolution_bitcast_fusion
  637.1 0.2 convolution_bitcast_fusion.4
  637.3 40.4 %all-reduce.1 = (f32[64,64]{0,1:T(8,128)S(1)}, f32[64,64]{0,1:T(8,128)S(1)}) all-reduce(f32[64,64]{0,1:T(8,128)S(1)} %convolution_bitcast_fusion.5, f32[64,64]{0,1:T(8,128)S(1)} %convolution_bitcast_fusion.4), channel_id=1, replica_groups=mesh['outer'=1,'inner'=32] {'outer','inner'}, use_global_device_ids=true, to_apply=%region_6.7 | all-reduce | flops 8192 | bytes 65536 | tf_op jit(solution)/shard_map/psum | solution.py:107
  677.7 0.7 copy.69
  678.4 0.7 copy.70
  (57 shorter events, 1.5 us)
Async XLA Ops:
  7.2 628.2 %copy-start = (f32[1024,128]{1,0:T(8,128)S(1)}, f32[1024,128]{1,0:T(8,128)}, u32[]{:S(2)}) copy-start(f32[1024,128]{1,0:T(8,128)} %param.37) | copy-start | bytes 1572868
  7.2 1.5 copy-start.6
  7.2 134.1 %all-reduce.10.cloned.1.call-start = ((), (), s32[]{:S(2)}) async-start(), calls=%async_computation.2 | async-start | bytes 262144
  9.0 0.7 copy-start.16
  10.8 288.5 %all-reduce.6.cloned.1.call-start = ((), (), s32[]{:S(2)}) async-start(), calls=%async_computation | async-start | bytes 131072 | tf_op jit(solution)/shard_map/psum | solution.py:57
  10.8 130.5 %copy-start.17 = (f32[8,64]{1,0:T(8,128)S(1)}, f32[8,64]{1,0:T(8,128)}, u32[]{:S(2)}) copy-start(f32[8,64]{1,0:T(8,128)} %param.21) | copy-start | bytes 6148
  142.0 40.0 %copy-start.10 = (f32[8,256]{1,0:T(8,128)S(1)}, f32[8,256]{1,0:T(8,128)}, u32[]{:S(2)}) copy-start(f32[8,256]{1,0:T(8,128)} %param.28) | copy-start | bytes 24580
  182.0 0.7 copy-start.11
  183.6 0.7 copy-start.19
  183.6 0.7 copy-start.18
  183.6 394.9 %all-reduce.8.cloned.1.call-start = ((), (), s32[]{:S(2)}) async-start(), calls=%async_computation.1 | async-start | bytes 262144 | tf_op jit(solution)/shard_map/psum | solution.py:79
  221.3 78.0 %copy-start.12 = (f32[8,256]{1,0:T(8,128)S(1)}, f32[8,256]{1,0:T(8,128)}, u32[]{:S(2)}) copy-start(f32[8,256]{1,0:T(8,128)} %param.32) | copy-start | bytes 24580
  300.2 40.4 %copy-start.13 = (f32[8,256]{1,0:T(8,128)S(1)}, f32[8,256]{1,0:T(8,128)}, u32[]{:S(2)}) copy-start(f32[8,256]{1,0:T(8,128)} %param.33) | copy-start | bytes 24580
  340.8 37.0 %copy-start.14 = (f32[8,256]{1,0:T(8,128)S(1)}, f32[8,256]{1,0:T(8,128)}, u32[]{:S(2)}) copy-start(f32[8,256]{1,0:T(8,128)} %param.31) | copy-start | bytes 24580
  377.9 38.3 %copy-start.15 = (f32[8,256]{1,0:T(8,128)S(1)}, f32[8,256]{1,0:T(8,128)}, u32[]{:S(2)}) copy-start(f32[8,256]{1,0:T(8,128)} %param.29) | copy-start | bytes 24580
  416.4 37.3 %copy-start.9 = (f32[8,512]{1,0:T(8,128)S(1)}, f32[8,512]{1,0:T(8,128)}, u32[]{:S(2)}) copy-start(f32[8,512]{1,0:T(8,128)} %param.36) | copy-start | bytes 49156
  453.4 0.7 copy-start.8
  453.4 1.0 copy-start.5
  453.8 1.1 copy-start.7
  454.1 1.1 copy-start.1
  579.4 0.8 copy-start.2
  633.2 3.8 copy-start.3
  635.4 1.0 copy-start.4
Sparse Core Ops, SparseCore 0:
  14.1 127.1 all-reduce.9
  183.7 115.4 all-reduce.5
  456.5 121.9 all-reduce.7
where the time goes:
time: 686 us
  waiting for transfers between devices  330 us (48%)
  blocking collectives  309 us (45%)
  between operations  14.1 us (2%)
  other arithmetic  13.7 us (2%)
  matrix products  13.6 us (2%)
    unnamed x4, waiting for transfers between devices  130 us
    psum x1, waiting for transfers between devices, shards(): coefficients = lax.psum(projected, ('outer', 'inner')) / node_count  122 us
    psum x1, waiting for transfers between devices, shards(): summed = lax.psum(matmul_exact(sep_lower, y_sep), ('outer', 'inner'))  77.8 us
    psum x1, blocking collectives, shards(): g_summed, c_summed = lax.psum((g_local, c_local), ('outer', 'inner'))  40.4 us
    all_gather x1, blocking collectives, shards(): y_root_all = lax.all_gather(y_root, ('outer', 'inner'), axis=0, tiled=True)  40.4 us
    all_gather x1, blocking collectives, shards(): sep_whole = lax.all_gather(b_sep - t_sep, 'inner', axis=0, tiled=True)  40 us
    psum x1, blocking collectives, shards(): gram_matrix = lax.psum(local_gram, ('outer', 'inner')) / node_count  39.4 us
    all_gather x1, blocking collectives, shards(): z_sep_all = lax.all_gather(z_sep, 'inner', axis=0, tiled=True)  38.3 us
  transfers between devices with their start and end apart: 3, of which 3 were waited for; matrix products, arithmetic and copies ran while one was open for 0% of the time, Pallas kernels for 0%

commit v1 on v0

v1 whole, which is shorter than its diff:
```python
import math

import jax
import jax.numpy as jnp
from jax import lax
from jax.sharding import PartitionSpec as P

LANES = 128
REPLICATE_BYTES = 4 << 20


def matmul_exact(left, right):
    return jnp.dot(left, right, precision=lax.Precision.HIGHEST, preferred_element_type=jnp.float32)


def contract_rows(left, right):
    return lax.dot_general(
        left,
        right,
        (((0,), (0,)), ((), ())),
        precision=lax.Precision.HIGHEST,
        preferred_element_type=jnp.float32,
    )


def axis_count(axes):
    return math.prod(lax.axis_size(axis) for axis in axes)


def exchange(blocks, axes):
    return lax.all_to_all(blocks, axes, 0, 0, tiled=True)


def gather_blocks(block, axes):
    count = axis_count(axes)
    return exchange(jnp.broadcast_to(block[None], (count,) + block.shape), axes)


def sum_over(arrays, axes):
    count = axis_count(axes)
    sizes = [array.size for array in arrays]
    flat = jnp.concatenate([array.reshape(-1) for array in arrays])
    depth = -(-flat.size // (count * LANES))
    flat = jnp.pad(flat, (0, count * depth * LANES - flat.size))
    part = exchange(flat.reshape(count, depth, LANES), axes).sum(axis=0)
    whole = gather_blocks(part, axes).reshape(-1)
    results, start = [], 0
    for array, size in zip(arrays, sizes):
        results.append(whole[start : start + size].reshape(array.shape))
        start += size
    return results


def gather_rows(rows, axes):
    count = axis_count(axes)
    bits = count.bit_length() - 1
    if count != 1 << bits:
        return gather_blocks(rows, axes).reshape((-1,) + rows.shape[1:])
    here = lax.axis_index(axes)
    held = rows
    for step, bit in enumerate(reversed(range(bits))):
        pairs = [(source, source ^ (1 << bit)) for source in range(count)]
        other = lax.ppermute(held, axes, pairs)
        upper = ((here >> bit) & 1) == 1
        first = jnp.where(upper, other, held)
        second = jnp.where(upper, held, other)
        held = jnp.stack([first, second], axis=step)
    return held.reshape((-1,) + rows.shape[1:])


def fold_triangles(lower, upper, row_start):
    row = row_start + lax.broadcasted_iota(jnp.int32, lower.shape, 0)
    col = lax.broadcasted_iota(jnp.int32, lower.shape, 1)
    diagonal = jnp.sum(jnp.where(row == col, lower, 0.0), axis=1, keepdims=True)
    return jnp.where(col < row, lower, upper), diagonal


def unfold_triangles(folded, diagonal):
    row = lax.broadcasted_iota(jnp.int32, folded.shape, 0)
    col = lax.broadcasted_iota(jnp.int32, folded.shape, 1)
    lower = jnp.where(col < row, folded, jnp.where(col == row, diagonal, 0.0))
    upper = jnp.where(col >= row, folded, 0.0)
    return lower, upper


def shards(
    b_leaf,
    b_sep,
    b_root,
    leaf_linv,
    leaf_uinv,
    leaf_lower,
    leaf_upper,
    sep_rows,
    sep_linv,
    sep_uinv,
    sep_lower,
    sep_upper,
    root_linv,
    root_uinv,
    basis_leaf,
    basis_sep,
    basis_root,
    g_blocks,
    c_blocks,
    block_cols,
):
    everyone = ("outer", "inner")
    group = ("inner",)
    ports = b_leaf.shape[1]
    sep_local = b_sep.shape[0]
    root_local = b_root.shape[0]
    sep_width = sep_linv.shape[1]
    root_width = root_linv.shape[1]
    in_group = lax.axis_index(group) * sep_local
    in_root = lax.axis_index(everyone) * root_local

    sep_folded, sep_diagonal = fold_triangles(sep_linv, sep_uinv, in_group)
    sep_packed = [sep_folded, jnp.broadcast_to(sep_diagonal, (sep_local, LANES))]
    replicate = 4 * 3 * root_width * root_width <= REPLICATE_BYTES and (
        lax.axis_size("outer") == 1 and sep_local == root_local
    )
    if replicate:
        root_folded, root_diagonal = fold_triangles(root_linv, root_uinv, in_root)
        packed = sep_packed + [
            sep_lower.T,
            sep_upper,
            root_folded,
            jnp.concatenate(
                [b_root, jnp.broadcast_to(root_diagonal, (root_local, ports))], axis=1
            ),
        ]
    else:
        packed = sep_packed
    gathered = gather_rows(jnp.concatenate(packed, axis=1), group)
    pieces, start = [], 0
    for piece in packed:
        pieces.append(gathered[:, start : start + piece.shape[1]])
        start += piece.shape[1]
    sep_lower_tri, sep_upper_tri = unfold_triangles(pieces[0], pieces[1][:, :1])

    selector = (sep_rows[0][:, None] == jnp.arange(sep_width, dtype=jnp.int32)[None, :]).astype(
        jnp.float32
    )
    y_leaf = matmul_exact(leaf_linv, b_leaf)
    contrib = matmul_exact(leaf_lower, y_leaf)
    placed = -contract_rows(selector, contrib)
    own = lax.dynamic_slice(placed, (in_group, 0), (sep_local, ports)) + b_sep
    placed = lax.dynamic_update_slice(placed, own, (in_group, 0))
    (sources,) = sum_over([placed], group)
    y_sep = matmul_exact(sep_lower_tri, sources)
    if replicate:
        lower_all = pieces[2].T
        upper_all = pieces[3]
        root_lower_tri, root_upper_tri = unfold_triangles(pieces[4], pieces[5][:, ports : ports + 1])
        b_root_all = pieces[5][:, :ports]
        y_root = matmul_exact(root_lower_tri, b_root_all - matmul_exact(lower_all, y_sep))
        x_root_all = matmul_exact(root_upper_tri, y_root)
        z_sep = y_sep - matmul_exact(upper_all, x_root_all)
        x_root = lax.dynamic_slice(x_root_all, (in_root, 0), (root_local, ports))
    else:
        count = axis_count(everyone)
        y_own = lax.dynamic_slice(y_sep, (in_group, 0), (sep_local, ports))
        partial = matmul_exact(sep_lower, y_own).reshape(count, root_local, ports)
        sources_root = b_root - exchange(partial, everyone).sum(axis=0)
        whole = gather_blocks(sources_root, everyone).reshape(root_width, ports)
        y_root = matmul_exact(root_linv, whole)
        whole = gather_blocks(y_root, everyone).reshape(root_width, ports)
        x_root = matmul_exact(root_uinv, whole)
        whole = gather_blocks(x_root, everyone).reshape(root_width, ports)
        z_own = y_own - matmul_exact(sep_upper, whole)
        z_sep = gather_blocks(z_own, group).reshape(sep_width, ports)
    x_sep_all = matmul_exact(sep_upper_tri, z_sep)
    x_sep = lax.dynamic_slice(x_sep_all, (in_group, 0), (sep_local, ports))
    coupled = matmul_exact(selector, x_sep_all)
    x_leaf = matmul_exact(leaf_uinv, y_leaf - matmul_exact(leaf_upper, coupled))

    node_count = float(axis_count(everyone) * (b_leaf.shape[0] + sep_local + root_local))
    pieces_x = (x_leaf, x_sep, x_root)
    pieces_q = (basis_leaf, basis_sep, basis_root)
    projected = sum(contract_rows(basis, values) for basis, values in zip(pieces_q, pieces_x))
    (coefficients,) = sum_over([projected], everyone)
    coefficients = coefficients / node_count
    cleaned = [
        values - matmul_exact(basis, coefficients) for basis, values in zip(pieces_q, pieces_x)
    ]
    local_gram = sum(contract_rows(piece, piece) for piece in cleaned)

    block_rows = block_cols.shape[0]
    stored = block_cols.shape[1]
    block_size = g_blocks.shape[1]
    blocked = cleaned[0].reshape(block_rows, block_size, ports)
    picked = (
        block_cols[:, :, None] == jnp.arange(block_rows, dtype=jnp.int32)[None, None, :]
    ).astype(jnp.float32)

    def reduced(blocks):
        tiles = blocks.reshape(block_rows, stored, block_size, block_size)
        dense = jnp.sum(
            picked[:, :, :, None, None] * tiles[:, :, None, :, :], axis=1
        )
        dense = dense.transpose(0, 2, 1, 3).reshape(block_rows * block_size, -1)
        return contract_rows(cleaned[0], matmul_exact(dense, cleaned[0]))

    gram_matrix, g_sum, c_sum = sum_over(
        [local_gram, reduced(g_blocks), reduced(c_blocks)], everyone
    )
    chol_lower = jnp.linalg.cholesky(gram_matrix / node_count)
    inverse_lower = lax.linalg.triangular_solve(
        chol_lower, jnp.eye(ports, dtype=jnp.float32), left_side=True, lower=True
    )
    v_leaf, v_sep, v_root = (matmul_exact(piece, inverse_lower.T) for piece in cleaned)
    g_out = matmul_exact(matmul_exact(inverse_lower, g_sum), inverse_lower.T) / node_count
    c_out = matmul_exact(matmul_exact(inverse_lower, c_sum), inverse_lower.T) / node_count
    return (v_leaf, v_sep, v_root, coefficients, g_out, c_out)


def solution(mesh):
    rows = P(("outer", "inner"), None)
    columns = P(None, ("outer", "inner"))
    return jax.shard_map(
        shards,
        mesh=mesh,
        in_specs=(rows,) * 10 + (columns,) + (rows,) * 9,
        out_specs=(rows, rows, rows, P(), P(), P()),
        check_vma=False,
    )
```

time: 686 us -> 120 us (0.17)
  waiting for transfers between devices: 330 us -> 35 us
  blocking collectives: 309 us -> 32.4 us
  starting transfers between devices: 0.12 us -> 16.9 us
  between operations: 14.1 us -> 1.2 us
    all_gather x6 -> x0, blocking collectives: 230 us -> none  [the longest x1 40.4 us: shards(): y_root_all = lax.all_gather(y_root, ('outer', 'inner'), axis=0, tiled=True)]
    psum x2 -> x0, waiting for transfers between devices: 200 us -> none  [the longest x1 122 us: shards(): coefficients = lax.psum(projected, ('outer', 'inner')) / node_count]
    unnamed x4 -> x0, waiting for transfers between devices: 130 us -> none
    psum x2 -> x0, blocking collectives: 79.8 us -> none  [the longest x1 40.4 us: shards(): g_summed, c_summed = lax.psum((g_local, c_local), ('outer', 'inner'))]
    all_to_all x0 -> x3, blocking collectives: none -> 32.4 us  [exchange(): return lax.all_to_all(blocks, axes, 0, 0, tiled=True)]
    all_to_all x0 -> x3, waiting for transfers between devices: none -> 21.5 us  [exchange(): return lax.all_to_all(blocks, axes, 0, 0, tiled=True)]
    ppermute x0 -> x5, waiting for transfers between devices: none -> 13.5 us  [gather_rows(): other = lax.ppermute(held, axes, pairs)]
    ppermute x0 -> x5, starting transfers between devices: none -> 9.23 us  [gather_rows(): other = lax.ppermute(held, axes, pairs)]
  transfers between devices with their start and end apart: 3 -> 8, of which waited for: 3 -> 7; matrix products, arithmetic and copies ran while one was open for 0% -> 3% of each run, Pallas kernels for 0% -> 0%
where the time goes in v1:
time: 120 us; the launch traced here: 119 us
  waiting for transfers between devices  35 us (29%)
  blocking collectives  32.4 us (27%)
  starting transfers between devices  16.9 us (14%)
  other arithmetic  14 us (12%)
  matrix products  12.3 us (10%)
  local copies, waits for them, and re-layouts  7.5 us (6%)
  between operations  1.2 us (1%)
    all_to_all x3, blocking collectives, exchange(): return lax.all_to_all(blocks, axes, 0, 0, tiled=True)  32.4 us
    all_to_all x3, waiting for transfers between devices, exchange(): return lax.all_to_all(blocks, axes, 0, 0, tiled=True)  21.5 us
    ppermute x5, waiting for transfers between devices, gather_rows(): other = lax.ppermute(held, axes, pairs)  13.5 us
    dot_general x23, matrix products, matmul_exact(): jnp.dot(left, right, precision=lax.Precision.HIGHEST, preferred_element_t...  9.76 us
    ppermute x5, starting transfers between devices, gather_rows(): other = lax.ppermute(held, axes, pairs)  9.23 us
    all_to_all x3, starting transfers between devices, exchange(): return lax.all_to_all(blocks, axes, 0, 0, tiled=True)  7.72 us
    another operation x3, other arithmetic, shards(): chol_lower = jnp.linalg.cholesky(gram_matrix / node_count)  6.52 us
    another operation x2, other arithmetic, shards(): lax.linalg.triangular_solve(chol_lower, jnp.eye(ports, dtype=jnp.float32)...  5.55 us
  transfers between devices with their start and end apart: 8, of which 7 were waited for; matrix products, arithmetic and copies ran while one was open for 3% of the time, Pallas kernels for 0%

profile of v1, /device:TPU:0, one launch (start us, length us, event | category | flops | bytes accessed | tf_op | source)
XLA Modules:
  0.0 119.4 jit_solution(15789476541431602889)
XLA Ops:
  0.7 1.0 select_reduce_fusion.1
  1.9 0.8 concatenate.6
  2.7 4.1 %collective-permute-start = (f32[8,1280]{1,0:T(8,128)S(1)}, f32[8,1280]{1,0:T(8,128)S(1)}, u32[]{:S(2)}, u32[]{:S(2)}) collective-permute-start(f32[8,1280]{1,0:T(8,128)S(1)} %concatenate.6), channel_id=1, source_target_pairs={{0,16},{1,17},{2,18},{3,19},{4,20},{5,21},{6,22},{7,23},{8,24},{9,... | collective-permute-start | bytes 122888 | tf_op jit(solution)/shard_map/ppermute | solution.py:63
  6.7 2.4 %collective-permute-done = f32[8,1280]{1,0:T(8,128)S(1)} collective-permute-done((f32[8,1280]{1,0:T(8,128)S(1)}, f32[8,1280]{1,0:T(8,128)S(1)}, u32[]{:S(2)}, u32[]{:S(2)}) %collective-permute-start) | collective-permute-done | bytes 40992 | tf_op jit(solution)/shard_map/ppermute | solution.py:63
  9.2 1.5 %collective-permute-start.1 = (f32[2,8,1280]{2,1,0:T(8,128)S(1)}, f32[2,8,1280]{2,1,0:T(8,128)S(1)}, u32[]{:S(2)}, u32[]{:S(2)}) collective-permute-start(f32[2,8,1280]{2,1,0:T(8,128)S(1)} %pad_maximum_fusion.4), channel_id=1, source_target_pairs={{0,8},{1,9},{2,10},{3,11},{4,12},{5,13},{6,14},{7,15},{8,0},{9,1},... | collective-permute-start | bytes 245768 | tf_op jit(solution)/shard_map/ppermute | solution.py:63
  10.7 3.0 %collective-permute-done.1 = f32[2,8,1280]{2,1,0:T(8,128)S(1)} collective-permute-done((f32[2,8,1280]{2,1,0:T(8,128)S(1)}, f32[2,8,1280]{2,1,0:T(8,128)S(1)}, u32[]{:S(2)}, u32[]{:S(2)}) %collective-permute-start.1) | collective-permute-done | bytes 81952 | tf_op jit(solution)/shard_map/ppermute | solution.py:63
  13.7 1.8 %collective-permute-start.2 = (f32[2,2,8,1280]{3,2,1,0:T(8,128)S(1)}, f32[2,2,8,1280]{3,2,1,0:T(8,128)S(1)}, u32[]{:S(2)}, u32[]{:S(2)}) collective-permute-start(f32[2,2,8,1280]{3,2,1,0:T(8,128)S(1)} %pad_maximum_fusion.3), channel_id=1, source_target_pairs={{0,4},{1,5},{2,6},{3,7},{4,0},{5,1},{6,2},{7,3},{8,12},{9,13},{10,... | collective-permute-start | bytes 491528 | tf_op jit(solution)/shard_map/ppermute | solution.py:63
  15.5 3.6 %collective-permute-done.2 = f32[2,2,8,1280]{3,2,1,0:T(8,128)S(1)} collective-permute-done((f32[2,2,8,1280]{3,2,1,0:T(8,128)S(1)}, f32[2,2,8,1280]{3,2,1,0:T(8,128)S(1)}, u32[]{:S(2)}, u32[]{:S(2)}) %collective-permute-start.2) | collective-permute-done | bytes 163872 | tf_op jit(solution)/shard_map/ppermute | solution.py:63
  19.2 1.8 %collective-permute-start.3 = (f32[2,2,2,8,1280]{4,3,2,1,0:T(8,128)S(1)}, f32[2,2,2,8,1280]{4,3,2,1,0:T(8,128)S(1)}, u32[]{:S(2)}, u32[]{:S(2)}) collective-permute-start(f32[2,2,2,8,1280]{4,3,2,1,0:T(8,128)S(1)} %pad_maximum_fusion.2), channel_id=1, source_target_pairs={{0,2},{1,3},{2,0},{3,1},{4,6},{5,7},{6,4},{7,5},{8,10},{9,11},{10,... | collective-permute-start | bytes 983048 | tf_op jit(solution)/shard_map/ppermute | solution.py:63
  21.0 0.4 fusion.57
  21.4 0.4 fusion.58
  21.8 4.5 %collective-permute-done.3 = f32[2,2,2,8,1280]{4,3,2,1,0:T(8,128)S(1)} collective-permute-done((f32[2,2,2,8,1280]{4,3,2,1,0:T(8,128)S(1)}, f32[2,2,2,8,1280]{4,3,2,1,0:T(8,128)S(1)}, u32[]{:S(2)}, u32[]{:S(2)}) %collective-permute-start.3) | collective-permute-done | bytes 327712 | tf_op jit(solution)/shard_map/ppermute | solution.py:63
  26.9 0.4 dynamic_update_slice.3
  27.5 13.4 %all_to_all.30 = f32[32,4,128]{2,1,0:T(4,128)S(1)} all-to-all(f32[32,4,128]{2,1,0:T(4,128)S(1)} %reshape.78), channel_id=1, replica_groups=mesh['outer'=1,'inner'=32] {'inner'}, dimensions={0} | all-to-all | bytes 131072 | tf_op jit(solution)/shard_map/all_to_all | solution.py:31
  41.0 0.6 broadcast_in_dim.73
  41.6 2.6 %all-to-all-start.1 = ((f32[32,4,128]{2,1,0:T(4,128)}), f32[32,4,128]{2,1,0:T(4,128)S(1)}, u32[]{:S(2)}, u32[]{:S(2)}) async-start(f32[32,4,128]{2,1,0:T(4,128)} %broadcast_in_dim.73), calls=%async_computation.1 | async-start | bytes 131072 | tf_op jit(solution)/shard_map/all_to_all | solution.py:31
  44.2 7.4 %all-to-all-done.1 = f32[32,4,128]{2,1,0:T(4,128)S(1)} async-done(((f32[32,4,128]{2,1,0:T(4,128)}), f32[32,4,128]{2,1,0:T(4,128)S(1)}, u32[]{:S(2)}, u32[]{:S(2)}) %all-to-all-start.1) | async-done | bytes 65568 | tf_op jit(solution)/shard_map/all_to_all | solution.py:31
  52.3 0.4 fusion.18
  53.1 0.5 fusion.13
  53.5 0.4 fusion.16
  53.9 0.4 convolution_subtract_fusion.1
  54.3 0.4 fusion.21
  55.7 0.4 fusion.2
  56.1 0.4 fusion.59
  56.5 0.4 fusion.1
  57.2 9.9 %all_to_all.31 = f32[32,8,128]{2,1,0:T(8,128)S(1)} all-to-all(f32[32,8,128]{2,1,0:T(8,128)S(1)} %reshape.79), channel_id=1, replica_groups=mesh['outer'=1,'inner'=32] {'outer','inner'}, dimensions={0} | all-to-all | bytes 262144 | tf_op jit(solution)/shard_map/all_to_all | solution.py:31
  67.1 0.7 broadcast_in_dim.76
  67.8 2.6 %all-to-all-start.3 = ((f32[32,8,128]{2,1,0:T(8,128)}), f32[32,8,128]{2,1,0:T(8,128)S(1)}, u32[]{:S(2)}, u32[]{:S(2)}) async-start(f32[32,8,128]{2,1,0:T(8,128)} %broadcast_in_dim.76), calls=%async_computation.3 | async-start | bytes 262144 | tf_op jit(solution)/shard_map/all_to_all | solution.py:31
  71.1 7.5 %all-to-all-done.3 = f32[32,8,128]{2,1,0:T(8,128)S(1)} async-done(((f32[32,8,128]{2,1,0:T(8,128)}), f32[32,8,128]{2,1,0:T(8,128)S(1)}, u32[]{:S(2)}, u32[]{:S(2)}) %all-to-all-start.3) | async-done | bytes 131104 | tf_op jit(solution)/shard_map/all_to_all | solution.py:31
  78.7 0.6 fusion.3
  79.3 0.6 fusion.4
  79.8 0.6 convolution_subtract_fusion
  81.1 0.4 fusion.8
  81.8 0.4 fusion.5
  82.5 9.1 %all_to_all.32 = f32[32,3,128]{2,1,0:T(4,128)S(1)} all-to-all(f32[32,3,128]{2,1,0:T(4,128)S(1)} %reshape.85), channel_id=1, replica_groups=mesh['outer'=1,'inner'=32] {'outer','inner'}, dimensions={0} | all-to-all | bytes 98304 | tf_op jit(solution)/shard_map/all_to_all | solution.py:31
  91.6 0.6 broadcast_in_dim.77
  92.3 2.6 %all-to-all-start.5 = ((f32[32,3,128]{2,1,0:T(4,128)}), f32[32,3,128]{2,1,0:T(4,128)S(1)}, u32[]{:S(2)}, u32[]{:S(2)}) async-start(f32[32,3,128]{2,1,0:T(4,128)} %broadcast_in_dim.77), calls=%async_computation.5 | async-start | bytes 131072 | tf_op jit(solution)/shard_map/all_to_all | solution.py:31
  94.8 0.8 copy.66
  95.6 6.6 %all-to-all-done.5 = f32[32,3,128]{2,1,0:T(4,128)S(1)} async-done(((f32[32,3,128]{2,1,0:T(4,128)}), f32[32,3,128]{2,1,0:T(4,128)S(1)}, u32[]{:S(2)}, u32[]{:S(2)}) %all-to-all-start.5) | async-done | bytes 49184 | tf_op jit(solution)/shard_map/all_to_all | solution.py:31
  102.5 5.8 %cholesky.17 = f32[64,64]{1,0:T(8,128)S(1)} custom-call(f32[64,64]{1,0:T(8,128)S(1)} %fusion.43), custom_call_target="Cholesky" | custom-call | tf_op jit(solution)/shard_map/jit(cholesky)/cholesky | solution.py:208
  108.4 0.6 compare_reduce_fusion
  109.1 0.7 fusion.36
  109.7 4.9 %custom-call.6 = f32[1,64,64]{1,2,0:T(8,128)S(1)} custom-call(f32[1,64,64]{2,1,0:T(8,128)S(1)} %fusion.36), custom_call_target="InvertDiagBlocksLowerTriangular" | custom-call | tf_op jit(solution)/shard_map/triangular_solve | solution.py:209
  115.2 0.8 fusion.65
  116.0 0.8 fusion.64
  116.8 0.8 fusion.63
  117.8 0.7 copy.68
  118.7 0.7 copy.67
  (87 shorter events, 6.6 us)
Async XLA Ops:
  0.6 55.8 %copy-start = (f32[256,512]{1,0:T(8,128)S(1)}, f32[256,512]{1,0:T(8,128)}, u32[]{:S(2)}) copy-start(f32[256,512]{1,0:T(8,128)} %param.34) | copy-start | bytes 1572868
  0.6 20.3 %copy-start.7 = (f32[256,64]{0,1:T(8,128)S(1)}, f32[256,64]{0,1:T(8,128)}, u32[]{:S(2)}) copy-start(f32[256,64]{0,1:T(8,128)} %param.20) | copy-start | bytes 196612
  0.7 20.3 %copy-start.4 = (f32[256,256]{1,0:T(8,128)S(1)}, f32[256,256]{1,0:T(8,128)}, u32[]{:S(2)}) copy-start(f32[256,256]{1,0:T(8,128)} %param.23) | copy-start | bytes 786436
  2.7 6.5 %collective-permute-start = (f32[8,1280]{1,0:T(8,128)S(1)}, f32[8,1280]{1,0:T(8,128)S(1)}, u32[]{:S(2)}, u32[]{:S(2)}) collective-permute-start(f32[8,1280]{1,0:T(8,128)S(1)} %concatenate.6), channel_id=1, source_target_pairs={{0,16},{1,17},{2,18},{3,19},{4,20},{5,21},{6,22},{7,23},{8,24},{9,... | collective-permute-start | bytes 122888 | tf_op jit(solution)/shard_map/ppermute | solution.py:63
  9.2 12.2 %copy-start.11 = (f32[8,64]{1,0:T(8,128)S(1)}, f32[8,64]{1,0:T(8,128)}, u32[]{:S(2)}) copy-start(f32[8,64]{1,0:T(8,128)} %param.21) | copy-start | bytes 6148
  9.2 12.3 %copy-start.5 = (f32[256,256]{1,0:T(8,128)S(1)}, f32[256,256]{1,0:T(8,128)}, u32[]{:S(2)}) copy-start(f32[256,256]{1,0:T(8,128)} %param.25) | copy-start | bytes 786436
  9.2 4.5 %collective-permute-start.1 = (f32[2,8,1280]{2,1,0:T(8,128)S(1)}, f32[2,8,1280]{2,1,0:T(8,128)S(1)}, u32[]{:S(2)}, u32[]{:S(2)}) collective-permute-start(f32[2,8,1280]{2,1,0:T(8,128)S(1)} %pad_maximum_fusion.4), channel_id=1, source_target_pairs={{0,8},{1,9},{2,10},{3,11},{4,12},{5,13},{6,14},{7,15},{8,0},{9,1},... | collective-permute-start | bytes 245768 | tf_op jit(solution)/shard_map/ppermute | solution.py:63
  13.7 5.4 %collective-permute-start.2 = (f32[2,2,8,1280]{3,2,1,0:T(8,128)S(1)}, f32[2,2,8,1280]{3,2,1,0:T(8,128)S(1)}, u32[]{:S(2)}, u32[]{:S(2)}) collective-permute-start(f32[2,2,8,1280]{3,2,1,0:T(8,128)S(1)} %pad_maximum_fusion.3), channel_id=1, source_target_pairs={{0,4},{1,5},{2,6},{3,7},{4,0},{5,1},{6,2},{7,3},{8,12},{9,13},{10,... | collective-permute-start | bytes 491528 | tf_op jit(solution)/shard_map/ppermute | solution.py:63
  19.2 7.1 %collective-permute-start.3 = (f32[2,2,2,8,1280]{4,3,2,1,0:T(8,128)S(1)}, f32[2,2,2,8,1280]{4,3,2,1,0:T(8,128)S(1)}, u32[]{:S(2)}, u32[]{:S(2)}) collective-permute-start(f32[2,2,2,8,1280]{4,3,2,1,0:T(8,128)S(1)} %pad_maximum_fusion.2), channel_id=1, source_target_pairs={{0,2},{1,3},{2,0},{3,1},{4,6},{5,7},{6,4},{7,5},{8,10},{9,11},{10,... | collective-permute-start | bytes 983048 | tf_op jit(solution)/shard_map/ppermute | solution.py:63
  21.8 4.7 %copy-start.10 = (s32[1,256]{1,0:T(1,128)S(1)}, s32[1,256]{1,0:T(1,128)}, u32[]{:S(2)}) copy-start(s32[1,256]{1,0:T(1,128)} %param.27) | copy-start | bytes 3076
  26.4 25.3 %collective-permute-start.4 = (f32[2,2,2,2,8,1280]{5,4,3,2,1,0:T(8,128)S(1)}, f32[2,2,2,2,8,1280]{5,4,3,2,1,0:T(8,128)S(1)}, u32[]{:S(2)}, u32[]{:S(2)}) collective-permute-start(f32[2,2,2,2,8,1280]{5,4,3,2,1,0:T(8,128)S(1)} %pad_maximum_fusion.1), channel_id=1, source_target_pairs={{0,1},{1,0},{2,3},{3,2},{4,5},{5,4},{6,7},{7,6},{8,9},{9,8},{10,11... | collective-permute-start | bytes 1966088 | tf_op jit(solution)/shard_map/ppermute | solution.py:63
  41.6 10.0 %all-to-all-start.1 = ((f32[32,4,128]{2,1,0:T(4,128)}), f32[32,4,128]{2,1,0:T(4,128)S(1)}, u32[]{:S(2)}, u32[]{:S(2)}) async-start(f32[32,4,128]{2,1,0:T(4,128)} %broadcast_in_dim.73), calls=%async_computation.1 | async-start | bytes 131072 | tf_op jit(solution)/shard_map/all_to_all | solution.py:31
  52.3 2.7 %copy-start.9 = (f32[8,512]{1,0:T(8,128)S(1)}, f32[8,512]{1,0:T(8,128)}, u32[]{:S(2)}) copy-start(f32[8,512]{1,0:T(8,128)} %param.35) | copy-start | bytes 49156
  52.8 2.6 %copy-start.8 = (f32[8,512]{1,0:T(8,128)S(1)}, f32[8,512]{1,0:T(8,128)}, u32[]{:S(2)}) copy-start(f32[8,512]{1,0:T(8,128)} %param.36) | copy-start | bytes 49156
  52.8 2.9 %copy-start.3 = (f32[256,256]{1,0:T(8,128)S(1)}, f32[256,256]{1,0:T(8,128)}, u32[]{:S(2)}) copy-start(f32[256,256]{1,0:T(8,128)} %param.26) | copy-start | bytes 786436
  53.1 3.0 %copy-start.6 = (f32[256,256]{1,0:T(8,128)S(1)}, f32[256,256]{1,0:T(8,128)}, u32[]{:S(2)}) copy-start(f32[256,256]{1,0:T(8,128)} %param.24) | copy-start | bytes 786436
  56.4 13.9 %copy-start.12 = (s32[2,4]{1,0:T(2,128)S(1)}, s32[2,4]{1,0:T(2,128)}, u32[]{:S(2)}) copy-start(s32[2,4]{1,0:T(2,128)} %param.39) | copy-start | bytes 100
  56.4 14.0 %copy-start.1 = (f32[1024,128]{1,0:T(8,128)S(1)}, f32[1024,128]{1,0:T(8,128)}, u32[]{:S(2)}) copy-start(f32[1024,128]{1,0:T(8,128)} %param.37) | copy-start | bytes 1572868
  56.5 14.0 %copy-start.2 = (f32[1024,128]{1,0:T(8,128)S(1)}, f32[1024,128]{1,0:T(8,128)}, u32[]{:S(2)}) copy-start(f32[1024,128]{1,0:T(8,128)} %param.38) | copy-start | bytes 1572868
  67.8 10.8 %all-to-all-start.3 = ((f32[32,8,128]{2,1,0:T(8,128)}), f32[32,8,128]{2,1,0:T(8,128)S(1)}, u32[]{:S(2)}, u32[]{:S(2)}) async-start(f32[32,8,128]{2,1,0:T(8,128)} %broadcast_in_dim.76), calls=%async_computation.3 | async-start | bytes 262144 | tf_op jit(solution)/shard_map/all_to_all | solution.py:31
  92.3 10.0 %all-to-all-start.5 = ((f32[32,3,128]{2,1,0:T(4,128)}), f32[32,3,128]{2,1,0:T(4,128)S(1)}, u32[]{:S(2)}, u32[]{:S(2)}) async-start(f32[32,3,128]{2,1,0:T(4,128)} %broadcast_in_dim.77), calls=%async_computation.5 | async-start | bytes 131072 | tf_op jit(solution)/shard_map/all_to_all | solution.py:31

commit v2 on v0

v2 whole, which is shorter than its diff:
```python
import functools
import math

import jax
import jax.numpy as jnp
from jax import lax
from jax.experimental import pallas as pl
from jax.experimental.pallas import tpu as pltpu
from jax.sharding import PartitionSpec as P


LANES = 128
SUBLANES = 8
REPLICATE_BYTES = 4 << 20
VMEM_BYTES = 12 << 20
HOP_BITS = 2
EVERYONE = ("outer", "inner")
GROUP = ("inner",)
WHOLE = pl.BlockSpec(memory_space=pltpu.VMEM)
SCALAR = pl.BlockSpec(memory_space=pltpu.SMEM)


def contract(left, right, left_dim, right_dim, precision=lax.Precision.HIGHEST):
    return lax.dot_general(
        left,
        right,
        (((left_dim,), (right_dim,)), ((), ())),
        precision=precision,
        preferred_element_type=jnp.float32,
    )


def parts_of(value):
    high = value.astype(jnp.bfloat16)
    rest = value - high.astype(jnp.float32)
    middle = rest.astype(jnp.bfloat16)
    return high, middle, (rest - middle.astype(jnp.float32)).astype(jnp.bfloat16)


def dot_parts(left, right, right_dim):
    rows = left.shape[0]
    high, middle, low = parts_of(left)
    first, second, third = parts_of(right)
    three = contract(jnp.concatenate([high, middle, low], axis=0), first, 1, right_dim, None)
    two = contract(jnp.concatenate([high, middle], axis=0), second, 1, right_dim, None)
    one = contract(high, third, 1, right_dim, None)
    small = three[2 * rows :] + two[rows:] + one
    return three[:rows] + ((three[rows : 2 * rows] + two[:rows]) + small)


def dot_nn(left, right):
    return dot_parts(left, right, 0)


def dot_nt(left, right):
    return dot_parts(left, right, 1)


def dot_tn(left, right):
    return contract(left, right, 0, 0)


def axis_count(axes):
    return math.prod(lax.axis_size(axis) for axis in axes)


def shape_of(*dims):
    return jax.ShapeDtypeStruct(dims, jnp.float32)


def call(body, outs, operands, scalars=0, flops=0, limit=VMEM_BYTES):
    specs = [SCALAR] * scalars + [WHOLE] * (len(operands) - scalars)
    moved = sum(4 * operand.size for operand in operands) + sum(
        4 * math.prod(out.shape) for out in outs
    )
    return pl.pallas_call(
        body,
        out_shape=outs,
        in_specs=specs,
        out_specs=[WHOLE] * len(outs),
        compiler_params=pltpu.CompilerParams(vmem_limit_bytes=limit),
        cost_estimate=pl.CostEstimate(flops=flops, bytes_accessed=moved, transcendentals=0),
    )(*operands)


def iota(shape, dim):
    return lax.broadcasted_iota(jnp.int32, shape, dim)


def halves_up(wide):
    count = wide.shape[1] // LANES
    return jnp.concatenate(
        [wide[:, LANES * at : LANES * (at + 1)] for at in range(count)], axis=0
    )


def halves_down(tall, rows):
    count = tall.shape[0] // rows
    return jnp.concatenate([tall[rows * at : rows * (at + 1)] for at in range(count)], axis=1)


def exchange(blocks, axes):
    return lax.all_to_all(blocks, axes, 0, 0, tiled=True)


def gather_blocks(block, axes):
    count = axis_count(axes)
    return exchange(jnp.broadcast_to(block[None], (count,) + block.shape), axes)


def spread_kernel(scale, in_ref, out_ref):
    total = jnp.sum(in_ref[...], axis=0) * scale
    out_ref[...] = jnp.broadcast_to(total[None], out_ref.shape)


def sum_over(tall, axes, scale=1.0):
    count = axis_count(axes)
    size = tall.size
    depth = -(-size // (count * LANES))
    blocks = tall
    if size != count * depth * LANES:
        blocks = jnp.pad(tall.reshape(-1), (0, count * depth * LANES - size))
    blocks = blocks.reshape(count, depth, LANES)
    received = exchange(blocks, axes)
    (spread,) = call(
        functools.partial(spread_kernel, scale), [shape_of(count, depth, LANES)], [received]
    )
    whole = exchange(spread, axes)
    if size != count * depth * LANES:
        whole = whole.reshape(-1)[:size]
    return whole.reshape(tall.shape)


def swap_by_bits(blocks, position):
    size, bit = len(blocks), 0
    while 1 << bit < size:
        flip = ((position >> bit) & 1) == 1
        blocks = [
            jnp.where(flip, blocks[slot ^ (1 << bit)], blocks[slot]) for slot in range(size)
        ]
        bit += 1
    return blocks


def gather_rows(rows, axes):
    count = axis_count(axes)
    bits = count.bit_length() - 1
    here = lax.axis_index(axes)
    held = rows
    low = bits
    stage = 0
    while low > 1:
        width = min(HOP_BITS, low - 1)
        low -= width
        blocks = [held]
        for pattern in range(1, 1 << width):
            pairs = [(source, source ^ (pattern << low)) for source in range(count)]
            blocks.append(lax.ppermute(held, axes, pairs))
        held = jnp.stack(swap_by_bits(blocks, here >> low), axis=stage)
        stage += 1
    pairs = [(source, source ^ 1) for source in range(count)]
    other = lax.ppermute(held, axes, pairs)
    shape = (-1,) + rows.shape[1:]
    return held.reshape(shape), other.reshape(shape)


def leaf_kernel(at_ref, b_ref, linv_ref, lower_ref, rows_ref, b_sep_ref, y_ref, sources_ref):
    y_leaf = dot_nt(b_ref[...], linv_ref[...])
    y_ref[...] = y_leaf
    contrib = dot_nt(y_leaf, lower_ref[...])
    width = sources_ref.shape[0] // b_ref.shape[0] * LANES
    extent = rows_ref.shape[1]
    hits = iota((width, extent), 0) == rows_ref[...]
    placed = dot_nt(contrib, hits.astype(jnp.float32))
    own_rows = b_sep_ref.shape[0]
    own = iota((own_rows, width), 1) == iota((own_rows, width), 0) + at_ref[0]
    sources = dot_tn(b_sep_ref[...], own.astype(jnp.float32)) - placed
    sources_ref[...] = halves_up(sources)


def pack_kernel(
    at_ref, sl_ref, su_ref, lower_ref, upper_ref, rl_ref, ru_ref, b_root_ref, out_ref
):
    rows, width = sl_ref.shape
    own = iota((rows, width), 0) + at_ref[0]
    col = iota((rows, width), 1)

    def fold(lower, upper):
        diagonal = jnp.sum(jnp.where(col == own, lower, 0.0), axis=1, keepdims=True)
        return jnp.where(col < own, lower, upper), diagonal

    sep, sep_diagonal = fold(sl_ref[...], su_ref[...])
    root, root_diagonal = fold(rl_ref[...], ru_ref[...])
    out_ref[:, :width] = sep
    out_ref[:, width : 2 * width] = lower_ref[...]
    out_ref[:, 2 * width : 3 * width] = upper_ref[...]
    out_ref[:, 3 * width : 4 * width] = root
    ports = b_root_ref.shape[1]
    quarter = (LANES - ports) // 2
    out_ref[:, 4 * width :] = jnp.concatenate(
        [
            b_root_ref[...],
            jnp.broadcast_to(sep_diagonal, (rows, quarter)),
            jnp.broadcast_to(root_diagonal, (rows, quarter)),
        ],
        axis=1,
    )


def solve_kernel(
    at_ref,
    sources_ref,
    mine_ref,
    other_ref,
    y_ref,
    rows_ref,
    leaf_upper_ref,
    leaf_uinv_ref,
    q_leaf_ref,
    q_sep_ref,
    q_root_ref,
    x_ref,
    partial_ref,
):
    ports, extent = y_ref.shape
    own_rows = q_sep_ref.shape[0]
    width = 2 * mine_ref.shape[0]
    odd = (at_ref[0] // own_rows) % 2 == 1

    def piece(start, size):
        blocks = []
        for at in range(mine_ref.shape[0] // own_rows):
            mine = mine_ref[own_rows * at : own_rows * (at + 1), start : start + size]
            other = other_ref[own_rows * at : own_rows * (at + 1), start : start + size]
            blocks.append(jnp.where(odd, other, mine))
            blocks.append(jnp.where(odd, mine, other))
        return jnp.concatenate(blocks, axis=0)

    row = iota((width, width), 0)
    col = iota((width, width), 1)

    def unfold(folded, diagonal):
        lower = jnp.where(col < row, folded, jnp.where(col == row, diagonal, 0.0))
        return lower, jnp.where(col >= row, folded, 0.0)

    extra = piece(4 * width, LANES)
    quarter = (LANES - ports) // 2
    sep_l, sep_u = unfold(piece(0, width), extra[:, ports : ports + 1])
    root_l, root_u = unfold(
        piece(3 * width, width), extra[:, ports + quarter : ports + quarter + 1]
    )
    b_root = extra.T[:ports]
    sources = halves_down(sources_ref[...], ports)
    y_sep = dot_nt(sources, sep_l)
    y_root = dot_nt(b_root - dot_nn(y_sep, piece(width, width)), root_l)
    x_root = dot_nt(y_root, root_u)
    x_sep = dot_nt(y_sep - dot_nt(x_root, piece(2 * width, width)), sep_u)
    hits = (iota((width, extent), 0) == rows_ref[...]).astype(jnp.float32)
    coupled = dot_nn(x_sep, hits)
    x_leaf = dot_nt(y_ref[...] - dot_nt(coupled, leaf_upper_ref[...]), leaf_uinv_ref[...])
    own = iota((LANES, width), 1) - at_ref[0] == iota((LANES, width), 0)
    own = own & (iota((LANES, width), 0) < own_rows)
    shifted = iota((LANES, width), 1) - at_ref[0] == iota((LANES, width), 0) - own_rows
    shifted = shifted & (iota((LANES, width), 0) >= own_rows)
    shifted = shifted & (iota((LANES, width), 0) < 2 * own_rows)
    x_own = dot_nt(x_sep, own.astype(jnp.float32)) + dot_nt(x_root, shifted.astype(jnp.float32))
    x_ref[:, :extent] = x_leaf
    x_ref[:, extent:] = x_own
    q_own = jnp.concatenate([q_sep_ref[...], q_root_ref[...]], axis=0)
    partial = dot_nn(x_leaf, q_leaf_ref[...]) + dot_nn(x_own[:, : 2 * own_rows], q_own)
    partial_ref[...] = halves_up(partial)


def dense_kernel(cols_ref, g_ref, c_ref, g_out_ref, c_out_ref):
    block_rows, stored = cols_ref.shape
    size = g_ref.shape[1]
    for blocks_ref, out_ref in ((g_ref, g_out_ref), (c_ref, c_out_ref)):
        for row in range(block_rows):
            for col in range(block_rows):
                total = jnp.zeros((size, size), jnp.float32)
                for slot in range(stored):
                    start = (row * stored + slot) * size
                    block = blocks_ref[start : start + size, :]
                    total = total + jnp.where(cols_ref[row, slot] == col, block, 0.0)
                out_ref[size * row : size * (row + 1), size * col : size * (col + 1)] = total


def clean_kernel(
    coef_ref, x_ref, q_leaf_ref, q_sep_ref, q_root_ref, g_ref, c_ref, coef_out, clean_out, out_ref
):
    ports, extent = x_ref.shape[0], q_leaf_ref.shape[0]
    coef = halves_down(coef_ref[...], ports)
    coef_out[...] = coef
    leaf = x_ref[:, :extent] - dot_nt(coef, q_leaf_ref[...])
    q_own = jnp.concatenate([q_sep_ref[...], q_root_ref[...]], axis=0)
    pad = LANES - q_own.shape[0]
    q_own = jnp.concatenate([q_own, jnp.zeros((pad, q_own.shape[1]), jnp.float32)], axis=0)
    own = x_ref[:, extent:] - dot_nt(coef, q_own)
    clean_out[:, :extent] = leaf
    clean_out[:, extent:] = own
    g_image = dot_nt(leaf, g_ref[...])
    c_image = dot_nt(leaf, c_ref[...])
    products = dot_nt(leaf, jnp.concatenate([leaf, g_image, c_image], axis=0))
    gram = products[:, :ports] + dot_nt(own, own)
    out_ref[:ports, :] = jnp.concatenate([gram, products[:, ports : 2 * ports]], axis=1)
    out_ref[ports:, :] = jnp.concatenate(
        [products[:, 2 * ports :], jnp.zeros((ports, LANES - ports), jnp.float32)], axis=1
    )


def eliminate(tiles, offset, step):
    shape = tiles[0].shape
    rows = iota(shape, 0)
    tiles = list(tiles)

    def whole_row(tile, at):
        return jnp.broadcast_to(tile[at : at + 1, :], shape)

    def whole_col(tile, at):
        return jnp.broadcast_to(tile[:, at : at + 1], shape)

    for first in range(0, len(tiles) * SUBLANES, step):
        top, base = divmod(first, SUBLANES)
        pivots = [whole_row(tiles[top], base + t) for t in range(step)]
        columns = [
            [whole_col(tile, offset + first + t) for tile in tiles[top:]] for t in range(step)
        ]
        corner = [[whole_row(columns[u][0], base + t) for u in range(step)] for t in range(step)]
        factors = []
        for t in range(step):
            inverse = 1.0 / corner[t][t]
            for u in range(t + 1, step):
                ratio = corner[u][t] * inverse
                pivots[u] = pivots[u] - ratio * pivots[t]
                for v in range(t + 1, step):
                    corner[u][v] = corner[u][v] - ratio * corner[t][v]
            factor = [column * inverse for column in columns[t]]
            for v in range(t + 1, step):
                columns[v] = [c - f * corner[t][v] for c, f in zip(columns[v], factor)]
            factor[0] = jnp.where(rows > base + t, factor[0], 0.0)
            factors.append(factor)
        for at in range(top, len(tiles)):
            value = tiles[at]
            for t in range(step):
                value = value - factors[t][at - top] * pivots[t]
            tiles[at] = value
    return tiles


def tail_kernel(
    sums_ref, clean_ref, v_leaf_ref, v_sep_ref, v_root_ref, g_ref, c_ref
):
    ports = clean_ref.shape[0]
    extent = v_leaf_ref.shape[1]
    own_rows = v_sep_ref.shape[0]
    diagonal = iota((ports, ports), 0) == iota((ports, ports), 1)
    gram = sums_ref[:ports, :ports]
    joined = jnp.concatenate([jnp.where(diagonal, 1.0, 0.0), gram], axis=1)
    tiles = [joined[at : at + SUBLANES] for at in range(0, ports, SUBLANES)]
    joined = jnp.concatenate(eliminate(tiles, ports, SUBLANES), axis=0)
    pivots = jnp.sum(jnp.where(diagonal, joined[:, ports:], 0.0), axis=1, keepdims=True)
    inverse = joined[:, :ports] / jnp.sqrt(pivots)
    v_leaf_ref[...] = dot_nn(inverse, clean_ref[:, :extent])
    own = dot_nn(inverse, clean_ref[:, extent:]).T
    v_sep_ref[...] = own[:own_rows]
    v_root_ref[...] = own[own_rows : 2 * own_rows]
    g_sum = sums_ref[:ports, ports : 2 * ports]
    c_sum = sums_ref[ports:, :ports]
    g_ref[...] = dot_nt(dot_nn(inverse, g_sum), inverse)
    c_ref[...] = dot_nt(dot_nn(inverse, c_sum), inverse)


def solve_replicated(at, sources, b_root, factors, leaf, bases):
    sep_linv, sep_uinv, sep_lower, sep_upper, root_linv, root_uinv = factors
    ports, extent = leaf[0].shape
    sep_local, sep_width = sep_linv.shape
    basis = bases[0].shape[1]
    (packed,) = call(
        pack_kernel,
        [shape_of(sep_local, 4 * sep_width + LANES)],
        [at, sep_linv, sep_uinv, sep_lower.T, sep_upper, root_linv, root_uinv, b_root],
        scalars=1,
    )
    mine, other = gather_rows(packed, GROUP)
    return call(
        solve_kernel,
        [shape_of(ports, extent + LANES), shape_of(basis // LANES * ports, LANES)],
        [at, sources, mine, other, *leaf, *bases],
        scalars=1,
        flops=22 * extent * extent * ports,
    )


def solve_spread(at, sources, b_root, factors, leaf, bases):
    sep_linv, sep_uinv, sep_lower, sep_upper, root_linv, root_uinv = factors
    y_leaf, sep_rows, leaf_upper, leaf_uinv = leaf
    ports = y_leaf.shape[0]
    sep_local, sep_width = sep_linv.shape
    root_local, root_width = root_linv.shape
    row = iota((sep_local, sep_width), 0) + at[0]
    col = iota((sep_local, sep_width), 1)
    diagonal = jnp.sum(jnp.where(row == col, sep_linv, 0.0), axis=1, keepdims=True)
    folded = jnp.concatenate(
        [jnp.where(col < row, sep_linv, sep_uinv), jnp.broadcast_to(diagonal, (sep_local, LANES))],
        axis=1,
    )
    mine, other = gather_rows(folded, GROUP)
    odd = lax.axis_index(GROUP) % 2 == 1
    pair = jnp.stack(
        [
            block.reshape(-1, sep_local, folded.shape[1])
            for block in (jnp.where(odd, other, mine), jnp.where(odd, mine, other))
        ],
        axis=1,
    ).reshape(sep_width, -1)
    row = iota((sep_width, sep_width), 0)
    col = iota((sep_width, sep_width), 1)
    square = pair[:, :sep_width]
    sep_l = jnp.where(col < row, square, jnp.where(col == row, pair[:, sep_width:][:, :1], 0.0))
    sep_u = jnp.where(col >= row, square, 0.0)

    def own_rows(value):
        return lax.dynamic_slice(value, (at[0], 0), (sep_local, ports))

    y_sep = contract(sep_l, halves_down(sources, ports), 1, 1)
    count = axis_count(EVERYONE)
    update = contract(sep_lower, own_rows(y_sep), 1, 0).reshape(count, root_local, ports)
    held = b_root - exchange(update, EVERYONE).sum(axis=0)
    for factor in (root_linv, root_uinv):
        whole = gather_blocks(held, EVERYONE).reshape(root_width, ports)
        held = contract(factor, whole, 1, 0)
    x_root = held
    whole = gather_blocks(x_root, EVERYONE).reshape(root_width, ports)
    z_sep = own_rows(y_sep) - contract(sep_upper, whole, 1, 0)
    whole = gather_blocks(z_sep, GROUP).reshape(sep_width, ports)
    x_sep = contract(sep_u, whole, 1, 0)
    coupled = x_sep[sep_rows[0]]
    inner = y_leaf - contract(coupled, leaf_upper, 0, 1)
    x_leaf = contract(inner, leaf_uinv, 1, 1)
    own = jnp.concatenate([own_rows(x_sep), x_root], axis=0)
    partial = contract(x_leaf, bases[0], 1, 0) + contract(
        own, jnp.concatenate(bases[1:], axis=0), 0, 0
    )
    pad = jnp.zeros((ports, LANES - own.shape[0]), jnp.float32)
    return jnp.concatenate([x_leaf, own.T, pad], axis=1), halves_up(partial)


def shards(
    b_leaf,
    b_sep,
    b_root,
    leaf_linv,
    leaf_uinv,
    leaf_lower,
    leaf_upper,
    sep_rows,
    sep_linv,
    sep_uinv,
    sep_lower,
    sep_upper,
    root_linv,
    root_uinv,
    basis_leaf,
    basis_sep,
    basis_root,
    g_blocks,
    c_blocks,
    block_cols,
):
    extent, ports = b_leaf.shape
    sep_local = b_sep.shape[0]
    root_local = b_root.shape[0]
    sep_width = sep_linv.shape[1]
    basis = basis_leaf.shape[1]
    at = (lax.axis_index(GROUP) * sep_local).astype(jnp.int32).reshape(1)
    count = axis_count(EVERYONE)
    node_count = float(count * (extent + sep_local + root_local))
    square = extent * extent * ports

    y_leaf, sources = call(
        leaf_kernel,
        [shape_of(ports, extent), shape_of(sep_width // LANES * ports, LANES)],
        [at, b_leaf.T, leaf_linv, leaf_lower, sep_rows, b_sep],
        scalars=1,
        flops=6 * square,
        limit=None,
    )
    sources = sum_over(sources, GROUP)
    factors = (sep_linv, sep_uinv, sep_lower, sep_upper, root_linv, root_uinv)
    bases = (basis_leaf, basis_sep, basis_root)
    leaf = (y_leaf, sep_rows, leaf_upper, leaf_uinv)
    replicate = count == axis_count(GROUP) and sep_local == root_local
    if replicate and 4 * sep_width * (4 * sep_width + LANES) <= REPLICATE_BYTES:
        x_all, partial = solve_replicated(at, sources, b_root, factors, leaf, bases)
    else:
        x_all, partial = solve_spread(at, sources, b_root, factors, leaf, bases)
    coefficients = sum_over(partial, EVERYONE, 1.0 / node_count)
    g_dense, c_dense = call(
        dense_kernel, [shape_of(extent, extent)] * 2, [block_cols, g_blocks, c_blocks], scalars=1
    )
    coef_out, cleaned, products = call(
        clean_kernel,
        [shape_of(ports, basis), shape_of(ports, extent + LANES), shape_of(2 * ports, LANES)],
        [coefficients, x_all, basis_leaf, basis_sep, basis_root, g_dense, c_dense],
        flops=14 * square,
    )
    sums = sum_over(products, EVERYONE, 1.0 / node_count)
    v_leaf, v_sep, v_root, g_out, c_out = call(
        tail_kernel,
        [
            shape_of(ports, extent),
            shape_of(sep_local, ports),
            shape_of(root_local, ports),
            shape_of(ports, ports),
            shape_of(ports, ports),
        ],
        [sums, cleaned],
        flops=4 * square,
    )
    return (v_leaf.T, v_sep, v_root, coef_out.T, g_out, c_out)


def solution(mesh):
    rows = P(EVERYONE, None)
    columns = P(None, EVERYONE)
    return jax.shard_map(
        shards,
        mesh=mesh,
        in_specs=(rows,) * 10 + (columns,) + (rows,) * 9,
        out_specs=(rows, rows, rows, P(), P(), P()),
        check_vma=False,
    )
```

time: 686 us -> 97.3 us (0.14)
  waiting for transfers between devices: 330 us -> 22.7 us
  blocking collectives: 309 us -> 39.1 us
  starting transfers between devices: 0.12 us -> 14.6 us
  matrix products: 13.6 us -> 0 us
  other arithmetic: 13.7 us -> 0.17 us
  between operations: 14.1 us -> 0.86 us
  Pallas kernels: 0 us -> 12.3 us
    all_gather x6 -> x0, blocking collectives: 230 us -> none  [the longest x1 40.4 us: shards(): y_root_all = lax.all_gather(y_root, ('outer', 'inner'), axis=0, tiled=True)]
    psum x2 -> x0, waiting for transfers between devices: 200 us -> none  [the longest x1 122 us: shards(): coefficients = lax.psum(projected, ('outer', 'inner')) / node_count]
    unnamed x4 -> x0, waiting for transfers between devices: 130 us -> none
    psum x2 -> x0, blocking collectives: 79.8 us -> none  [the longest x1 40.4 us: shards(): g_summed, c_summed = lax.psum((g_local, c_local), ('outer', 'inner'))]
    all_to_all x0 -> x4, blocking collectives: none -> 39.1 us  [exchange(): return lax.all_to_all(blocks, axes, 0, 0, tiled=True)]
    all_to_all x0 -> x2, waiting for transfers between devices: none -> 13.6 us  [exchange(): return lax.all_to_all(blocks, axes, 0, 0, tiled=True)]
    dot_general x28 -> x0, matrix products: 13.4 us -> none  [the longest x17 8.18 us: matmul_exact(): jnp.dot(left, right, precision=lax.Precision.HIGHEST, preferred_element_t...]
    pallas_call x0 -> x9, Pallas kernels: none -> 12.3 us  [call(): pl.pallas_call(body, out_shape=outs, in_specs=specs, out_specs=[WHOLE] *...]
  transfers between devices with their start and end apart: 3 -> 9, of which waited for: 3 -> 6; matrix products, arithmetic and copies ran while one was open for 0% -> 1% of each run, Pallas kernels for 0% -> 4%
where the time goes in v2:
time: 97.3 us; the launch traced here: 96.6 us
  blocking collectives  39.1 us (40%)
  waiting for transfers between devices  22.7 us (23%)
  starting transfers between devices  14.6 us (15%)
  Pallas kernels  12.3 us (13%)
  local copies, waits for them, and re-layouts  6.76 us (7%)
    all_to_all x4, blocking collectives, exchange(): return lax.all_to_all(blocks, axes, 0, 0, tiled=True)  39.1 us
    all_to_all x2, waiting for transfers between devices, exchange(): return lax.all_to_all(blocks, axes, 0, 0, tiled=True)  13.6 us
    pallas_call x9, Pallas kernels, call(): pl.pallas_call(body, out_shape=outs, in_specs=specs, out_specs=[WHOLE] *...  12.3 us
    ppermute x6, starting transfers between devices, gather_rows(): blocks.append(lax.ppermute(held, axes, pairs))  9.27 us
    ppermute x6, waiting for transfers between devices, gather_rows(): blocks.append(lax.ppermute(held, axes, pairs))  9.13 us
    unnamed x34, local copies, waits for them, and re-layouts  5.54 us
    all_to_all x2, starting transfers between devices, exchange(): return lax.all_to_all(blocks, axes, 0, 0, tiled=True)  5.28 us
  transfers between devices with their start and end apart: 9, of which 6 were waited for; matrix products, arithmetic and copies ran while one was open for 1% of the time, Pallas kernels for 4%

profile of v2, /device:TPU:0, one launch (start us, length us, event | category | flops | bytes accessed | tf_op | source)
XLA Modules:
  0.0 96.6 jit_solution(1142311865892053520)
XLA Ops:
  0.7 0.7 copy-done.8
  1.3 0.7 copy-done.9
  2.0 0.7 copy-done.10
  2.7 0.7 copy-done.11
  3.4 0.7 copy-done.12
  4.1 0.7 copy-done.13
  4.8 0.7 copy-done.15
  5.5 0.1 shard_map.237
  5.6 5.1 %collective-permute-start = (f32[8,1152]{1,0:T(8,128)S(1)}, f32[8,1152]{1,0:T(8,128)S(1)}, u32[]{:S(2)}, u32[]{:S(2)}) collective-permute-start(f32[8,1152]{1,0:T(8,128)S(1)} %shard_map.237), channel_id=1, source_target_pairs={{0,24},{1,25},{2,26},{3,27},{4,28},{5,29},{6,30},{7,31},{8,16},{9,... | collective-permute-start | bytes 110600 | tf_op jit(solution)/shard_map/ppermute | solution.py:158
  10.7 0.0 collective-permute-start.1
  10.7 0.6 collective-permute-start.2
  11.3 1.3 %collective-permute-done = f32[8,1152]{1,0:T(8,128)S(1)} collective-permute-done((f32[8,1152]{1,0:T(8,128)S(1)}, f32[8,1152]{1,0:T(8,128)S(1)}, u32[]{:S(2)}, u32[]{:S(2)}) %collective-permute-start) | collective-permute-done | bytes 36896 | tf_op jit(solution)/shard_map/ppermute | solution.py:158
  12.6 2.9 %collective-permute-done.1 = f32[8,1152]{1,0:T(8,128)S(1)} collective-permute-done((f32[8,1152]{1,0:T(8,128)S(1)}, f32[8,1152]{1,0:T(8,128)S(1)}, u32[]{:S(2)}, u32[]{:S(2)}) %collective-permute-start.1) | collective-permute-done | bytes 36896 | tf_op jit(solution)/shard_map/ppermute | solution.py:158
  15.5 0.0 collective-permute-done.2
  15.6 2.5 %collective-permute-start.3 = (f32[4,8,1152]{2,1,0:T(8,128)S(1)}, f32[4,8,1152]{2,1,0:T(8,128)S(1)}, u32[]{:S(2)}, u32[]{:S(2)}) collective-permute-start(f32[4,8,1152]{2,1,0:T(8,128)S(1)} %pad_maximum_fusion.1), channel_id=1, source_target_pairs={{0,6},{1,7},{2,4},{3,5},{4,2},{5,3},{6,0},{7,1},{8,14},{9,15},{10,... | collective-permute-start | bytes 442376 | tf_op jit(solution)/shard_map/ppermute | solution.py:158
  18.1 0.5 collective-permute-start.4
  18.6 0.5 collective-permute-start.5
  19.1 4.1 %collective-permute-done.3 = f32[4,8,1152]{2,1,0:T(8,128)S(1)} collective-permute-done((f32[4,8,1152]{2,1,0:T(8,128)S(1)}, f32[4,8,1152]{2,1,0:T(8,128)S(1)}, u32[]{:S(2)}, u32[]{:S(2)}) %collective-permute-start.3) | collective-permute-done | bytes 147488 | tf_op jit(solution)/shard_map/ppermute | solution.py:158
  23.3 0.8 collective-permute-done.4
  24.0 0.0 collective-permute-done.5
  24.2 0.1 collective-permute-start.6
  24.3 2.5 %shard_map.235 = (f32[64,256]{1,0:T(8,128)}, f32[128,128]{1,0:T(8,128)}) custom-call(s32[1]{0:T(128)} %bitcast.at_ref, f32[64,256]{1,0:T(8,128)} %bitcast.38, f32[256,256]{1,0:T(8,128)} %linv_ref.1, f32[256,256]{1,0:T(8,128)} %lower_ref.1, s32[1,256]{1,0:T(1,128)} %rows_ref.3, f32[8,64]{1,0:T(8,128)} %b_sep_ref.1), custom_call_target="tpu_custom_call" | custom-call | flops 25165824 | bytes 723972 | tf_op jit(solution)/shard_map/pallas_call | solution.py:76
  26.8 10.9 %all_to_all.30.in_ref = f32[32,4,128]{2,1,0:T(4,128)S(1)} all-to-all(f32[32,4,128]{2,1,0:T(4,128)} %bitcast.37), channel_id=1, replica_groups=mesh['outer'=1,'inner'=32] {'inner'}, dimensions={0} | all-to-all | bytes 131072 | tf_op jit(solution)/shard_map/all_to_all | solution.py:103
  37.7 0.7 shard_map.236
  38.4 2.6 %all-to-all-start.1 = ((f32[32,4,128]{2,1,0:T(4,128)}), f32[32,4,128]{2,1,0:T(4,128)S(1)}, u32[]{:S(2)}, u32[]{:S(2)}) async-start(f32[32,4,128]{2,1,0:T(4,128)} %shard_map.236), calls=%async_computation.1 | async-start | bytes 131072 | tf_op jit(solution)/shard_map/all_to_all | solution.py:103
  41.0 0.0 copy-start
  41.0 0.0 copy-start.3
  41.0 0.0 copy-start.4
  41.1 0.0 copy-start.7
  41.1 0.0 collective-permute-done.6
  41.1 0.0 copy-start.5
  41.1 0.0 copy-start.6
  41.1 1.2 %copy.27 = f32[4,4,8,1152]{3,2,1,0:T(8,128)S(1)} copy(f32[4,4,8,1152]{3,2,0,1:T(8,128)} %collective-permute-done.6) | data formatting | bytes 1179648 | tf_op jit(solution)/shard_map/ppermute | solution.py:162
  42.3 6.1 %all-to-all-done.1 = f32[32,4,128]{2,1,0:T(4,128)S(1)} async-done(((f32[32,4,128]{2,1,0:T(4,128)}), f32[32,4,128]{2,1,0:T(4,128)S(1)}, u32[]{:S(2)}, u32[]{:S(2)}) %all-to-all-start.1) | async-done | bytes 65568 | tf_op jit(solution)/shard_map/all_to_all | solution.py:103
  48.4 0.0 copy-done.3
  48.4 0.0 copy-done.7
  48.4 0.6 copy-done.14
  49.1 2.9 %shard_map.238 = (f32[64,384]{1,0:T(8,128)S(1)}, f32[256,128]{1,0:T(8,128)S(1)}) custom-call(s32[1]{0:T(128)} %bitcast.at_ref, f32[128,128]{1,0:T(8,128)S(1)} %bitcast.32, f32[128,1152]{1,0:T(8,128)S(1)} %bitcast.29, f32[128,1152]{1,0:T(8,128)S(1)} %bitcast.30, f32[64,256]{1,0:T(8,128)S(1)} %copy-done.7, s32[1,256]{1,0:T(1,128)S(1)} %copy-done.14, ...), custom_call_target="tpu_custom_call" | custom-call | flops 92274688 | bytes 2622468 | tf_op jit(solution)/shard_map/pallas_call | solution.py:76
  52.0 0.0 copy-start.1
  52.0 10.0 %all_to_all.31.in_ref = f32[32,8,128]{2,1,0:T(8,128)S(1)} all-to-all(f32[32,8,128]{2,1,0:T(8,128)S(1)} %bitcast.34), channel_id=1, replica_groups=mesh['outer'=1,'inner'=32] {'outer','inner'}, dimensions={0} | all-to-all | bytes 262144 | tf_op jit(solution)/shard_map/all_to_all | solution.py:103
  62.0 0.7 shard_map.239
  62.7 2.7 %all-to-all-start.3 = ((f32[32,8,128]{2,1,0:T(8,128)}), f32[32,8,128]{2,1,0:T(8,128)S(1)}, u32[]{:S(2)}, u32[]{:S(2)}) async-start(f32[32,8,128]{2,1,0:T(8,128)} %shard_map.239), calls=%async_computation.3 | async-start | bytes 262144 | tf_op jit(solution)/shard_map/all_to_all | solution.py:103
  65.5 0.7 shard_map.240
  66.2 7.5 %all-to-all-done.3 = f32[32,8,128]{2,1,0:T(8,128)S(1)} async-done(((f32[32,8,128]{2,1,0:T(8,128)}), f32[32,8,128]{2,1,0:T(8,128)S(1)}, u32[]{:S(2)}, u32[]{:S(2)}) %all-to-all-start.3) | async-done | bytes 131104 | tf_op jit(solution)/shard_map/all_to_all | solution.py:103
  73.6 1.3 %shard_map.241 = (f32[64,512]{1,0:T(8,128)}, f32[64,384]{1,0:T(8,128)S(1)}, f32[128,128]{1,0:T(8,128)S(1)}) custom-call(f32[256,128]{1,0:T(8,128)S(1)} %bitcast.31, f32[64,384]{1,0:T(8,128)S(1)} %get-tuple-element.23.x_ref, f32[256,512]{1,0:T(8,128)S(1)} %copy-done, f32[8,512]{1,0:T(8,128)S(1)} %copy-done.5, f32[8,512]{1,0:T(8,128)S(1)} %copy-done.6, ...), custom_call_target="tpu_custom_call" | custom-call | flops 58720256 | bytes 1605632 | tf_op jit(solution)/shard_map/pallas_call | solution.py:76
  74.9 9.1 %all_to_all.32.in_ref = f32[32,4,128]{2,1,0:T(4,128)S(1)} all-to-all(f32[32,4,128]{2,1,0:T(4,128)S(1)} %bitcast.35), channel_id=1, replica_groups=mesh['outer'=1,'inner'=32] {'outer','inner'}, dimensions={0} | all-to-all | bytes 131072 | tf_op jit(solution)/shard_map/all_to_all | solution.py:103
  84.1 9.1 %all_to_all.33 = f32[32,4,128]{2,1,0:T(4,128)S(1)} all-to-all(f32[32,4,128]{2,1,0:T(4,128)S(1)} %shard_map.242), channel_id=1, replica_groups=mesh['outer'=1,'inner'=32] {'outer','inner'}, dimensions={0} | all-to-all | bytes 131072 | tf_op jit(solution)/shard_map/all_to_all | solution.py:103
  93.2 3.4 %shard_map.243 = (f32[64,256]{1,0:T(8,128)}, f32[8,64]{1,0:T(8,128)}, f32[8,64]{1,0:T(8,128)}, f32[64,64]{1,0:T(8,128)}, f32[64,64]{1,0:T(8,128)}) custom-call(f32[128,128]{1,0:T(8,128)S(1)} %bitcast.33, f32[64,384]{1,0:T(8,128)S(1)} %get-tuple-element.27.clean_ref), custom_call_target="tpu_custom_call" | custom-call | flops 16777216 | bytes 266240 | tf_op jit(solution)/shard_map/pallas_call | solution.py:76
  (24 shorter events, 0.3 us)
Async XLA Ops:
  0.6 0.7 copy-start.8
  1.3 0.7 copy-start.9
  2.0 0.7 copy-start.10
  2.7 0.7 copy-start.11
  3.4 0.7 copy-start.12
  4.1 0.7 copy-start.13
  4.8 0.7 copy-start.15
  5.6 7.0 %collective-permute-start = (f32[8,1152]{1,0:T(8,128)S(1)}, f32[8,1152]{1,0:T(8,128)S(1)}, u32[]{:S(2)}, u32[]{:S(2)}) collective-permute-start(f32[8,1152]{1,0:T(8,128)S(1)} %shard_map.237), channel_id=1, source_target_pairs={{0,24},{1,25},{2,26},{3,27},{4,28},{5,29},{6,30},{7,31},{8,16},{9,... | collective-permute-start | bytes 110600 | tf_op jit(solution)/shard_map/ppermute | solution.py:158
  10.7 4.9 %collective-permute-start.1 = (f32[8,1152]{1,0:T(8,128)S(1)}, f32[8,1152]{1,0:T(8,128)S(1)}, u32[]{:S(2)}, u32[]{:S(2)}) collective-permute-start(f32[8,1152]{1,0:T(8,128)S(1)} %shard_map.237), channel_id=1, source_target_pairs={{0,16},{1,17},{2,18},{3,19},{4,20},{5,21},{6,22},{7,23},{8,24},{9,... | collective-permute-start | bytes 110600 | tf_op jit(solution)/shard_map/ppermute | solution.py:158
  10.7 4.9 %collective-permute-start.2 = (f32[8,1152]{1,0:T(8,128)S(1)}, f32[8,1152]{1,0:T(8,128)S(1)}, u32[]{:S(2)}, u32[]{:S(2)}) collective-permute-start(f32[8,1152]{1,0:T(8,128)S(1)} %shard_map.237), channel_id=1, source_target_pairs={{0,8},{1,9},{2,10},{3,11},{4,12},{5,13},{6,14},{7,15},{8,0},{9,1},... | collective-permute-start | bytes 110600 | tf_op jit(solution)/shard_map/ppermute | solution.py:158
  15.6 7.7 %collective-permute-start.3 = (f32[4,8,1152]{2,1,0:T(8,128)S(1)}, f32[4,8,1152]{2,1,0:T(8,128)S(1)}, u32[]{:S(2)}, u32[]{:S(2)}) collective-permute-start(f32[4,8,1152]{2,1,0:T(8,128)S(1)} %pad_maximum_fusion.1), channel_id=1, source_target_pairs={{0,6},{1,7},{2,4},{3,5},{4,2},{5,3},{6,0},{7,1},{8,14},{9,15},{10,... | collective-permute-start | bytes 442376 | tf_op jit(solution)/shard_map/ppermute | solution.py:158
  18.1 6.0 %collective-permute-start.4 = (f32[4,8,1152]{2,1,0:T(8,128)S(1)}, f32[4,8,1152]{2,1,0:T(8,128)S(1)}, u32[]{:S(2)}, u32[]{:S(2)}) collective-permute-start(f32[4,8,1152]{2,1,0:T(8,128)S(1)} %pad_maximum_fusion.1), channel_id=1, source_target_pairs={{0,4},{1,5},{2,6},{3,7},{4,0},{5,1},{6,2},{7,3},{8,12},{9,13},{10,... | collective-permute-start | bytes 442376 | tf_op jit(solution)/shard_map/ppermute | solution.py:158
  18.6 5.4 %collective-permute-start.5 = (f32[4,8,1152]{2,1,0:T(8,128)S(1)}, f32[4,8,1152]{2,1,0:T(8,128)S(1)}, u32[]{:S(2)}, u32[]{:S(2)}) collective-permute-start(f32[4,8,1152]{2,1,0:T(8,128)S(1)} %pad_maximum_fusion.1), channel_id=1, source_target_pairs={{0,2},{1,3},{2,0},{3,1},{4,6},{5,7},{6,4},{7,5},{8,10},{9,11},{10,... | collective-permute-start | bytes 442376 | tf_op jit(solution)/shard_map/ppermute | solution.py:158
  24.2 16.9 %collective-permute-start.6 = (f32[4,4,8,1152]{3,2,0,1:T(8,128)S(1)}, f32[4,4,8,1152]{3,2,0,1:T(8,128)}, u32[]{:S(2)}, u32[]{:S(2)}) collective-permute-start(f32[4,4,8,1152]{3,2,0,1:T(8,128)S(1)} %pad_maximum_fusion), channel_id=1, source_target_pairs={{0,1},{1,0},{2,3},{3,2},{4,5},{5,4},{6,7},{7,6},{8,9},{9,8},{10,11... | collective-permute-start | bytes 1769480 | tf_op jit(solution)/shard_map/ppermute | solution.py:162
  38.4 10.0 %all-to-all-start.1 = ((f32[32,4,128]{2,1,0:T(4,128)}), f32[32,4,128]{2,1,0:T(4,128)S(1)}, u32[]{:S(2)}, u32[]{:S(2)}) async-start(f32[32,4,128]{2,1,0:T(4,128)} %shard_map.236), calls=%async_computation.1 | async-start | bytes 131072 | tf_op jit(solution)/shard_map/all_to_all | solution.py:103
  41.0 7.4 %copy-start = (f32[256,512]{1,0:T(8,128)S(1)}, f32[256,512]{1,0:T(8,128)}, u32[]{:S(2)}) copy-start(f32[256,512]{1,0:T(8,128)} %q_leaf_ref.3) | copy-start | bytes 1572868
  41.0 7.4 %copy-start.3 = (f32[256,256]{1,0:T(8,128)S(1)}, f32[256,256]{1,0:T(8,128)}, u32[]{:S(2)}) copy-start(f32[256,256]{1,0:T(8,128)} %leaf_upper_ref.1) | copy-start | bytes 786436
  41.0 7.3 %copy-start.4 = (f32[256,256]{1,0:T(8,128)S(1)}, f32[256,256]{1,0:T(8,128)}, u32[]{:S(2)}) copy-start(f32[256,256]{1,0:T(8,128)} %leaf_uinv_ref.1) | copy-start | bytes 786436
  41.1 7.3 %copy-start.7 = (f32[64,256]{1,0:T(8,128)S(1)}, f32[64,256]{1,0:T(8,128)}, u32[]{:S(2)}) copy-start(f32[64,256]{1,0:T(8,128)} %get-tuple-element.21.y_ref) | copy-start | bytes 196612
  41.1 7.3 %copy-start.5 = (f32[8,512]{1,0:T(8,128)S(1)}, f32[8,512]{1,0:T(8,128)}, u32[]{:S(2)}) copy-start(f32[8,512]{1,0:T(8,128)} %q_sep_ref.3) | copy-start | bytes 49156
  41.1 7.3 %copy-start.6 = (f32[8,512]{1,0:T(8,128)S(1)}, f32[8,512]{1,0:T(8,128)}, u32[]{:S(2)}) copy-start(f32[8,512]{1,0:T(8,128)} %q_root_ref.3) | copy-start | bytes 49156
  48.4 0.7 copy-start.14
  49.1 16.4 %copy-start.2 = (f32[1024,128]{1,0:T(8,128)S(1)}, f32[1024,128]{1,0:T(8,128)}, u32[]{:S(2)}) copy-start(f32[1024,128]{1,0:T(8,128)} %c_ref.1) | copy-start | bytes 1572868
  52.0 13.5 %copy-start.1 = (f32[1024,128]{1,0:T(8,128)S(1)}, f32[1024,128]{1,0:T(8,128)}, u32[]{:S(2)}) copy-start(f32[1024,128]{1,0:T(8,128)} %g_ref.1) | copy-start | bytes 1572868
  62.7 2.7 %copy-start.16 = (s32[2,4]{1,0:T(2,128)S(1)}, s32[2,4]{1,0:T(2,128)}, u32[]{:S(2)}) copy-start(s32[2,4]{1,0:T(2,128)} %cols_ref.1) | copy-start | bytes 100
  62.7 10.9 %all-to-all-start.3 = ((f32[32,8,128]{2,1,0:T(8,128)}), f32[32,8,128]{2,1,0:T(8,128)S(1)}, u32[]{:S(2)}, u32[]{:S(2)}) async-start(f32[32,8,128]{2,1,0:T(8,128)} %shard_map.239), calls=%async_computation.3 | async-start | bytes 262144 | tf_op jit(solution)/shard_map/all_to_all | solution.py:103

commit v3 on v2

--- a/solution.py
+++ b/solution.py
@@ -14,6 +14,8 @@
 REPLICATE_BYTES = 4 << 20
 VMEM_BYTES = 12 << 20
 HOP_BITS = 2
+HOP_DEVICES = 64
+FIRST_UPWARD = True
 EVERYONE = ("outer", "inner")
 GROUP = ("inner",)
 WHOLE = pl.BlockSpec(memory_space=pltpu.VMEM)
@@ -68,19 +70,40 @@
     return jax.ShapeDtypeStruct(dims, jnp.float32)
 
 
-def call(body, outs, operands, scalars=0, flops=0, limit=VMEM_BYTES):
+def call(body, outs, operands, far=(), scalars=0, flops=0, limit=VMEM_BYTES):
     specs = [SCALAR] * scalars + [WHOLE] * (len(operands) - scalars)
+    specs += [pl.BlockSpec(memory_space=pltpu.HBM)] * len(far)
+    operands = [*operands, *far]
     moved = sum(4 * operand.size for operand in operands) + sum(
         4 * math.prod(out.shape) for out in outs
     )
+    scratch = [pltpu.VMEM(operand.shape, operand.dtype) for operand in far]
+    if far:
+        scratch.append(pltpu.SemaphoreType.DMA((len(far),)))
     return pl.pallas_call(
         body,
         out_shape=outs,
         in_specs=specs,
         out_specs=[WHOLE] * len(outs),
+        scratch_shapes=scratch,
         compiler_params=pltpu.CompilerParams(vmem_limit_bytes=limit),
         cost_estimate=pl.CostEstimate(flops=flops, bytes_accessed=moved, transcendentals=0),
     )(*operands)
+
+
+def fetch(far, copies, semaphores):
+    moves = [
+        pltpu.make_async_copy(source, target, semaphores.at[at])
+        for at, (source, target) in enumerate(zip(far, copies))
+    ]
+    for move in moves:
+        move.start()
+
+    def read(at):
+        moves[at].wait()
+        return copies[at][...]
+
+    return read
 
 
 def iota(shape, dim):
@@ -131,6 +154,61 @@
     return whole.reshape(tall.shape)
 
 
+def is_power_of_two(count):
+    return count & (count - 1) == 0
+
+
+def hop(value, axes, low, width):
+    count = axis_count(axes)
+    total = value
+    for pattern in range(1, 1 << width):
+        pairs = [(source, source ^ (pattern << low)) for source in range(count)]
+        total = total + lax.ppermute(value, axes, pairs)
+    return total
+
+
+def halves_of(tall, axes):
+    half = tall.shape[0] // 2
+    odd = lax.axis_index(axes) % 2 == 1
+    kept = jnp.where(odd, tall[half:], tall[:half])
+    return kept, jnp.where(odd, tall[:half], tall[half:])
+
+
+def swap_pair(value, axes):
+    count = axis_count(axes)
+    return lax.ppermute(value, axes, [(source, source ^ 1) for source in range(count)])
+
+
+def join_halves(mine, other, axes):
+    odd = lax.axis_index(axes) % 2 == 1
+    return jnp.concatenate([jnp.where(odd, other, mine), jnp.where(odd, mine, other)])
+
+
+def half_by_hops(kept, sent, axes, upward):
+    total = kept + swap_pair(sent, axes)
+    spans = spans_of(axis_count(axes).bit_length() - 1)
+    if upward:
+        spans.reverse()
+    for low, width in spans:
+        total = hop(total, axes, low, width)
+    return total
+
+
+def sum_by_hops(kept, sent, axes, scale, upward):
+    total = half_by_hops(kept, sent, axes, upward) * scale
+    return join_halves(total, swap_pair(total, axes), axes)
+
+
+def by_hops(count):
+    return is_power_of_two(count) and 1 < count <= HOP_DEVICES
+
+
+def sum_all(tall, axes, scale, upward):
+    if by_hops(axis_count(axes)) and tall.shape[0] % (2 * SUBLANES) == 0:
+        return sum_by_hops(*halves_of(tall, axes), axes, scale, upward)
+    return sum_over(tall, axes, scale)
+
+
 def swap_by_bits(blocks, position):
     size, bit = len(blocks), 0
     while 1 << bit < size:
@@ -142,74 +220,85 @@
     return blocks
 
 
-def gather_rows(rows, axes):
-    count = axis_count(axes)
-    bits = count.bit_length() - 1
-    here = lax.axis_index(axes)
-    held = rows
-    low = bits
-    stage = 0
+def spans_of(bits):
+    spans, low = [], bits
     while low > 1:
         width = min(HOP_BITS, low - 1)
         low -= width
+        spans.append((low, width))
+    return spans
+
+
+def gather_rows(rows, axes):
+    count = axis_count(axes)
+    here = lax.axis_index(axes)
+    held = rows
+    places, size = [0], 1
+    spans = spans_of(count.bit_length() - 1)
+    for low, width in spans:
         blocks = [held]
         for pattern in range(1, 1 << width):
             pairs = [(source, source ^ (pattern << low)) for source in range(count)]
             blocks.append(lax.ppermute(held, axes, pairs))
-        held = jnp.stack(swap_by_bits(blocks, here >> low), axis=stage)
-        stage += 1
-    pairs = [(source, source ^ 1) for source in range(count)]
-    other = lax.ppermute(held, axes, pairs)
-    shape = (-1,) + rows.shape[1:]
-    return held.reshape(shape), other.reshape(shape)
-
-
-def leaf_kernel(at_ref, b_ref, linv_ref, lower_ref, rows_ref, b_sep_ref, y_ref, sources_ref):
-    y_leaf = dot_nt(b_ref[...], linv_ref[...])
+        held = jnp.concatenate(swap_by_bits(blocks, here >> low))
+        places = [digit * size + place for place in places for digit in range(1 << width)]
+        size <<= width
+    return held, swap_pair(held, axes), places
+
+
+def leaf_kernel(count, at_ref, *refs):
+    far, (y_ref, kept_ref, sent_ref, *packed_ref) = refs[:count], refs[count : -count - 1]
+    read = fetch(far, refs[-count - 1 : -1], refs[-1])
+    b_leaf, linv = read(0), read(1)
+    y_leaf = dot_nt(b_leaf, linv)
     y_ref[...] = y_leaf
-    contrib = dot_nt(y_leaf, lower_ref[...])
-    width = sources_ref.shape[0] // b_ref.shape[0] * LANES
-    extent = rows_ref.shape[1]
-    hits = iota((width, extent), 0) == rows_ref[...]
+    contrib = dot_nt(y_leaf, read(2))
+    rows = read(3)
+    b_sep = read(4)
+    extent = rows.shape[1]
+    width = 2 * kept_ref.shape[0] // b_leaf.shape[0] * LANES
+    hits = iota((width, extent), 0) == rows
     placed = dot_nt(contrib, hits.astype(jnp.float32))
-    own_rows = b_sep_ref.shape[0]
+    own_rows = b_sep.shape[0]
     own = iota((own_rows, width), 1) == iota((own_rows, width), 0) + at_ref[0]
-    sources = dot_tn(b_sep_ref[...], own.astype(jnp.float32)) - placed
-    sources_ref[...] = halves_up(sources)
-
-
-def pack_kernel(
-    at_ref, sl_ref, su_ref, lower_ref, upper_ref, rl_ref, ru_ref, b_root_ref, out_ref
-):
-    rows, width = sl_ref.shape
-    own = iota((rows, width), 0) + at_ref[0]
+    tall = halves_up(dot_tn(b_sep, own.astype(jnp.float32)) - placed)
+    half = kept_ref.shape[0]
+    odd = (at_ref[0] // own_rows) % 2 == 1
+    kept_ref[...] = jnp.where(odd, tall[half:], tall[:half])
+    sent_ref[...] = jnp.where(odd, tall[:half], tall[half:])
+    if packed_ref:
+        pack_rows(at_ref[0], [read(at) for at in range(5, count)], packed_ref[0])
+
+
+def pack_rows(at, values, out_ref):
+    sep_l, sep_u, lower, upper, root_l, root_u, b_root = values
+    rows, width = sep_l.shape
+    own = iota((rows, width), 0) + at
     col = iota((rows, width), 1)
 
     def fold(lower, upper):
         diagonal = jnp.sum(jnp.where(col == own, lower, 0.0), axis=1, keepdims=True)
         return jnp.where(col < own, lower, upper), diagonal
 
-    sep, sep_diagonal = fold(sl_ref[...], su_ref[...])
-    root, root_diagonal = fold(rl_ref[...], ru_ref[...])
-    out_ref[:, :width] = sep
-    out_ref[:, width : 2 * width] = lower_ref[...]
-    out_ref[:, 2 * width : 3 * width] = upper_ref[...]
-    out_ref[:, 3 * width : 4 * width] = root
-    ports = b_root_ref.shape[1]
-    quarter = (LANES - ports) // 2
-    out_ref[:, 4 * width :] = jnp.concatenate(
+    sep, sep_diagonal = fold(sep_l, sep_u)
+    root, root_diagonal = fold(root_l, root_u)
+    quarter = (LANES - b_root.shape[1]) // 2
+    extra = jnp.concatenate(
         [
-            b_root_ref[...],
+            b_root,
             jnp.broadcast_to(sep_diagonal, (rows, quarter)),
             jnp.broadcast_to(root_diagonal, (rows, quarter)),
         ],
         axis=1,
     )
+    out_ref[...] = halves_up(jnp.concatenate([sep, lower, upper, root, extra], axis=1))
 
 
 def solve_kernel(
+    places,
     at_ref,
-    sources_ref,
+    half_ref,
+    pair_ref,
     mine_ref,
     other_ref,
     y_ref,
@@ -223,18 +312,24 @@
     partial_ref,
 ):
     ports, extent = y_ref.shape
-    own_rows = q_sep_ref.shape[0]
-    width = 2 * mine_ref.shape[0]
+    own_rows = SUBLANES
+    width = 2 * len(places) * own_rows
+    tall = mine_ref.shape[0] // len(places)
     odd = (at_ref[0] // own_rows) % 2 == 1
 
-    def piece(start, size):
-        blocks = []
-        for at in range(mine_ref.shape[0] // own_rows):
-            mine = mine_ref[own_rows * at : own_rows * (at + 1), start : start + size]
-            other = other_ref[own_rows * at : own_rows * (at + 1), start : start + size]
-            blocks.append(jnp.where(odd, other, mine))
-            blocks.append(jnp.where(odd, mine, other))
-        return jnp.concatenate(blocks, axis=0)
+    def ordered(mine, other):
+        return jnp.where(odd, other, mine), jnp.where(odd, mine, other)
+
+    def piece(first, size):
+        strips = []
+        for lane in range(first // LANES, (first + size) // LANES):
+            blocks = []
+            for place in places:
+                start = place * tall + lane * own_rows
+                rows = slice(start, start + own_rows)
+                blocks.extend(ordered(mine_ref[rows], other_ref[rows]))
+            strips.append(jnp.concatenate(blocks, axis=0))
+        return jnp.concatenate(strips, axis=1)
 
     row = iota((width, width), 0)
     col = iota((width, width), 1)
@@ -250,7 +345,7 @@
         piece(3 * width, width), extra[:, ports + quarter : ports + quarter + 1]
     )
     b_root = extra.T[:ports]
-    sources = halves_down(sources_ref[...], ports)
+    sources = halves_down(jnp.concatenate(ordered(half_ref[...], pair_ref[...]), axis=0), ports)
     y_sep = dot_nt(sources, sep_l)
     y_root = dot_nt(b_root - dot_nn(y_sep, piece(width, width)), root_l)
     x_root = dot_nt(y_root, root_u)
@@ -370,22 +465,16 @@
     c_ref[...] = dot_nt(dot_nn(inverse, c_sum), inverse)
 
 
-def solve_replicated(at, sources, b_root, factors, leaf, bases):
-    sep_linv, sep_uinv, sep_lower, sep_upper, root_linv, root_uinv = factors
-    ports, extent = leaf[0].shape
-    sep_local, sep_width = sep_linv.shape
-    basis = bases[0].shape[1]
-    (packed,) = call(
-        pack_kernel,
-        [shape_of(sep_local, 4 * sep_width + LANES)],
-        [at, sep_linv, sep_uinv, sep_lower.T, sep_upper, root_linv, root_uinv, b_root],
-        scalars=1,
-    )
-    mine, other = gather_rows(packed, GROUP)
+def solve_replicated(at, kept, sent, packed, y_leaf, late):
+    ports, extent = y_leaf.shape
+    basis = late[-1].shape[1]
+    mine, other, places = gather_rows(packed, GROUP)
+    half = half_by_hops(kept, sent, GROUP, FIRST_UPWARD)
+    pair = swap_pair(half, GROUP)
     return call(
-        solve_kernel,
+        functools.partial(solve_kernel, places),
         [shape_of(ports, extent + LANES), shape_of(basis // LANES * ports, LANES)],
-        [at, sources, mine, other, *leaf, *bases],
+        [at, half, pair, mine, other, y_leaf, *late],
         scalars=1,
         flops=22 * extent * extent * ports,
     )
@@ -404,15 +493,7 @@
         [jnp.where(col < row, sep_linv, sep_uinv), jnp.broadcast_to(diagonal, (sep_local, LANES))],
         axis=1,
     )
-    mine, other = gather_rows(folded, GROUP)
-    odd = lax.axis_index(GROUP) % 2 == 1
-    pair = jnp.stack(
-        [
-            block.reshape(-1, sep_local, folded.shape[1])
-            for block in (jnp.where(odd, other, mine), jnp.where(odd, mine, other))
-        ],
-        axis=1,
-    ).reshape(sep_width, -1)
+    pair = gather_blocks(folded, GROUP).reshape(sep_width, -1)
     row = iota((sep_width, sep_width), 0)
     col = iota((sep_width, sep_width), 1)
     square = pair[:, :sep_width]
@@ -477,24 +558,40 @@
     node_count = float(count * (extent + sep_local + root_local))
     square = extent * extent * ports
 
-    y_leaf, sources = call(
-        leaf_kernel,
-        [shape_of(ports, extent), shape_of(sep_width // LANES * ports, LANES)],
-        [at, b_leaf.T, leaf_linv, leaf_lower, sep_rows, b_sep],
+    factors = (sep_linv, sep_uinv, sep_lower, sep_upper, root_linv, root_uinv)
+    bases = (basis_leaf, basis_sep, basis_root)
+    replicate = (
+        count == axis_count(GROUP)
+        and sep_local == root_local == SUBLANES
+        and by_hops(count)
+        and 4 * sep_width * (4 * sep_width + LANES) <= REPLICATE_BYTES
+    )
+    tall = sep_width // LANES * ports
+    outs = [shape_of(ports, extent), shape_of(tall // 2, LANES), shape_of(tall // 2, LANES)]
+    far = [b_leaf.T, leaf_linv, leaf_lower, sep_rows, b_sep]
+    if replicate:
+        outs.append(shape_of((4 * sep_width // LANES + 1) * sep_local, LANES))
+        far += [sep_linv, sep_uinv, sep_lower.T, sep_upper, root_linv, root_uinv, b_root]
+    y_leaf, kept, sent, *packed = call(
+        functools.partial(leaf_kernel, len(far)),
+        outs,
+        [at],
+        far=far,
         scalars=1,
         flops=6 * square,
         limit=None,
     )
-    sources = sum_over(sources, GROUP)
-    factors = (sep_linv, sep_uinv, sep_lower, sep_upper, root_linv, root_uinv)
-    bases = (basis_leaf, basis_sep, basis_root)
-    leaf = (y_leaf, sep_rows, leaf_upper, leaf_uinv)
-    replicate = count == axis_count(GROUP) and sep_local == root_local
-    if replicate and 4 * sep_width * (4 * sep_width + LANES) <= REPLICATE_BYTES:
-        x_all, partial = solve_replicated(at, sources, b_root, factors, leaf, bases)
+    if replicate:
+        late = [sep_rows, leaf_upper, leaf_uinv, *bases]
+        x_all, partial = solve_replicated(at, kept, sent, *packed, y_leaf, late)
     else:
+        if by_hops(axis_count(GROUP)):
+            sources = sum_by_hops(kept, sent, GROUP, 1.0, False)
+        else:
+            sources = sum_over(join_halves(kept, sent, GROUP), GROUP)
+        leaf = (y_leaf, sep_rows, leaf_upper, leaf_uinv)
         x_all, partial = solve_spread(at, sources, b_root, factors, leaf, bases)
-    coefficients = sum_over(partial, EVERYONE, 1.0 / node_count)
+    coefficients = sum_all(partial, EVERYONE, 1.0 / node_count, True)
     g_dense, c_dense = call(
         dense_kernel, [shape_of(extent, extent)] * 2, [block_cols, g_blocks, c_blocks], scalars=1
     )
@@ -504,7 +601,7 @@
         [coefficients, x_all, basis_leaf, basis_sep, basis_root, g_dense, c_dense],
         flops=14 * square,
     )
-    sums = sum_over(products, EVERYONE, 1.0 / node_count)
+    sums = sum_all(products, EVERYONE, 1.0 / node_count, False)
     v_leaf, v_sep, v_root, g_out, c_out = call(
         tail_kernel,
         [

time: 97.3 us -> 87.5 us (0.90)
  blocking collectives: 39.1 us -> 0 us
  starting transfers between devices: 14.6 us -> 33.9 us
  waiting for transfers between devices: 22.7 us -> 39.5 us
  local copies, waits for them, and re-layouts: 6.76 us -> 0.64 us
  Pallas kernels: 12.3 us -> 11.1 us
    all_to_all x4 -> x0, blocking collectives: 39.1 us -> none  [exchange(): return lax.all_to_all(blocks, axes, 0, 0, tiled=True)]
    ppermute x1 -> x25, waiting for transfers between devices: 0.01 us -> 29.3 us  [the longest x18 22.8 us: hop(): total = total + lax.ppermute(value, axes, pairs)]
    ppermute x1 -> x25, starting transfers between devices: 0.07 us -> 24.6 us  [the longest x18 23.9 us: hop(): total = total + lax.ppermute(value, axes, pairs)]
    all_to_all x2 -> x0, waiting for transfers between devices: 13.6 us -> none  [exchange(): return lax.all_to_all(blocks, axes, 0, 0, tiled=True)]
    all_to_all x2 -> x0, starting transfers between devices: 5.28 us -> none  [exchange(): return lax.all_to_all(blocks, axes, 0, 0, tiled=True)]
    unnamed x34 -> x24, local copies, waits for them, and re-layouts: 5.54 us -> 0.64 us
    pallas_call x9 -> x5, Pallas kernels: 12.3 us -> 11.1 us  [call(): pl.pallas_call(body, out_shape=outs, in_specs=specs, out_specs=[WHOLE] *...]
    ppermute x1 -> x0, local copies, waits for them, and re-layouts: 1.18 us -> none  [gather_rows(): other = lax.ppermute(held, axes, pairs)]
  transfers between devices with their start and end apart: 9 -> 31, of which waited for: 6 -> 25; matrix products, arithmetic and copies ran while one was open for 1% -> 0% of each run, Pallas kernels for 4% -> 1%
where the time goes in v3:
time: 87.5 us; the launch traced here: 87.2 us
  waiting for transfers between devices  39.5 us (45%)
  starting transfers between devices  33.9 us (39%)
  Pallas kernels  11.1 us (13%)
  other arithmetic  1.08 us (1%)
  between operations  0.98 us (1%)
    ppermute x18, starting transfers between devices, hop(): total = total + lax.ppermute(value, axes, pairs)  23.9 us
    ppermute x18, waiting for transfers between devices, hop(): total = total + lax.ppermute(value, axes, pairs)  22.8 us
    pallas_call x5, Pallas kernels, call(): pl.pallas_call(body, out_shape=outs, in_specs=specs, out_specs=[WHOLE] *...  11.1 us
    ppermute x6, waiting for transfers between devices, gather_rows(): blocks.append(lax.ppermute(held, axes, pairs))  10.3 us
    ppermute x6, starting transfers between devices, gather_rows(): blocks.append(lax.ppermute(held, axes, pairs))  9.26 us
    ppermute x7, waiting for transfers between devices, swap_pair(): lax.ppermute(value, axes, [(source, source ^ 1) for source in range(count)])  6.49 us
  transfers between devices with their start and end apart: 31, of which 25 were waited for; matrix products, arithmetic and copies ran while one was open for 0% of the time, Pallas kernels for 1%

profile of v3, /device:TPU:0, one launch (start us, length us, event | category | flops | bytes accessed | tf_op | source)
XLA Modules:
  0.0 87.2 jit_solution(17759092674298330676)
XLA Ops:
  0.6 2.8 %shard_map.235 = (f32[64,256]{1,0:T(8,128)}, f32[64,128]{1,0:T(8,128)}, f32[64,128]{1,0:T(8,128)}, f32[72,128]{1,0:T(8,128)}) custom-call(s32[1]{0:T(128)} %bitcast.at_ref, f32[64,256]{1,0:T(8,128)} %bitcast.5, f32[256,256]{1,0:T(8,128)} %refs_1_.1, f32[256,256]{1,0:T(8,128)} %refs_2_.1, s32[1,256]{1,0:T(1,128)} %rows_ref.1, f32[8,64]{1,0:T(8,128)} %refs_4_.1, ...), custom_call_target="tpu_custom_call" | custom-call | flops 25165824 | bytes 812036 | tf_op jit(solution)/shard_map/pallas_call | solution.py:83
  3.5 3.1 %collective-permute-start.10 = (f32[72,128]{1,0:T(8,128)}, f32[72,128]{1,0:T(8,128)S(1)}, u32[]{:S(2)}, u32[]{:S(2)}) collective-permute-start(f32[72,128]{1,0:T(8,128)} %get-tuple-element.24), channel_id=1, source_target_pairs={{0,8},{1,9},{2,10},{3,11},{4,12},{5,13},{6,14},{7,15},{8,0},{9,1},... | collective-permute-start | bytes 110600 | tf_op jit(solution)/shard_map/ppermute | solution.py:242
  6.6 2.5 %collective-permute-start.8 = (f32[72,128]{1,0:T(8,128)}, f32[72,128]{1,0:T(8,128)S(1)}, u32[]{:S(2)}, u32[]{:S(2)}) collective-permute-start(f32[72,128]{1,0:T(8,128)} %get-tuple-element.24), channel_id=1, source_target_pairs={{0,24},{1,25},{2,26},{3,27},{4,28},{5,29},{6,30},{7,31},{8,16},{9,... | collective-permute-start | bytes 110600 | tf_op jit(solution)/shard_map/ppermute | solution.py:242
  9.2 3.9 %collective-permute-done.8 = f32[72,128]{1,0:T(8,128)S(1)} collective-permute-done((f32[72,128]{1,0:T(8,128)}, f32[72,128]{1,0:T(8,128)S(1)}, u32[]{:S(2)}, u32[]{:S(2)}) %collective-permute-start.8) | collective-permute-done | bytes 36896 | tf_op jit(solution)/shard_map/ppermute | solution.py:242
  13.0 1.5 %collective-permute-done.9 = f32[72,128]{1,0:T(8,128)S(1)} collective-permute-done((f32[72,128]{1,0:T(8,128)}, f32[72,128]{1,0:T(8,128)S(1)}, u32[]{:S(2)}, u32[]{:S(2)}) %collective-permute-start.9) | collective-permute-done | bytes 36896 | tf_op jit(solution)/shard_map/ppermute | solution.py:242
  14.5 0.8 broadcast_select_fusion.17
  15.3 2.5 %collective-permute-start.11 = (f32[288,128]{1,0:T(8,128)S(1)}, f32[288,128]{1,0:T(8,128)S(1)}, u32[]{:S(2)}, u32[]{:S(2)}) collective-permute-start(f32[288,128]{1,0:T(8,128)S(1)} %pad_maximum_fusion.1), channel_id=1, source_target_pairs={{0,6},{1,7},{2,4},{3,5},{4,2},{5,3},{6,0},{7,1},{8,14},{9,15},{10,... | collective-permute-start | bytes 442376 | tf_op jit(solution)/shard_map/ppermute | solution.py:242
  18.9 4.1 %collective-permute-done.11 = f32[288,128]{1,0:T(8,128)S(1)} collective-permute-done((f32[288,128]{1,0:T(8,128)S(1)}, f32[288,128]{1,0:T(8,128)S(1)}, u32[]{:S(2)}, u32[]{:S(2)}) %collective-permute-start.11) | collective-permute-done | bytes 147488 | tf_op jit(solution)/shard_map/ppermute | solution.py:242
  23.0 0.8 collective-permute-done.12
  24.1 0.6 copy-done.11
  24.7 1.5 %collective-permute-done = f32[64,128]{1,0:T(8,128)S(1)} collective-permute-done((f32[64,128]{1,0:T(8,128)S(1)}, f32[64,128]{1,0:T(8,128)S(1)}, u32[]{:S(2)}, u32[]{:S(2)}) %collective-permute-start) | collective-permute-done | bytes 32800 | tf_op jit(solution)/shard_map/ppermute | solution.py:179
  26.1 1.6 %collective-permute-start.1 = (f32[64,128]{1,0:T(8,128)S(1)}, f32[64,128]{1,0:T(8,128)S(1)}, u32[]{:S(2)}, u32[]{:S(2)}) collective-permute-start(f32[64,128]{1,0:T(8,128)S(1)} %add.75), channel_id=1, source_target_pairs={{0,2},{1,3},{2,0},{3,1},{4,6},{5,7},{6,4},{7,5},{8,10},{9,11},{10,... | collective-permute-start | bytes 98312 | tf_op jit(solution)/shard_map/ppermute | solution.py:166
  27.7 0.7 collective-permute-start.2
  28.5 1.2 %collective-permute-start.3 = (f32[64,128]{1,0:T(8,128)S(1)}, f32[64,128]{1,0:T(8,128)S(1)}, u32[]{:S(2)}, u32[]{:S(2)}) collective-permute-start(f32[64,128]{1,0:T(8,128)S(1)} %add.75), channel_id=1, source_target_pairs={{0,6},{1,7},{2,4},{3,5},{4,2},{5,3},{6,0},{7,1},{8,14},{9,15},{10,... | collective-permute-start | bytes 98312 | tf_op jit(solution)/shard_map/ppermute | solution.py:166
  30.1 1.9 %collective-permute-done.2 = f32[64,128]{1,0:T(8,128)S(1)} collective-permute-done((f32[64,128]{1,0:T(8,128)S(1)}, f32[64,128]{1,0:T(8,128)S(1)}, u32[]{:S(2)}, u32[]{:S(2)}) %collective-permute-start.2) | collective-permute-done | bytes 32800 | tf_op jit(solution)/shard_map/ppermute | solution.py:166
  32.0 1.3 %collective-permute-done.3 = f32[64,128]{1,0:T(8,128)S(1)} collective-permute-done((f32[64,128]{1,0:T(8,128)S(1)}, f32[64,128]{1,0:T(8,128)S(1)}, u32[]{:S(2)}, u32[]{:S(2)}) %collective-permute-start.3) | collective-permute-done | bytes 32800 | tf_op jit(solution)/shard_map/ppermute | solution.py:166
  33.7 2.5 %collective-permute-start.5 = (f32[64,128]{1,0:T(8,128)S(1)}, f32[64,128]{1,0:T(8,128)S(1)}, u32[]{:S(2)}, u32[]{:S(2)}) collective-permute-start(f32[64,128]{1,0:T(8,128)S(1)} %add_add_fusion.3), channel_id=1, source_target_pairs={{0,16},{1,17},{2,18},{3,19},{4,20},{5,21},{6,22},{7,23},{8,24},{9,... | collective-permute-start | bytes 98312 | tf_op jit(solution)/shard_map/ppermute | solution.py:166
  36.2 1.5 %collective-permute-start.6 = (f32[64,128]{1,0:T(8,128)S(1)}, f32[64,128]{1,0:T(8,128)S(1)}, u32[]{:S(2)}, u32[]{:S(2)}) collective-permute-start(f32[64,128]{1,0:T(8,128)S(1)} %add_add_fusion.3), channel_id=1, source_target_pairs={{0,24},{1,25},{2,26},{3,27},{4,28},{5,29},{6,30},{7,31},{8,16},{9,... | collective-permute-start | bytes 98312 | tf_op jit(solution)/shard_map/ppermute | solution.py:166
  37.7 0.8 collective-permute-done.5
  38.5 3.4 %collective-permute-done.6 = f32[64,128]{1,0:T(8,128)S(1)} collective-permute-done((f32[64,128]{1,0:T(8,128)S(1)}, f32[64,128]{1,0:T(8,128)S(1)}, u32[]{:S(2)}, u32[]{:S(2)}) %collective-permute-start.6) | collective-permute-done | bytes 32800 | tf_op jit(solution)/shard_map/ppermute | solution.py:166
  42.1 1.2 %collective-permute-done.7.pair_ref = f32[64,128]{1,0:T(8,128)S(1)} collective-permute-done((f32[64,128]{1,0:T(8,128)S(1)}, f32[64,128]{1,0:T(8,128)S(1)}, u32[]{:S(2)}, u32[]{:S(2)}) %collective-permute-start.7) | collective-permute-done | bytes 32800 | tf_op jit(solution)/shard_map/ppermute | solution.py:179
  43.3 2.9 %shard_map.236 = (f32[64,384]{1,0:T(8,128)S(1)}, f32[256,128]{1,0:T(8,128)S(1)}) custom-call(s32[1]{0:T(128)} %bitcast.at_ref, f32[64,128]{1,0:T(8,128)S(1)} %add_add_fusion.2.half_ref, f32[64,128]{1,0:T(8,128)S(1)} %collective-permute-done.7.pair_ref, f32[1152,128]{1,0:T(8,128)S(1)} %pad_maximum_fusion.mine_ref, ...), custom_call_target="tpu_custom_call" | custom-call | flops 92274688 | bytes 2622468 | tf_op jit(solution)/shard_map/pallas_call | solution.py:83
  46.5 1.1 %collective-permute-done.15 = f32[128,128]{1,0:T(8,128)S(1)} collective-permute-done((f32[128,128]{1,0:T(8,128)S(1)}, f32[128,128]{1,0:T(8,128)S(1)}, u32[]{:S(2)}, u32[]{:S(2)}) %collective-permute-start.15) | collective-permute-done | bytes 65568 | tf_op jit(solution)/shard_map/ppermute | solution.py:179
  47.6 1.3 %collective-permute-start.16 = (f32[128,128]{1,0:T(8,128)S(1)}, f32[128,128]{1,0:T(8,128)S(1)}, u32[]{:S(2)}, u32[]{:S(2)}) collective-permute-start(f32[128,128]{1,0:T(8,128)S(1)} %select_add_fusion), channel_id=1, source_target_pairs={{0,2},{1,3},{2,0},{3,1},{4,6},{5,7},{6,4},{7,5},{8,10},{9,11},{10,... | collective-permute-start | bytes 196616 | tf_op jit(solution)/shard_map/ppermute | solution.py:166
  48.9 0.6 collective-permute-start.17
  49.5 1.7 %collective-permute-start.18 = (f32[128,128]{1,0:T(8,128)S(1)}, f32[128,128]{1,0:T(8,128)S(1)}, u32[]{:S(2)}, u32[]{:S(2)}) collective-permute-start(f32[128,128]{1,0:T(8,128)S(1)} %select_add_fusion), channel_id=1, source_target_pairs={{0,6},{1,7},{2,4},{3,5},{4,2},{5,3},{6,0},{7,1},{8,14},{9,15},{10,... | collective-permute-start | bytes 196616 | tf_op jit(solution)/shard_map/ppermute | solution.py:166
  51.1 0.8 collective-permute-done.16
  51.9 1.9 %collective-permute-done.17 = f32[128,128]{1,0:T(8,128)S(1)} collective-permute-done((f32[128,128]{1,0:T(8,128)S(1)}, f32[128,128]{1,0:T(8,128)S(1)}, u32[]{:S(2)}, u32[]{:S(2)}) %collective-permute-start.17) | collective-permute-done | bytes 65568 | tf_op jit(solution)/shard_map/ppermute | solution.py:166
  53.9 0.8 collective-permute-done.18
  54.7 2.1 %collective-permute-start.20 = (f32[128,128]{1,0:T(8,128)S(1)}, f32[128,128]{1,0:T(8,128)S(1)}, u32[]{:S(2)}, u32[]{:S(2)}) collective-permute-start(f32[128,128]{1,0:T(8,128)S(1)} %add_add_fusion), channel_id=1, source_target_pairs={{0,16},{1,17},{2,18},{3,19},{4,20},{5,21},{6,22},{7,23},{8,24},{9,... | collective-permute-start | bytes 196616 | tf_op jit(solution)/shard_map/ppermute | solution.py:166
  56.8 2.3 %collective-permute-start.21 = (f32[128,128]{1,0:T(8,128)S(1)}, f32[128,128]{1,0:T(8,128)S(1)}, u32[]{:S(2)}, u32[]{:S(2)}) collective-permute-start(f32[128,128]{1,0:T(8,128)S(1)} %add_add_fusion), channel_id=1, source_target_pairs={{0,24},{1,25},{2,26},{3,27},{4,28},{5,29},{6,30},{7,31},{8,16},{9,... | collective-permute-start | bytes 196616 | tf_op jit(solution)/shard_map/ppermute | solution.py:166
  59.1 1.6 %collective-permute-done.20 = f32[128,128]{1,0:T(8,128)S(1)} collective-permute-done((f32[128,128]{1,0:T(8,128)S(1)}, f32[128,128]{1,0:T(8,128)S(1)}, u32[]{:S(2)}, u32[]{:S(2)}) %collective-permute-start.20) | collective-permute-done | bytes 65568 | tf_op jit(solution)/shard_map/ppermute | solution.py:166
  60.7 2.2 %collective-permute-done.21 = f32[128,128]{1,0:T(8,128)S(1)} collective-permute-done((f32[128,128]{1,0:T(8,128)S(1)}, f32[128,128]{1,0:T(8,128)S(1)}, u32[]{:S(2)}, u32[]{:S(2)}) %collective-permute-start.21) | collective-permute-done | bytes 65568 | tf_op jit(solution)/shard_map/ppermute | solution.py:166
  63.0 0.7 shard_map.237
  64.2 1.3 %shard_map.238 = (f32[64,512]{1,0:T(8,128)}, f32[64,384]{1,0:T(8,128)S(1)}, f32[128,128]{1,0:T(8,128)S(1)}) custom-call(f32[256,128]{1,0:T(8,128)S(1)} %pad_maximum_fusion.2.coef_ref, f32[64,384]{1,0:T(8,128)S(1)} %get-tuple-element.27.x_ref, f32[256,512]{1,0:T(8,128)S(1)} %copy-done, f32[8,512]{1,0:T(8,128)S(1)} %copy-done.5, f32[8,512]{1,0:T(8,128)S(1)} %copy-done.6, ...), custom_call_target="tpu_custom_call" | custom-call | flops 58720256 | bytes 1605632 | tf_op jit(solution)/shard_map/pallas_call | solution.py:83
  65.7 1.1 %collective-permute-done.23 = f32[64,128]{1,0:T(8,128)S(1)} collective-permute-done((f32[64,128]{1,0:T(8,128)S(1)}, f32[64,128]{1,0:T(8,128)S(1)}, u32[]{:S(2)}, u32[]{:S(2)}) %collective-permute-start.23) | collective-permute-done | bytes 32800 | tf_op jit(solution)/shard_map/ppermute | solution.py:179
  66.8 2.9 %collective-permute-start.25 = (f32[64,128]{1,0:T(8,128)S(1)}, f32[64,128]{1,0:T(8,128)S(1)}, u32[]{:S(2)}, u32[]{:S(2)}) collective-permute-start(f32[64,128]{1,0:T(8,128)S(1)} %select_add_fusion.1), channel_id=1, source_target_pairs={{0,16},{1,17},{2,18},{3,19},{4,20},{5,21},{6,22},{7,23},{8,24},{9,... | collective-permute-start | bytes 98312 | tf_op jit(solution)/shard_map/ppermute | solution.py:166
  69.6 1.5 %collective-permute-start.26 = (f32[64,128]{1,0:T(8,128)S(1)}, f32[64,128]{1,0:T(8,128)S(1)}, u32[]{:S(2)}, u32[]{:S(2)}) collective-permute-start(f32[64,128]{1,0:T(8,128)S(1)} %select_add_fusion.1), channel_id=1, source_target_pairs={{0,24},{1,25},{2,26},{3,27},{4,28},{5,29},{6,30},{7,31},{8,16},{9,... | collective-permute-start | bytes 98312 | tf_op jit(solution)/shard_map/ppermute | solution.py:166
  71.1 0.5 collective-permute-done.25
  71.7 3.6 %collective-permute-done.26 = f32[64,128]{1,0:T(8,128)S(1)} collective-permute-done((f32[64,128]{1,0:T(8,128)S(1)}, f32[64,128]{1,0:T(8,128)S(1)}, u32[]{:S(2)}, u32[]{:S(2)}) %collective-permute-start.26) | collective-permute-done | bytes 32800 | tf_op jit(solution)/shard_map/ppermute | solution.py:166
  75.4 1.6 %collective-permute-start.27 = (f32[64,128]{1,0:T(8,128)S(1)}, f32[64,128]{1,0:T(8,128)S(1)}, u32[]{:S(2)}, u32[]{:S(2)}) collective-permute-start(f32[64,128]{1,0:T(8,128)S(1)} %add_add_fusion.1), channel_id=1, source_target_pairs={{0,2},{1,3},{2,0},{3,1},{4,6},{5,7},{6,4},{7,5},{8,10},{9,11},{10,... | collective-permute-start | bytes 98312 | tf_op jit(solution)/shard_map/ppermute | solution.py:166
  77.0 0.7 collective-permute-start.28
  77.7 1.2 %collective-permute-start.29 = (f32[64,128]{1,0:T(8,128)S(1)}, f32[64,128]{1,0:T(8,128)S(1)}, u32[]{:S(2)}, u32[]{:S(2)}) collective-permute-start(f32[64,128]{1,0:T(8,128)S(1)} %add_add_fusion.1), channel_id=1, source_target_pairs={{0,6},{1,7},{2,4},{3,5},{4,2},{5,3},{6,0},{7,1},{8,14},{9,15},{10,... | collective-permute-start | bytes 98312 | tf_op jit(solution)/shard_map/ppermute | solution.py:166
  78.9 0.7 collective-permute-done.27
  79.6 1.3 %collective-permute-done.28 = f32[64,128]{1,0:T(8,128)S(1)} collective-permute-done((f32[64,128]{1,0:T(8,128)S(1)}, f32[64,128]{1,0:T(8,128)S(1)}, u32[]{:S(2)}, u32[]{:S(2)}) %collective-permute-start.28) | collective-permute-done | bytes 32800 | tf_op jit(solution)/shard_map/ppermute | solution.py:166
  80.9 1.6 %collective-permute-done.29 = f32[64,128]{1,0:T(8,128)S(1)} collective-permute-done((f32[64,128]{1,0:T(8,128)S(1)}, f32[64,128]{1,0:T(8,128)S(1)}, u32[]{:S(2)}, u32[]{:S(2)}) %collective-permute-start.29) | collective-permute-done | bytes 32800 | tf_op jit(solution)/shard_map/ppermute | solution.py:166
  82.6 1.2 %collective-permute-done.30 = f32[64,128]{1,0:T(8,128)S(1)} collective-permute-done((f32[64,128]{1,0:T(8,128)S(1)}, f32[64,128]{1,0:T(8,128)S(1)}, u32[]{:S(2)}, u32[]{:S(2)}) %collective-permute-start.30) | collective-permute-done | bytes 32800 | tf_op jit(solution)/shard_map/ppermute | solution.py:179
  83.8 3.4 %shard_map.239 = (f32[64,256]{1,0:T(8,128)}, f32[8,64]{1,0:T(8,128)}, f32[8,64]{1,0:T(8,128)}, f32[64,64]{1,0:T(8,128)}, f32[64,64]{1,0:T(8,128)}) custom-call(f32[128,128]{1,0:T(8,128)S(1)} %pad_maximum_fusion.3.sums_ref, f32[64,384]{1,0:T(8,128)S(1)} %get-tuple-element.31.clean_ref), custom_call_target="tpu_custom_call" | custom-call | flops 16777216 | bytes 266240 | tf_op jit(solution)/shard_map/pallas_call | solution.py:83
  (63 shorter events, 3.7 us)
Async XLA Ops:
  3.5 5.7 %collective-permute-start.10 = (f32[72,128]{1,0:T(8,128)}, f32[72,128]{1,0:T(8,128)S(1)}, u32[]{:S(2)}, u32[]{:S(2)}) collective-permute-start(f32[72,128]{1,0:T(8,128)} %get-tuple-element.24), channel_id=1, source_target_pairs={{0,8},{1,9},{2,10},{3,11},{4,12},{5,13},{6,14},{7,15},{8,0},{9,1},... | collective-permute-start | bytes 110600 | tf_op jit(solution)/shard_map/ppermute | solution.py:242
  6.6 6.5 %collective-permute-start.8 = (f32[72,128]{1,0:T(8,128)}, f32[72,128]{1,0:T(8,128)S(1)}, u32[]{:S(2)}, u32[]{:S(2)}) collective-permute-start(f32[72,128]{1,0:T(8,128)} %get-tuple-element.24), channel_id=1, source_target_pairs={{0,24},{1,25},{2,26},{3,27},{4,28},{5,29},{6,30},{7,31},{8,16},{9,... | collective-permute-start | bytes 110600 | tf_op jit(solution)/shard_map/ppermute | solution.py:242
  9.0 5.5 %collective-permute-start.9 = (f32[72,128]{1,0:T(8,128)}, f32[72,128]{1,0:T(8,128)S(1)}, u32[]{:S(2)}, u32[]{:S(2)}) collective-permute-start(f32[72,128]{1,0:T(8,128)} %get-tuple-element.24), channel_id=1, source_target_pairs={{0,16},{1,17},{2,18},{3,19},{4,20},{5,21},{6,22},{7,23},{8,24},{9,... | collective-permute-start | bytes 110600 | tf_op jit(solution)/shard_map/ppermute | solution.py:242
  15.3 7.7 %collective-permute-start.11 = (f32[288,128]{1,0:T(8,128)S(1)}, f32[288,128]{1,0:T(8,128)S(1)}, u32[]{:S(2)}, u32[]{:S(2)}) collective-permute-start(f32[288,128]{1,0:T(8,128)S(1)} %pad_maximum_fusion.1), channel_id=1, source_target_pairs={{0,6},{1,7},{2,4},{3,5},{4,2},{5,3},{6,0},{7,1},{8,14},{9,15},{10,... | collective-permute-start | bytes 442376 | tf_op jit(solution)/shard_map/ppermute | solution.py:242
  17.8 5.9 %collective-permute-start.12 = (f32[288,128]{1,0:T(8,128)S(1)}, f32[288,128]{1,0:T(8,128)S(1)}, u32[]{:S(2)}, u32[]{:S(2)}) collective-permute-start(f32[288,128]{1,0:T(8,128)S(1)} %pad_maximum_fusion.1), channel_id=1, source_target_pairs={{0,4},{1,5},{2,6},{3,7},{4,0},{5,1},{6,2},{7,3},{8,12},{9,13},{10,... | collective-permute-start | bytes 442376 | tf_op jit(solution)/shard_map/ppermute | solution.py:242
  18.3 5.5 %collective-permute-start.13 = (f32[288,128]{1,0:T(8,128)S(1)}, f32[288,128]{1,0:T(8,128)S(1)}, u32[]{:S(2)}, u32[]{:S(2)}) collective-permute-start(f32[288,128]{1,0:T(8,128)S(1)} %pad_maximum_fusion.1), channel_id=1, source_target_pairs={{0,2},{1,3},{2,0},{3,1},{4,6},{5,7},{6,4},{7,5},{8,10},{9,11},{10,... | collective-permute-start | bytes 442376 | tf_op jit(solution)/shard_map/ppermute | solution.py:242
  23.9 0.8 copy-start.11
  23.9 2.2 %copy-start.10 = (f32[64,128]{1,0:T(8,128)S(1)}, f32[64,128]{1,0:T(8,128)}, u32[]{:S(2)}) copy-start(f32[64,128]{1,0:T(8,128)} %get-tuple-element.22) | copy-start | bytes 98308
  23.9 19.3 %copy-start = (f32[256,512]{1,0:T(8,128)S(1)}, f32[256,512]{1,0:T(8,128)}, u32[]{:S(2)}) copy-start(f32[256,512]{1,0:T(8,128)} %q_leaf_ref.3) | copy-start | bytes 1572868
  23.9 19.3 %copy-start.4 = (f32[256,256]{1,0:T(8,128)S(1)}, f32[256,256]{1,0:T(8,128)}, u32[]{:S(2)}) copy-start(f32[256,256]{1,0:T(8,128)} %leaf_uinv_ref.1) | copy-start | bytes 786436
  24.0 19.3 %copy-start.3 = (f32[256,256]{1,0:T(8,128)S(1)}, f32[256,256]{1,0:T(8,128)}, u32[]{:S(2)}) copy-start(f32[256,256]{1,0:T(8,128)} %leaf_upper_ref.1) | copy-start | bytes 786436
  24.0 19.2 %collective-permute-start.14 = (f32[1152,128]{1,0:T(8,128)S(1)}, f32[1152,128]{1,0:T(8,128)S(1)}, u32[]{:S(2)}, u32[]{:S(2)}) collective-permute-start(f32[1152,128]{1,0:T(8,128)S(1)} %pad_maximum_fusion.mine_ref), channel_id=1, source_target_pairs={{0,1},{1,0},{2,3},{3,2},{4,5},{5,4},{6,7},{7,6},{8,9},{9,8},{10,11... | collective-permute-start | bytes 1769480 | tf_op jit(solution)/shard_map/ppermute | solution.py:179
  24.7 1.5 %collective-permute-start = (f32[64,128]{1,0:T(8,128)S(1)}, f32[64,128]{1,0:T(8,128)S(1)}, u32[]{:S(2)}, u32[]{:S(2)}) collective-permute-start(f32[64,128]{1,0:T(8,128)S(1)} %copy-done.11), channel_id=1, source_target_pairs={{0,1},{1,0},{2,3},{3,2},{4,5},{5,4},{6,7},{7,6},{8,9},{9,8},{10,11... | collective-permute-start | bytes 98312 | tf_op jit(solution)/shard_map/ppermute | solution.py:179
  26.1 4.0 %collective-permute-start.1 = (f32[64,128]{1,0:T(8,128)S(1)}, f32[64,128]{1,0:T(8,128)S(1)}, u32[]{:S(2)}, u32[]{:S(2)}) collective-permute-start(f32[64,128]{1,0:T(8,128)S(1)} %add.75), channel_id=1, source_target_pairs={{0,2},{1,3},{2,0},{3,1},{4,6},{5,7},{6,4},{7,5},{8,10},{9,11},{10,... | collective-permute-start | bytes 98312 | tf_op jit(solution)/shard_map/ppermute | solution.py:166
  27.7 4.3 %collective-permute-start.2 = (f32[64,128]{1,0:T(8,128)S(1)}, f32[64,128]{1,0:T(8,128)S(1)}, u32[]{:S(2)}, u32[]{:S(2)}) collective-permute-start(f32[64,128]{1,0:T(8,128)S(1)} %add.75), channel_id=1, source_target_pairs={{0,4},{1,5},{2,6},{3,7},{4,0},{5,1},{6,2},{7,3},{8,12},{9,13},{10,... | collective-permute-start | bytes 98312 | tf_op jit(solution)/shard_map/ppermute | solution.py:166
  28.5 4.8 %collective-permute-start.3 = (f32[64,128]{1,0:T(8,128)S(1)}, f32[64,128]{1,0:T(8,128)S(1)}, u32[]{:S(2)}, u32[]{:S(2)}) collective-permute-start(f32[64,128]{1,0:T(8,128)S(1)} %add.75), channel_id=1, source_target_pairs={{0,6},{1,7},{2,4},{3,5},{4,2},{5,3},{6,0},{7,1},{8,14},{9,15},{10,... | collective-permute-start | bytes 98312 | tf_op jit(solution)/shard_map/ppermute | solution.py:166
  33.3 10.0 %copy-start.7 = (f32[64,256]{1,0:T(8,128)S(1)}, f32[64,256]{1,0:T(8,128)}, u32[]{:S(2)}) copy-start(f32[64,256]{1,0:T(8,128)} %get-tuple-element.25.y_ref) | copy-start | bytes 196612
  33.3 4.5 %collective-permute-start.4 = (f32[64,128]{1,0:T(8,128)S(1)}, f32[64,128]{1,0:T(8,128)S(1)}, u32[]{:S(2)}, u32[]{:S(2)}) collective-permute-start(f32[64,128]{1,0:T(8,128)S(1)} %add_add_fusion.3), channel_id=1, source_target_pairs={{0,8},{1,9},{2,10},{3,11},{4,12},{5,13},{6,14},{7,15},{8,0},{9,1},... | collective-permute-start | bytes 98312 | tf_op jit(solution)/shard_map/ppermute | solution.py:166
  33.7 4.8 %collective-permute-start.5 = (f32[64,128]{1,0:T(8,128)S(1)}, f32[64,128]{1,0:T(8,128)S(1)}, u32[]{:S(2)}, u32[]{:S(2)}) collective-permute-start(f32[64,128]{1,0:T(8,128)S(1)} %add_add_fusion.3), channel_id=1, source_target_pairs={{0,16},{1,17},{2,18},{3,19},{4,20},{5,21},{6,22},{7,23},{8,24},{9,... | collective-permute-start | bytes 98312 | tf_op jit(solution)/shard_map/ppermute | solution.py:166
  36.2 5.7 %collective-permute-start.6 = (f32[64,128]{1,0:T(8,128)S(1)}, f32[64,128]{1,0:T(8,128)S(1)}, u32[]{:S(2)}, u32[]{:S(2)}) collective-permute-start(f32[64,128]{1,0:T(8,128)S(1)} %add_add_fusion.3), channel_id=1, source_target_pairs={{0,24},{1,25},{2,26},{3,27},{4,28},{5,29},{6,30},{7,31},{8,16},{9,... | collective-permute-start | bytes 98312 | tf_op jit(solution)/shard_map/ppermute | solution.py:166
  41.9 1.3 %copy-start.6 = (f32[8,512]{1,0:T(8,128)S(1)}, f32[8,512]{1,0:T(8,128)}, u32[]{:S(2)}) copy-start(f32[8,512]{1,0:T(8,128)} %q_root_ref.3) | copy-start | bytes 49156
  42.0 1.3 %copy-start.5 = (f32[8,512]{1,0:T(8,128)S(1)}, f32[8,512]{1,0:T(8,128)}, u32[]{:S(2)}) copy-start(f32[8,512]{1,0:T(8,128)} %q_sep_ref.3) | copy-start | bytes 49156
  42.0 1.3 %collective-permute-start.7 = (f32[64,128]{1,0:T(8,128)S(1)}, f32[64,128]{1,0:T(8,128)S(1)}, u32[]{:S(2)}, u32[]{:S(2)}) collective-permute-start(f32[64,128]{1,0:T(8,128)S(1)} %add_add_fusion.2.half_ref), channel_id=1, source_target_pairs={{0,1},{1,0},{2,3},{3,2},{4,5},{5,4},{6,7},{7,6},{8,9},{9,8},{10,11... | collective-permute-start | bytes 98312 | tf_op jit(solution)/shard_map/ppermute | solution.py:179
  42.1 1.2 %copy-start.8 = (s32[1,256]{1,0:T(1,128)S(1)}, s32[1,256]{1,0:T(1,128)}, u32[]{:S(2)}) copy-start(s32[1,256]{1,0:T(1,128)} %rows_ref.1) | copy-start | bytes 3076
  46.2 16.7 %copy-start.1 = (f32[1024,128]{1,0:T(8,128)S(1)}, f32[1024,128]{1,0:T(8,128)}, u32[]{:S(2)}) copy-start(f32[1024,128]{1,0:T(8,128)} %g_ref.1) | copy-start | bytes 1572868
  46.2 16.7 %copy-start.2 = (f32[1024,128]{1,0:T(8,128)S(1)}, f32[1024,128]{1,0:T(8,128)}, u32[]{:S(2)}) copy-start(f32[1024,128]{1,0:T(8,128)} %c_ref.1) | copy-start | bytes 1572868
  46.3 1.3 %collective-permute-start.15 = (f32[128,128]{1,0:T(8,128)S(1)}, f32[128,128]{1,0:T(8,128)S(1)}, u32[]{:S(2)}, u32[]{:S(2)}) collective-permute-start(f32[128,128]{1,0:T(8,128)S(1)} %slice_select_fusion), channel_id=1, source_target_pairs={{0,1},{1,0},{2,3},{3,2},{4,5},{5,4},{6,7},{7,6},{8,9},{9,8},{10,11... | collective-permute-start | bytes 196616 | tf_op jit(solution)/shard_map/ppermute | solution.py:179
  47.6 4.3 %collective-permute-start.16 = (f32[128,128]{1,0:T(8,128)S(1)}, f32[128,128]{1,0:T(8,128)S(1)}, u32[]{:S(2)}, u32[]{:S(2)}) collective-permute-start(f32[128,128]{1,0:T(8,128)S(1)} %select_add_fusion), channel_id=1, source_target_pairs={{0,2},{1,3},{2,0},{3,1},{4,6},{5,7},{6,4},{7,5},{8,10},{9,11},{10,... | collective-permute-start | bytes 196616 | tf_op jit(solution)/shard_map/ppermute | solution.py:166
  48.9 5.0 %collective-permute-start.17 = (f32[128,128]{1,0:T(8,128)S(1)}, f32[128,128]{1,0:T(8,128)S(1)}, u32[]{:S(2)}, u32[]{:S(2)}) collective-permute-start(f32[128,128]{1,0:T(8,128)S(1)} %select_add_fusion), channel_id=1, source_target_pairs={{0,4},{1,5},{2,6},{3,7},{4,0},{5,1},{6,2},{7,3},{8,12},{9,13},{10,... | collective-permute-start | bytes 196616 | tf_op jit(solution)/shard_map/ppermute | solution.py:166
  49.5 5.2 %collective-permute-start.18 = (f32[128,128]{1,0:T(8,128)S(1)}, f32[128,128]{1,0:T(8,128)S(1)}, u32[]{:S(2)}, u32[]{:S(2)}) collective-permute-start(f32[128,128]{1,0:T(8,128)S(1)} %select_add_fusion), channel_id=1, source_target_pairs={{0,6},{1,7},{2,4},{3,5},{4,2},{5,3},{6,0},{7,1},{8,14},{9,15},{10,... | collective-permute-start | bytes 196616 | tf_op jit(solution)/shard_map/ppermute | solution.py:166
  54.6 8.3 %copy-start.9 = (s32[2,4]{1,0:T(2,128)S(1)}, s32[2,4]{1,0:T(2,128)}, u32[]{:S(2)}) copy-start(s32[2,4]{1,0:T(2,128)} %cols_ref.1) | copy-start | bytes 100
  54.6 4.5 %collective-permute-start.19 = (f32[128,128]{1,0:T(8,128)S(1)}, f32[128,128]{1,0:T(8,128)S(1)}, u32[]{:S(2)}, u32[]{:S(2)}) collective-permute-start(f32[128,128]{1,0:T(8,128)S(1)} %add_add_fusion), channel_id=1, source_target_pairs={{0,8},{1,9},{2,10},{3,11},{4,12},{5,13},{6,14},{7,15},{8,0},{9,1},... | collective-permute-start | bytes 196616 | tf_op jit(solution)/shard_map/ppermute | solution.py:166
  54.7 5.9 %collective-permute-start.20 = (f32[128,128]{1,0:T(8,128)S(1)}, f32[128,128]{1,0:T(8,128)S(1)}, u32[]{:S(2)}, u32[]{:S(2)}) collective-permute-start(f32[128,128]{1,0:T(8,128)S(1)} %add_add_fusion), channel_id=1, source_target_pairs={{0,16},{1,17},{2,18},{3,19},{4,20},{5,21},{6,22},{7,23},{8,24},{9,... | collective-permute-start | bytes 196616 | tf_op jit(solution)/shard_map/ppermute | solution.py:166
  56.8 6.1 %collective-permute-start.21 = (f32[128,128]{1,0:T(8,128)S(1)}, f32[128,128]{1,0:T(8,128)S(1)}, u32[]{:S(2)}, u32[]{:S(2)}) collective-permute-start(f32[128,128]{1,0:T(8,128)S(1)} %add_add_fusion), channel_id=1, source_target_pairs={{0,24},{1,25},{2,26},{3,27},{4,28},{5,29},{6,30},{7,31},{8,16},{9,... | collective-permute-start | bytes 196616 | tf_op jit(solution)/shard_map/ppermute | solution.py:166
  62.9 1.3 %collective-permute-start.22 = (f32[128,128]{1,0:T(8,128)S(1)}, f32[128,128]{1,0:T(8,128)S(1)}, u32[]{:S(2)}, u32[]{:S(2)}) collective-permute-start(f32[128,128]{1,0:T(8,128)S(1)} %add_multiply_fusion), channel_id=1, source_target_pairs={{0,1},{1,0},{2,3},{3,2},{4,5},{5,4},{6,7},{7,6},{8,9},{9,8},{10,11... | collective-permute-start | bytes 196616 | tf_op jit(solution)/shard_map/ppermute | solution.py:179
  65.5 1.2 %collective-permute-start.23 = (f32[64,128]{1,0:T(8,128)S(1)}, f32[64,128]{1,0:T(8,128)S(1)}, u32[]{:S(2)}, u32[]{:S(2)}) collective-permute-start(f32[64,128]{1,0:T(8,128)S(1)} %slice_select_fusion.1), channel_id=1, source_target_pairs={{0,1},{1,0},{2,3},{3,2},{4,5},{5,4},{6,7},{7,6},{8,9},{9,8},{10,11... | collective-permute-start | bytes 98312 | tf_op jit(solution)/shard_map/ppermute | solution.py:179
  66.8 4.4 %collective-permute-start.24 = (f32[64,128]{1,0:T(8,128)S(1)}, f32[64,128]{1,0:T(8,128)S(1)}, u32[]{:S(2)}, u32[]{:S(2)}) collective-permute-start(f32[64,128]{1,0:T(8,128)S(1)} %select_add_fusion.1), channel_id=1, source_target_pairs={{0,8},{1,9},{2,10},{3,11},{4,12},{5,13},{6,14},{7,15},{8,0},{9,1},... | collective-permute-start | bytes 98312 | tf_op jit(solution)/shard_map/ppermute | solution.py:166
  66.8 4.9 %collective-permute-start.25 = (f32[64,128]{1,0:T(8,128)S(1)}, f32[64,128]{1,0:T(8,128)S(1)}, u32[]{:S(2)}, u32[]{:S(2)}) collective-permute-start(f32[64,128]{1,0:T(8,128)S(1)} %select_add_fusion.1), channel_id=1, source_target_pairs={{0,16},{1,17},{2,18},{3,19},{4,20},{5,21},{6,22},{7,23},{8,24},{9,... | collective-permute-start | bytes 98312 | tf_op jit(solution)/shard_map/ppermute | solution.py:166
  69.6 5.7 %collective-permute-start.26 = (f32[64,128]{1,0:T(8,128)S(1)}, f32[64,128]{1,0:T(8,128)S(1)}, u32[]{:S(2)}, u32[]{:S(2)}) collective-permute-start(f32[64,128]{1,0:T(8,128)S(1)} %select_add_fusion.1), channel_id=1, source_target_pairs={{0,24},{1,25},{2,26},{3,27},{4,28},{5,29},{6,30},{7,31},{8,16},{9,... | collective-permute-start | bytes 98312 | tf_op jit(solution)/shard_map/ppermute | solution.py:166
  75.4 4.3 %collective-permute-start.27 = (f32[64,128]{1,0:T(8,128)S(1)}, f32[64,128]{1,0:T(8,128)S(1)}, u32[]{:S(2)}, u32[]{:S(2)}) collective-permute-start(f32[64,128]{1,0:T(8,128)S(1)} %add_add_fusion.1), channel_id=1, source_target_pairs={{0,2},{1,3},{2,0},{3,1},{4,6},{5,7},{6,4},{7,5},{8,10},{9,11},{10,... | collective-permute-start | bytes 98312 | tf_op jit(solution)/shard_map/ppermute | solution.py:166
  77.0 3.9 %collective-permute-start.28 = (f32[64,128]{1,0:T(8,128)S(1)}, f32[64,128]{1,0:T(8,128)S(1)}, u32[]{:S(2)}, u32[]{:S(2)}) collective-permute-start(f32[64,128]{1,0:T(8,128)S(1)} %add_add_fusion.1), channel_id=1, source_target_pairs={{0,4},{1,5},{2,6},{3,7},{4,0},{5,1},{6,2},{7,3},{8,12},{9,13},{10,... | collective-permute-start | bytes 98312 | tf_op jit(solution)/shard_map/ppermute | solution.py:166
  77.7 4.8 %collective-permute-start.29 = (f32[64,128]{1,0:T(8,128)S(1)}, f32[64,128]{1,0:T(8,128)S(1)}, u32[]{:S(2)}, u32[]{:S(2)}) collective-permute-start(f32[64,128]{1,0:T(8,128)S(1)} %add_add_fusion.1), channel_id=1, source_target_pairs={{0,6},{1,7},{2,4},{3,5},{4,2},{5,3},{6,0},{7,1},{8,14},{9,15},{10,... | collective-permute-start | bytes 98312 | tf_op jit(solution)/shard_map/ppermute | solution.py:166
  82.5 1.3 %collective-permute-start.30 = (f32[64,128]{1,0:T(8,128)S(1)}, f32[64,128]{1,0:T(8,128)S(1)}, u32[]{:S(2)}, u32[]{:S(2)}) collective-permute-start(f32[64,128]{1,0:T(8,128)S(1)} %add_multiply_fusion.1), channel_id=1, source_target_pairs={{0,1},{1,0},{2,3},{3,2},{4,5},{5,4},{6,7},{7,6},{8,9},{9,8},{10,11... | collective-permute-start | bytes 98312 | tf_op jit(solution)/shard_map/ppermute | solution.py:179

commit v4 on v3

--- a/solution.py
+++ b/solution.py
@@ -294,6 +294,25 @@
     out_ref[...] = halves_up(jnp.concatenate([sep, lower, upper, root, extra], axis=1))
 
 
+def fold_kernel(
+    at_ref, y_ref, rows_ref, upper_ref, uinv_ref, q_ref, q_sep_ref, y_out_ref, carry_ref
+):
+    extent = y_ref.shape[1]
+    width = carry_ref.shape[0]
+    hits = (iota((width, extent), 0) == rows_ref[...]).astype(jnp.float32)
+    carried = dot_nt(hits, upper_ref[...])
+    both = jnp.concatenate([y_ref[...], carried], axis=0)
+    solved = dot_nt(both, uinv_ref[...])
+    projected = dot_nn(solved, q_ref[...])
+    ports = y_ref.shape[0]
+    y_out_ref[:, :extent] = solved[:ports]
+    y_out_ref[:, extent:] = projected[:ports]
+    carry_ref[:, :extent] = solved[ports:]
+    carry_ref[:, extent:] = projected[ports:]
+    own = pl.ds(pl.multiple_of(at_ref[0], SUBLANES), q_sep_ref.shape[0])
+    carry_ref[own, extent:] = carry_ref[own, extent:] - q_sep_ref[...]
+
+
 def solve_kernel(
     places,
     at_ref,
@@ -302,16 +321,12 @@
     mine_ref,
     other_ref,
     y_ref,
-    rows_ref,
-    leaf_upper_ref,
-    leaf_uinv_ref,
-    q_leaf_ref,
-    q_sep_ref,
+    carry_ref,
     q_root_ref,
     x_ref,
     partial_ref,
 ):
-    ports, extent = y_ref.shape
+    ports = y_ref.shape[0]
     own_rows = SUBLANES
     width = 2 * len(places) * own_rows
     tall = mine_ref.shape[0] // len(places)
@@ -350,20 +365,16 @@
     y_root = dot_nt(b_root - dot_nn(y_sep, piece(width, width)), root_l)
     x_root = dot_nt(y_root, root_u)
     x_sep = dot_nt(y_sep - dot_nt(x_root, piece(2 * width, width)), sep_u)
-    hits = (iota((width, extent), 0) == rows_ref[...]).astype(jnp.float32)
-    coupled = dot_nn(x_sep, hits)
-    x_leaf = dot_nt(y_ref[...] - dot_nt(coupled, leaf_upper_ref[...]), leaf_uinv_ref[...])
     own = iota((LANES, width), 1) - at_ref[0] == iota((LANES, width), 0)
-    own = own & (iota((LANES, width), 0) < own_rows)
-    shifted = iota((LANES, width), 1) - at_ref[0] == iota((LANES, width), 0) - own_rows
-    shifted = shifted & (iota((LANES, width), 0) >= own_rows)
-    shifted = shifted & (iota((LANES, width), 0) < 2 * own_rows)
-    x_own = dot_nt(x_sep, own.astype(jnp.float32)) + dot_nt(x_root, shifted.astype(jnp.float32))
-    x_ref[:, :extent] = x_leaf
-    x_ref[:, extent:] = x_own
-    q_own = jnp.concatenate([q_sep_ref[...], q_root_ref[...]], axis=0)
-    partial = dot_nn(x_leaf, q_leaf_ref[...]) + dot_nn(x_own[:, : 2 * own_rows], q_own)
-    partial_ref[...] = halves_up(partial)
+    own = (own & (iota((LANES, width), 0) < own_rows)).astype(jnp.float32)
+    root_own = dot_nt(x_root, own)[:, :own_rows]
+    folded = y_ref[...] - dot_nn(x_sep, carry_ref[...])
+    extent = y_ref.shape[1] - q_root_ref.shape[1]
+    partial_ref[...] = halves_up(folded[:, extent:] + dot_nn(root_own, q_root_ref[...]))
+    x_ref[:, :extent] = folded[:, :extent]
+    sep_own = dot_nt(x_sep, own)[:, :own_rows]
+    pad = jnp.zeros((ports, LANES - 2 * own_rows), jnp.float32)
+    x_ref[:, extent:] = jnp.concatenate([sep_own, root_own, pad], axis=1)
 
 
 def dense_kernel(cols_ref, g_ref, c_ref, g_out_ref, c_out_ref):
@@ -393,14 +404,13 @@
     own = x_ref[:, extent:] - dot_nt(coef, q_own)
     clean_out[:, :extent] = leaf
     clean_out[:, extent:] = own
-    g_image = dot_nt(leaf, g_ref[...])
-    c_image = dot_nt(leaf, c_ref[...])
-    products = dot_nt(leaf, jnp.concatenate([leaf, g_image, c_image], axis=0))
+    images = dot_nt(leaf, jnp.concatenate([g_ref[...], c_ref[...]], axis=0))
+    products = dot_nt(
+        leaf, jnp.concatenate([leaf, images[:, :extent], images[:, extent:]], axis=0)
+    )
     gram = products[:, :ports] + dot_nt(own, own)
     out_ref[:ports, :] = jnp.concatenate([gram, products[:, ports : 2 * ports]], axis=1)
-    out_ref[ports:, :] = jnp.concatenate(
-        [products[:, 2 * ports :], jnp.zeros((ports, LANES - ports), jnp.float32)], axis=1
-    )
+    out_ref[ports:, :] = jnp.concatenate([gram, products[:, 2 * ports :]], axis=1)
 
 
 def eliminate(tiles, offset, step):
@@ -442,39 +452,58 @@
     return tiles
 
 
-def tail_kernel(
-    sums_ref, clean_ref, v_leaf_ref, v_sep_ref, v_root_ref, g_ref, c_ref
-):
-    ports = clean_ref.shape[0]
-    extent = v_leaf_ref.shape[1]
-    own_rows = v_sep_ref.shape[0]
+def factor_kernel(half_ref, inverse_ref):
+    ports = inverse_ref.shape[0]
     diagonal = iota((ports, ports), 0) == iota((ports, ports), 1)
-    gram = sums_ref[:ports, :ports]
-    joined = jnp.concatenate([jnp.where(diagonal, 1.0, 0.0), gram], axis=1)
+    joined = jnp.concatenate([jnp.where(diagonal, 1.0, 0.0), half_ref[:, :ports]], axis=1)
     tiles = [joined[at : at + SUBLANES] for at in range(0, ports, SUBLANES)]
     joined = jnp.concatenate(eliminate(tiles, ports, SUBLANES), axis=0)
     pivots = jnp.sum(jnp.where(diagonal, joined[:, ports:], 0.0), axis=1, keepdims=True)
     inverse = joined[:, :ports] / jnp.sqrt(pivots)
-    v_leaf_ref[...] = dot_nn(inverse, clean_ref[:, :extent])
-    own = dot_nn(inverse, clean_ref[:, extent:]).T
+    inverse_ref[...] = inverse
+
+
+def finish_kernel(
+    at_ref, half_ref, pair_ref, inverse_ref, clean_ref, v_leaf_ref, v_sep_ref, v_root_ref, g_ref, c_ref
+):
+    ports = inverse_ref.shape[0]
+    extent = v_leaf_ref.shape[1]
+    own_rows = v_sep_ref.shape[0]
+    inverse = inverse_ref[...]
+    left = dot_nn(
+        inverse,
+        jnp.concatenate([half_ref[:, ports:], pair_ref[:, ports:], clean_ref[...]], axis=1),
+    )
+    v_leaf_ref[...] = left[:, LANES : LANES + extent]
+    own = left[:, LANES + extent :].T
     v_sep_ref[...] = own[:own_rows]
     v_root_ref[...] = own[own_rows : 2 * own_rows]
-    g_sum = sums_ref[:ports, ports : 2 * ports]
-    c_sum = sums_ref[ports:, :ports]
-    g_ref[...] = dot_nt(dot_nn(inverse, g_sum), inverse)
-    c_ref[...] = dot_nt(dot_nn(inverse, c_sum), inverse)
+    left = jnp.concatenate([left[:, :ports], left[:, ports : 2 * ports]], axis=0)
+    whole = dot_nt(left, inverse)
+    odd = at_ref[0] == 1
+    g_ref[...] = jnp.where(odd, whole[ports:], whole[:ports])
+    c_ref[...] = jnp.where(odd, whole[:ports], whole[ports:])
 
 
 def solve_replicated(at, kept, sent, packed, y_leaf, late):
     ports, extent = y_leaf.shape
     basis = late[-1].shape[1]
+    rows, upper, uinv, q_leaf, q_sep, q_root = late
+    width = 2 * kept.shape[0] // ports * LANES
+    folded, carry = call(
+        fold_kernel,
+        [shape_of(ports, extent + basis), shape_of(width, extent + basis)],
+        [at, y_leaf, rows, upper, uinv, q_leaf, q_sep],
+        scalars=1,
+        flops=30 * extent * extent * ports,
+    )
     mine, other, places = gather_rows(packed, GROUP)
     half = half_by_hops(kept, sent, GROUP, FIRST_UPWARD)
     pair = swap_pair(half, GROUP)
     return call(
         functools.partial(solve_kernel, places),
         [shape_of(ports, extent + LANES), shape_of(basis // LANES * ports, LANES)],
-        [at, half, pair, mine, other, y_leaf, *late],
+        [at, half, pair, mine, other, folded, carry, q_root],
         scalars=1,
         flops=22 * extent * extent * ports,
     )
@@ -601,9 +630,17 @@
         [coefficients, x_all, basis_leaf, basis_sep, basis_root, g_dense, c_dense],
         flops=14 * square,
     )
-    sums = sum_all(products, EVERYONE, 1.0 / node_count, False)
+    parity = (lax.axis_index(EVERYONE) % 2).astype(jnp.int32).reshape(1)
+    if by_hops(count):
+        kept, sent = halves_of(products, EVERYONE)
+        half = half_by_hops(kept, sent, EVERYONE, False) * (1.0 / node_count)
+        pair = swap_pair(half, EVERYONE)
+    else:
+        sums = sum_over(products, EVERYONE, 1.0 / node_count)
+        half, pair = halves_of(sums, EVERYONE)
+    (inverse,) = call(factor_kernel, [shape_of(ports, ports)], [half])
     v_leaf, v_sep, v_root, g_out, c_out = call(
-        tail_kernel,
+        finish_kernel,
         [
             shape_of(ports, extent),
             shape_of(sep_local, ports),
@@ -611,7 +648,8 @@
             shape_of(ports, ports),
             shape_of(ports, ports),
         ],
-        [sums, cleaned],
+        [parity, half, pair, inverse, cleaned],
+        scalars=1,
         flops=4 * square,
     )
     return (v_leaf.T, v_sep, v_root, coef_out.T, g_out, c_out)

time: 87.5 us -> 87 us (level)
  waiting for transfers between devices: 39.5 us -> 37 us
  Pallas kernels: 11.1 us -> 12.1 us
    ppermute x7, waiting for transfers between devices: 6.49 us -> 3.94 us  [swap_pair(): lax.ppermute(value, axes, [(source, source ^ 1) for source in range(count)])]
    pallas_call x5 -> x7, Pallas kernels: 11.1 us -> 12.1 us  [call(): pl.pallas_call(body, out_shape=outs, in_specs=specs, out_specs=[WHOLE] *...]
  transfers between devices with their start and end apart: 31 -> 31, of which waited for: 25 -> 23; matrix products, arithmetic and copies ran while one was open for 0% -> 0% of each run, Pallas kernels for 1% -> 5%
where the time goes in v4:
time: 87 us; the launch traced here: 86.7 us
  waiting for transfers between devices  37 us (43%)
  starting transfers between devices  34.3 us (39%)
  Pallas kernels  12.1 us (14%)
  local copies, waits for them, and re-layouts  1.27 us (1%)
  other arithmetic  1.08 us (1%)
  between operations  1.02 us (1%)
    ppermute x18, starting transfers between devices, hop(): total = total + lax.ppermute(value, axes, pairs)  23.9 us
    ppermute x18, waiting for transfers between devices, hop(): total = total + lax.ppermute(value, axes, pairs)  22.8 us
    pallas_call x7, Pallas kernels, call(): pl.pallas_call(body, out_shape=outs, in_specs=specs, out_specs=[WHOLE] *...  12.1 us
    ppermute x6, waiting for transfers between devices, gather_rows(): blocks.append(lax.ppermute(held, axes, pairs))  10.3 us
    ppermute x6, starting transfers between devices, gather_rows(): blocks.append(lax.ppermute(held, axes, pairs))  9.26 us
    ppermute x7, waiting for transfers between devices, swap_pair(): lax.ppermute(value, axes, [(source, source ^ 1) for source in range(count)])  3.94 us
  transfers between devices with their start and end apart: 31, of which 23 were waited for; matrix products, arithmetic and copies ran while one was open for 0% of the time, Pallas kernels for 5%

profile of v4, /device:TPU:0, one launch (start us, length us, event | category | flops | bytes accessed | tf_op | source)
XLA Modules:
  0.0 86.7 jit_solution(10653374785246123325)
XLA Ops:
  0.6 2.8 %shard_map.235 = (f32[64,256]{1,0:T(8,128)}, f32[64,128]{1,0:T(8,128)}, f32[64,128]{1,0:T(8,128)}, f32[72,128]{1,0:T(8,128)}) custom-call(s32[1]{0:T(128)} %bitcast.1.at_ref, f32[64,256]{1,0:T(8,128)} %bitcast.6, f32[256,256]{1,0:T(8,128)} %refs_1_.1, f32[256,256]{1,0:T(8,128)} %refs_2_.1, s32[1,256]{1,0:T(1,128)} %rows_ref.1, f32[8,64]{1,0:T(8,128)} %refs_4_.1, ...), custom_call_target="tpu_custom_call" | custom-call | flops 25165824 | bytes 812036 | tf_op jit(solution)/shard_map/pallas_call | solution.py:83
  3.5 3.1 %collective-permute-start.10 = (f32[72,128]{1,0:T(8,128)}, f32[72,128]{1,0:T(8,128)S(1)}, u32[]{:S(2)}, u32[]{:S(2)}) collective-permute-start(f32[72,128]{1,0:T(8,128)} %get-tuple-element.26), channel_id=1, source_target_pairs={{0,8},{1,9},{2,10},{3,11},{4,12},{5,13},{6,14},{7,15},{8,0},{9,1},... | collective-permute-start | bytes 110600 | tf_op jit(solution)/shard_map/ppermute | solution.py:242
  6.6 2.5 %collective-permute-start.8 = (f32[72,128]{1,0:T(8,128)}, f32[72,128]{1,0:T(8,128)S(1)}, u32[]{:S(2)}, u32[]{:S(2)}) collective-permute-start(f32[72,128]{1,0:T(8,128)} %get-tuple-element.26), channel_id=1, source_target_pairs={{0,24},{1,25},{2,26},{3,27},{4,28},{5,29},{6,30},{7,31},{8,16},{9,... | collective-permute-start | bytes 110600 | tf_op jit(solution)/shard_map/ppermute | solution.py:242
  9.2 3.9 %collective-permute-done.8 = f32[72,128]{1,0:T(8,128)S(1)} collective-permute-done((f32[72,128]{1,0:T(8,128)}, f32[72,128]{1,0:T(8,128)S(1)}, u32[]{:S(2)}, u32[]{:S(2)}) %collective-permute-start.8) | collective-permute-done | bytes 36896 | tf_op jit(solution)/shard_map/ppermute | solution.py:242
  13.0 1.5 %collective-permute-done.9 = f32[72,128]{1,0:T(8,128)S(1)} collective-permute-done((f32[72,128]{1,0:T(8,128)}, f32[72,128]{1,0:T(8,128)S(1)}, u32[]{:S(2)}, u32[]{:S(2)}) %collective-permute-start.9) | collective-permute-done | bytes 36896 | tf_op jit(solution)/shard_map/ppermute | solution.py:242
  14.5 0.8 broadcast_select_fusion.17
  15.3 2.5 %collective-permute-start.11 = (f32[288,128]{1,0:T(8,128)S(1)}, f32[288,128]{1,0:T(8,128)S(1)}, u32[]{:S(2)}, u32[]{:S(2)}) collective-permute-start(f32[288,128]{1,0:T(8,128)S(1)} %pad_maximum_fusion.1), channel_id=1, source_target_pairs={{0,6},{1,7},{2,4},{3,5},{4,2},{5,3},{6,0},{7,1},{8,14},{9,15},{10,... | collective-permute-start | bytes 442376 | tf_op jit(solution)/shard_map/ppermute | solution.py:242
  18.9 4.1 %collective-permute-done.11 = f32[288,128]{1,0:T(8,128)S(1)} collective-permute-done((f32[288,128]{1,0:T(8,128)S(1)}, f32[288,128]{1,0:T(8,128)S(1)}, u32[]{:S(2)}, u32[]{:S(2)}) %collective-permute-start.11) | collective-permute-done | bytes 147488 | tf_op jit(solution)/shard_map/ppermute | solution.py:242
  23.0 0.8 collective-permute-done.12
  24.1 0.6 copy-done.11
  24.7 1.5 %collective-permute-done = f32[64,128]{1,0:T(8,128)S(1)} collective-permute-done((f32[64,128]{1,0:T(8,128)S(1)}, f32[64,128]{1,0:T(8,128)S(1)}, u32[]{:S(2)}, u32[]{:S(2)}) %collective-permute-start) | collective-permute-done | bytes 32800 | tf_op jit(solution)/shard_map/ppermute | solution.py:179
  26.1 1.6 %collective-permute-start.1 = (f32[64,128]{1,0:T(8,128)S(1)}, f32[64,128]{1,0:T(8,128)S(1)}, u32[]{:S(2)}, u32[]{:S(2)}) collective-permute-start(f32[64,128]{1,0:T(8,128)S(1)} %add.75), channel_id=1, source_target_pairs={{0,2},{1,3},{2,0},{3,1},{4,6},{5,7},{6,4},{7,5},{8,10},{9,11},{10,... | collective-permute-start | bytes 98312 | tf_op jit(solution)/shard_map/ppermute | solution.py:166
  27.7 0.7 collective-permute-start.2
  28.5 1.2 %collective-permute-start.3 = (f32[64,128]{1,0:T(8,128)S(1)}, f32[64,128]{1,0:T(8,128)S(1)}, u32[]{:S(2)}, u32[]{:S(2)}) collective-permute-start(f32[64,128]{1,0:T(8,128)S(1)} %add.75), channel_id=1, source_target_pairs={{0,6},{1,7},{2,4},{3,5},{4,2},{5,3},{6,0},{7,1},{8,14},{9,15},{10,... | collective-permute-start | bytes 98312 | tf_op jit(solution)/shard_map/ppermute | solution.py:166
  30.1 1.9 %collective-permute-done.2 = f32[64,128]{1,0:T(8,128)S(1)} collective-permute-done((f32[64,128]{1,0:T(8,128)S(1)}, f32[64,128]{1,0:T(8,128)S(1)}, u32[]{:S(2)}, u32[]{:S(2)}) %collective-permute-start.2) | collective-permute-done | bytes 32800 | tf_op jit(solution)/shard_map/ppermute | solution.py:166
  32.0 1.3 %collective-permute-done.3 = f32[64,128]{1,0:T(8,128)S(1)} collective-permute-done((f32[64,128]{1,0:T(8,128)S(1)}, f32[64,128]{1,0:T(8,128)S(1)}, u32[]{:S(2)}, u32[]{:S(2)}) %collective-permute-start.3) | collective-permute-done | bytes 32800 | tf_op jit(solution)/shard_map/ppermute | solution.py:166
  33.7 2.5 %collective-permute-start.5 = (f32[64,128]{1,0:T(8,128)S(1)}, f32[64,128]{1,0:T(8,128)S(1)}, u32[]{:S(2)}, u32[]{:S(2)}) collective-permute-start(f32[64,128]{1,0:T(8,128)S(1)} %add_add_fusion.3), channel_id=1, source_target_pairs={{0,16},{1,17},{2,18},{3,19},{4,20},{5,21},{6,22},{7,23},{8,24},{9,... | collective-permute-start | bytes 98312 | tf_op jit(solution)/shard_map/ppermute | solution.py:166
  36.2 1.5 %collective-permute-start.6 = (f32[64,128]{1,0:T(8,128)S(1)}, f32[64,128]{1,0:T(8,128)S(1)}, u32[]{:S(2)}, u32[]{:S(2)}) collective-permute-start(f32[64,128]{1,0:T(8,128)S(1)} %add_add_fusion.3), channel_id=1, source_target_pairs={{0,24},{1,25},{2,26},{3,27},{4,28},{5,29},{6,30},{7,31},{8,16},{9,... | collective-permute-start | bytes 98312 | tf_op jit(solution)/shard_map/ppermute | solution.py:166
  37.8 0.8 collective-permute-done.5
  38.5 3.4 %collective-permute-done.6 = f32[64,128]{1,0:T(8,128)S(1)} collective-permute-done((f32[64,128]{1,0:T(8,128)S(1)}, f32[64,128]{1,0:T(8,128)S(1)}, u32[]{:S(2)}, u32[]{:S(2)}) %collective-permute-start.6) | collective-permute-done | bytes 32800 | tf_op jit(solution)/shard_map/ppermute | solution.py:166
  42.1 0.6 copy-done.5
  42.7 1.7 %shard_map.236 = (f32[64,768]{1,0:T(8,128)S(1)}, f32[256,768]{1,0:T(8,128)S(1)}) custom-call(s32[1]{0:T(128)} %bitcast.1.at_ref, f32[64,256]{1,0:T(8,128)S(1)} %copy-done.7, s32[1,256]{1,0:T(1,128)S(1)} %copy-done.8, f32[256,256]{1,0:T(8,128)S(1)} %copy-done.3, f32[256,256]{1,0:T(8,128)S(1)} %copy-done.4, f32[256,512]{1,0:T(8,128)S(1)} %copy-done, ...), custom_call_target="tpu_custom_call" | custom-call | flops 125829120 | bytes 2114564 | tf_op jit(solution)/shard_map/pallas_call | solution.py:83
  44.5 2.2 %shard_map.237 = (f32[64,384]{1,0:T(8,128)S(1)}, f32[256,128]{1,0:T(8,128)S(1)}) custom-call(s32[1]{0:T(128)} %bitcast.1.at_ref, f32[64,128]{1,0:T(8,128)S(1)} %add_add_fusion.2.half_ref, f32[64,128]{1,0:T(8,128)S(1)} %collective-permute-done.7.pair_ref, f32[1152,128]{1,0:T(8,128)S(1)} %pad_maximum_fusion.mine_ref, ...), custom_call_target="tpu_custom_call" | custom-call | flops 92274688 | bytes 2473988 | tf_op jit(solution)/shard_map/pallas_call | solution.py:83
  47.2 0.9 %collective-permute-done.15 = f32[128,128]{1,0:T(8,128)S(1)} collective-permute-done((f32[128,128]{1,0:T(8,128)S(1)}, f32[128,128]{1,0:T(8,128)S(1)}, u32[]{:S(2)}, u32[]{:S(2)}) %collective-permute-start.15) | collective-permute-done | bytes 65568 | tf_op jit(solution)/shard_map/ppermute | solution.py:179
  48.2 1.3 %collective-permute-start.16 = (f32[128,128]{1,0:T(8,128)S(1)}, f32[128,128]{1,0:T(8,128)S(1)}, u32[]{:S(2)}, u32[]{:S(2)}) collective-permute-start(f32[128,128]{1,0:T(8,128)S(1)} %select_add_fusion), channel_id=1, source_target_pairs={{0,2},{1,3},{2,0},{3,1},{4,6},{5,7},{6,4},{7,5},{8,10},{9,11},{10,... | collective-permute-start | bytes 196616 | tf_op jit(solution)/shard_map/ppermute | solution.py:166
  49.5 0.6 collective-permute-start.17
  50.0 1.7 %collective-permute-start.18 = (f32[128,128]{1,0:T(8,128)S(1)}, f32[128,128]{1,0:T(8,128)S(1)}, u32[]{:S(2)}, u32[]{:S(2)}) collective-permute-start(f32[128,128]{1,0:T(8,128)S(1)} %select_add_fusion), channel_id=1, source_target_pairs={{0,6},{1,7},{2,4},{3,5},{4,2},{5,3},{6,0},{7,1},{8,14},{9,15},{10,... | collective-permute-start | bytes 196616 | tf_op jit(solution)/shard_map/ppermute | solution.py:166
  51.7 0.9 collective-permute-done.16
  52.6 1.9 %collective-permute-done.17 = f32[128,128]{1,0:T(8,128)S(1)} collective-permute-done((f32[128,128]{1,0:T(8,128)S(1)}, f32[128,128]{1,0:T(8,128)S(1)}, u32[]{:S(2)}, u32[]{:S(2)}) %collective-permute-start.17) | collective-permute-done | bytes 65568 | tf_op jit(solution)/shard_map/ppermute | solution.py:166
  54.4 0.8 collective-permute-done.18
  55.3 2.1 %collective-permute-start.20 = (f32[128,128]{1,0:T(8,128)S(1)}, f32[128,128]{1,0:T(8,128)S(1)}, u32[]{:S(2)}, u32[]{:S(2)}) collective-permute-start(f32[128,128]{1,0:T(8,128)S(1)} %add_add_fusion), channel_id=1, source_target_pairs={{0,16},{1,17},{2,18},{3,19},{4,20},{5,21},{6,22},{7,23},{8,24},{9,... | collective-permute-start | bytes 196616 | tf_op jit(solution)/shard_map/ppermute | solution.py:166
  57.4 2.3 %collective-permute-start.21 = (f32[128,128]{1,0:T(8,128)S(1)}, f32[128,128]{1,0:T(8,128)S(1)}, u32[]{:S(2)}, u32[]{:S(2)}) collective-permute-start(f32[128,128]{1,0:T(8,128)S(1)} %add_add_fusion), channel_id=1, source_target_pairs={{0,24},{1,25},{2,26},{3,27},{4,28},{5,29},{6,30},{7,31},{8,16},{9,... | collective-permute-start | bytes 196616 | tf_op jit(solution)/shard_map/ppermute | solution.py:166
  59.7 1.6 %collective-permute-done.20 = f32[128,128]{1,0:T(8,128)S(1)} collective-permute-done((f32[128,128]{1,0:T(8,128)S(1)}, f32[128,128]{1,0:T(8,128)S(1)}, u32[]{:S(2)}, u32[]{:S(2)}) %collective-permute-start.20) | collective-permute-done | bytes 65568 | tf_op jit(solution)/shard_map/ppermute | solution.py:166
  61.2 2.2 %collective-permute-done.21 = f32[128,128]{1,0:T(8,128)S(1)} collective-permute-done((f32[128,128]{1,0:T(8,128)S(1)}, f32[128,128]{1,0:T(8,128)S(1)}, u32[]{:S(2)}, u32[]{:S(2)}) %collective-permute-start.21) | collective-permute-done | bytes 65568 | tf_op jit(solution)/shard_map/ppermute | solution.py:166
  63.6 0.7 shard_map.238
  64.8 1.4 %shard_map.239 = (f32[64,512]{1,0:T(8,128)}, f32[64,384]{1,0:T(8,128)S(1)}, f32[128,128]{1,0:T(8,128)S(1)}) custom-call(f32[256,128]{1,0:T(8,128)S(1)} %pad_maximum_fusion.2.coef_ref, f32[64,384]{1,0:T(8,128)S(1)} %get-tuple-element.31.x_ref, f32[256,512]{1,0:T(8,128)S(1)} %copy-done, f32[8,512]{1,0:T(8,128)S(1)} %copy-done.5, f32[8,512]{1,0:T(8,128)S(1)} %copy-done.6, ...), custom_call_target="tpu_custom_call" | custom-call | flops 58720256 | bytes 1605632 | tf_op jit(solution)/shard_map/pallas_call | solution.py:83
  66.4 1.0 %collective-permute-done.23 = f32[64,128]{1,0:T(8,128)S(1)} collective-permute-done((f32[64,128]{1,0:T(8,128)S(1)}, f32[64,128]{1,0:T(8,128)S(1)}, u32[]{:S(2)}, u32[]{:S(2)}) %collective-permute-start.23) | collective-permute-done | bytes 32800 | tf_op jit(solution)/shard_map/ppermute | solution.py:179
  67.5 2.9 %collective-permute-start.25 = (f32[64,128]{1,0:T(8,128)S(1)}, f32[64,128]{1,0:T(8,128)S(1)}, u32[]{:S(2)}, u32[]{:S(2)}) collective-permute-start(f32[64,128]{1,0:T(8,128)S(1)} %select_add_fusion.1), channel_id=1, source_target_pairs={{0,16},{1,17},{2,18},{3,19},{4,20},{5,21},{6,22},{7,23},{8,24},{9,... | collective-permute-start | bytes 98312 | tf_op jit(solution)/shard_map/ppermute | solution.py:166
  70.3 1.5 %collective-permute-start.26 = (f32[64,128]{1,0:T(8,128)S(1)}, f32[64,128]{1,0:T(8,128)S(1)}, u32[]{:S(2)}, u32[]{:S(2)}) collective-permute-start(f32[64,128]{1,0:T(8,128)S(1)} %select_add_fusion.1), channel_id=1, source_target_pairs={{0,24},{1,25},{2,26},{3,27},{4,28},{5,29},{6,30},{7,31},{8,16},{9,... | collective-permute-start | bytes 98312 | tf_op jit(solution)/shard_map/ppermute | solution.py:166
  72.4 3.6 %collective-permute-done.26 = f32[64,128]{1,0:T(8,128)S(1)} collective-permute-done((f32[64,128]{1,0:T(8,128)S(1)}, f32[64,128]{1,0:T(8,128)S(1)}, u32[]{:S(2)}, u32[]{:S(2)}) %collective-permute-start.26) | collective-permute-done | bytes 32800 | tf_op jit(solution)/shard_map/ppermute | solution.py:166
  76.1 1.6 %collective-permute-start.27 = (f32[64,128]{1,0:T(8,128)S(1)}, f32[64,128]{1,0:T(8,128)S(1)}, u32[]{:S(2)}, u32[]{:S(2)}) collective-permute-start(f32[64,128]{1,0:T(8,128)S(1)} %add_add_fusion.1), channel_id=1, source_target_pairs={{0,2},{1,3},{2,0},{3,1},{4,6},{5,7},{6,4},{7,5},{8,10},{9,11},{10,... | collective-permute-start | bytes 98312 | tf_op jit(solution)/shard_map/ppermute | solution.py:166
  77.7 0.7 collective-permute-start.28
  78.4 1.2 %collective-permute-start.29 = (f32[64,128]{1,0:T(8,128)S(1)}, f32[64,128]{1,0:T(8,128)S(1)}, u32[]{:S(2)}, u32[]{:S(2)}) collective-permute-start(f32[64,128]{1,0:T(8,128)S(1)} %add_add_fusion.1), channel_id=1, source_target_pairs={{0,6},{1,7},{2,4},{3,5},{4,2},{5,3},{6,0},{7,1},{8,14},{9,15},{10,... | collective-permute-start | bytes 98312 | tf_op jit(solution)/shard_map/ppermute | solution.py:166
  79.6 0.7 collective-permute-done.27
  80.3 1.3 %collective-permute-done.28 = f32[64,128]{1,0:T(8,128)S(1)} collective-permute-done((f32[64,128]{1,0:T(8,128)S(1)}, f32[64,128]{1,0:T(8,128)S(1)}, u32[]{:S(2)}, u32[]{:S(2)}) %collective-permute-start.28) | collective-permute-done | bytes 32800 | tf_op jit(solution)/shard_map/ppermute | solution.py:166
  81.6 1.6 %collective-permute-done.29 = f32[64,128]{1,0:T(8,128)S(1)} collective-permute-done((f32[64,128]{1,0:T(8,128)S(1)}, f32[64,128]{1,0:T(8,128)S(1)}, u32[]{:S(2)}, u32[]{:S(2)}) %collective-permute-start.29) | collective-permute-done | bytes 32800 | tf_op jit(solution)/shard_map/ppermute | solution.py:166
  83.3 2.2 %shard_map.240.inverse_ref = f32[64,64]{1,0:T(8,128)S(1)} custom-call(f32[64,128]{1,0:T(8,128)S(1)} %add_multiply_fusion.1.half_ref), custom_call_target="tpu_custom_call" | custom-call | bytes 49152 | tf_op jit(solution)/shard_map/pallas_call | solution.py:83
  85.5 1.2 %shard_map.241 = (f32[64,256]{1,0:T(8,128)}, f32[8,64]{1,0:T(8,128)}, f32[8,64]{1,0:T(8,128)}, f32[64,64]{1,0:T(8,128)}, f32[64,64]{1,0:T(8,128)}) custom-call(s32[1]{0:T(128)} %bitcast.at_ref, f32[64,128]{1,0:T(8,128)S(1)} %add_multiply_fusion.1.half_ref, f32[64,128]{1,0:T(8,128)S(1)} %collective-permute-done.30.pair_ref, ...), custom_call_target="tpu_custom_call" | custom-call | flops 16777216 | bytes 282628 | tf_op jit(solution)/shard_map/pallas_call | solution.py:83
  (63 shorter events, 4.7 us)
Async XLA Ops:
  3.5 5.7 %collective-permute-start.10 = (f32[72,128]{1,0:T(8,128)}, f32[72,128]{1,0:T(8,128)S(1)}, u32[]{:S(2)}, u32[]{:S(2)}) collective-permute-start(f32[72,128]{1,0:T(8,128)} %get-tuple-element.26), channel_id=1, source_target_pairs={{0,8},{1,9},{2,10},{3,11},{4,12},{5,13},{6,14},{7,15},{8,0},{9,1},... | collective-permute-start | bytes 110600 | tf_op jit(solution)/shard_map/ppermute | solution.py:242
  6.6 6.5 %collective-permute-start.8 = (f32[72,128]{1,0:T(8,128)}, f32[72,128]{1,0:T(8,128)S(1)}, u32[]{:S(2)}, u32[]{:S(2)}) collective-permute-start(f32[72,128]{1,0:T(8,128)} %get-tuple-element.26), channel_id=1, source_target_pairs={{0,24},{1,25},{2,26},{3,27},{4,28},{5,29},{6,30},{7,31},{8,16},{9,... | collective-permute-start | bytes 110600 | tf_op jit(solution)/shard_map/ppermute | solution.py:242
  9.1 5.5 %collective-permute-start.9 = (f32[72,128]{1,0:T(8,128)}, f32[72,128]{1,0:T(8,128)S(1)}, u32[]{:S(2)}, u32[]{:S(2)}) collective-permute-start(f32[72,128]{1,0:T(8,128)} %get-tuple-element.26), channel_id=1, source_target_pairs={{0,16},{1,17},{2,18},{3,19},{4,20},{5,21},{6,22},{7,23},{8,24},{9,... | collective-permute-start | bytes 110600 | tf_op jit(solution)/shard_map/ppermute | solution.py:242
  15.3 7.7 %collective-permute-start.11 = (f32[288,128]{1,0:T(8,128)S(1)}, f32[288,128]{1,0:T(8,128)S(1)}, u32[]{:S(2)}, u32[]{:S(2)}) collective-permute-start(f32[288,128]{1,0:T(8,128)S(1)} %pad_maximum_fusion.1), channel_id=1, source_target_pairs={{0,6},{1,7},{2,4},{3,5},{4,2},{5,3},{6,0},{7,1},{8,14},{9,15},{10,... | collective-permute-start | bytes 442376 | tf_op jit(solution)/shard_map/ppermute | solution.py:242
  17.8 5.9 %collective-permute-start.12 = (f32[288,128]{1,0:T(8,128)S(1)}, f32[288,128]{1,0:T(8,128)S(1)}, u32[]{:S(2)}, u32[]{:S(2)}) collective-permute-start(f32[288,128]{1,0:T(8,128)S(1)} %pad_maximum_fusion.1), channel_id=1, source_target_pairs={{0,4},{1,5},{2,6},{3,7},{4,0},{5,1},{6,2},{7,3},{8,12},{9,13},{10,... | collective-permute-start | bytes 442376 | tf_op jit(solution)/shard_map/ppermute | solution.py:242
  18.3 5.4 %collective-permute-start.13 = (f32[288,128]{1,0:T(8,128)S(1)}, f32[288,128]{1,0:T(8,128)S(1)}, u32[]{:S(2)}, u32[]{:S(2)}) collective-permute-start(f32[288,128]{1,0:T(8,128)S(1)} %pad_maximum_fusion.1), channel_id=1, source_target_pairs={{0,2},{1,3},{2,0},{3,1},{4,6},{5,7},{6,4},{7,5},{8,10},{9,11},{10,... | collective-permute-start | bytes 442376 | tf_op jit(solution)/shard_map/ppermute | solution.py:242
  23.9 0.8 copy-start.11
  23.9 2.2 %copy-start.10 = (f32[64,128]{1,0:T(8,128)S(1)}, f32[64,128]{1,0:T(8,128)}, u32[]{:S(2)}) copy-start(f32[64,128]{1,0:T(8,128)} %get-tuple-element.24) | copy-start | bytes 98308
  23.9 18.2 %copy-start = (f32[256,512]{1,0:T(8,128)S(1)}, f32[256,512]{1,0:T(8,128)}, u32[]{:S(2)}) copy-start(f32[256,512]{1,0:T(8,128)} %q_leaf_ref.1) | copy-start | bytes 1572868
  23.9 18.2 %copy-start.4 = (f32[256,256]{1,0:T(8,128)S(1)}, f32[256,256]{1,0:T(8,128)}, u32[]{:S(2)}) copy-start(f32[256,256]{1,0:T(8,128)} %uinv_ref.1) | copy-start | bytes 786436
  24.0 18.1 %copy-start.3 = (f32[256,256]{1,0:T(8,128)S(1)}, f32[256,256]{1,0:T(8,128)}, u32[]{:S(2)}) copy-start(f32[256,256]{1,0:T(8,128)} %upper_ref.1) | copy-start | bytes 786436
  24.0 20.5 %collective-permute-start.14 = (f32[1152,128]{1,0:T(8,128)S(1)}, f32[1152,128]{1,0:T(8,128)S(1)}, u32[]{:S(2)}, u32[]{:S(2)}) collective-permute-start(f32[1152,128]{1,0:T(8,128)S(1)} %pad_maximum_fusion.mine_ref), channel_id=1, source_target_pairs={{0,1},{1,0},{2,3},{3,2},{4,5},{5,4},{6,7},{7,6},{8,9},{9,8},{10,11... | collective-permute-start | bytes 1769480 | tf_op jit(solution)/shard_map/ppermute | solution.py:179
  24.7 1.5 %collective-permute-start = (f32[64,128]{1,0:T(8,128)S(1)}, f32[64,128]{1,0:T(8,128)S(1)}, u32[]{:S(2)}, u32[]{:S(2)}) collective-permute-start(f32[64,128]{1,0:T(8,128)S(1)} %copy-done.11), channel_id=1, source_target_pairs={{0,1},{1,0},{2,3},{3,2},{4,5},{5,4},{6,7},{7,6},{8,9},{9,8},{10,11... | collective-permute-start | bytes 98312 | tf_op jit(solution)/shard_map/ppermute | solution.py:179
  26.1 4.0 %collective-permute-start.1 = (f32[64,128]{1,0:T(8,128)S(1)}, f32[64,128]{1,0:T(8,128)S(1)}, u32[]{:S(2)}, u32[]{:S(2)}) collective-permute-start(f32[64,128]{1,0:T(8,128)S(1)} %add.75), channel_id=1, source_target_pairs={{0,2},{1,3},{2,0},{3,1},{4,6},{5,7},{6,4},{7,5},{8,10},{9,11},{10,... | collective-permute-start | bytes 98312 | tf_op jit(solution)/shard_map/ppermute | solution.py:166
  27.7 4.3 %collective-permute-start.2 = (f32[64,128]{1,0:T(8,128)S(1)}, f32[64,128]{1,0:T(8,128)S(1)}, u32[]{:S(2)}, u32[]{:S(2)}) collective-permute-start(f32[64,128]{1,0:T(8,128)S(1)} %add.75), channel_id=1, source_target_pairs={{0,4},{1,5},{2,6},{3,7},{4,0},{5,1},{6,2},{7,3},{8,12},{9,13},{10,... | collective-permute-start | bytes 98312 | tf_op jit(solution)/shard_map/ppermute | solution.py:166
  28.5 4.8 %collective-permute-start.3 = (f32[64,128]{1,0:T(8,128)S(1)}, f32[64,128]{1,0:T(8,128)S(1)}, u32[]{:S(2)}, u32[]{:S(2)}) collective-permute-start(f32[64,128]{1,0:T(8,128)S(1)} %add.75), channel_id=1, source_target_pairs={{0,6},{1,7},{2,4},{3,5},{4,2},{5,3},{6,0},{7,1},{8,14},{9,15},{10,... | collective-permute-start | bytes 98312 | tf_op jit(solution)/shard_map/ppermute | solution.py:166
  33.3 8.8 %copy-start.7 = (f32[64,256]{1,0:T(8,128)S(1)}, f32[64,256]{1,0:T(8,128)}, u32[]{:S(2)}) copy-start(f32[64,256]{1,0:T(8,128)} %get-tuple-element.27.y_ref) | copy-start | bytes 196612
  33.3 4.5 %collective-permute-start.4 = (f32[64,128]{1,0:T(8,128)S(1)}, f32[64,128]{1,0:T(8,128)S(1)}, u32[]{:S(2)}, u32[]{:S(2)}) collective-permute-start(f32[64,128]{1,0:T(8,128)S(1)} %add_add_fusion.3), channel_id=1, source_target_pairs={{0,8},{1,9},{2,10},{3,11},{4,12},{5,13},{6,14},{7,15},{8,0},{9,1},... | collective-permute-start | bytes 98312 | tf_op jit(solution)/shard_map/ppermute | solution.py:166
  33.7 4.8 %collective-permute-start.5 = (f32[64,128]{1,0:T(8,128)S(1)}, f32[64,128]{1,0:T(8,128)S(1)}, u32[]{:S(2)}, u32[]{:S(2)}) collective-permute-start(f32[64,128]{1,0:T(8,128)S(1)} %add_add_fusion.3), channel_id=1, source_target_pairs={{0,16},{1,17},{2,18},{3,19},{4,20},{5,21},{6,22},{7,23},{8,24},{9,... | collective-permute-start | bytes 98312 | tf_op jit(solution)/shard_map/ppermute | solution.py:166
  36.2 5.7 %collective-permute-start.6 = (f32[64,128]{1,0:T(8,128)S(1)}, f32[64,128]{1,0:T(8,128)S(1)}, u32[]{:S(2)}, u32[]{:S(2)}) collective-permute-start(f32[64,128]{1,0:T(8,128)S(1)} %add_add_fusion.3), channel_id=1, source_target_pairs={{0,24},{1,25},{2,26},{3,27},{4,28},{5,29},{6,30},{7,31},{8,16},{9,... | collective-permute-start | bytes 98312 | tf_op jit(solution)/shard_map/ppermute | solution.py:166
  42.0 0.7 copy-start.5
  42.0 2.5 %collective-permute-start.7 = (f32[64,128]{1,0:T(8,128)S(1)}, f32[64,128]{1,0:T(8,128)S(1)}, u32[]{:S(2)}, u32[]{:S(2)}) collective-permute-start(f32[64,128]{1,0:T(8,128)S(1)} %add_add_fusion.2.half_ref), channel_id=1, source_target_pairs={{0,1},{1,0},{2,3},{3,2},{4,5},{5,4},{6,7},{7,6},{8,9},{9,8},{10,11... | collective-permute-start | bytes 98312 | tf_op jit(solution)/shard_map/ppermute | solution.py:179
  42.1 0.7 copy-start.8
  42.7 1.7 %copy-start.6 = (f32[8,512]{1,0:T(8,128)S(1)}, f32[8,512]{1,0:T(8,128)}, u32[]{:S(2)}) copy-start(f32[8,512]{1,0:T(8,128)} %q_root_ref.3) | copy-start | bytes 49156
  46.7 16.9 %copy-start.1 = (f32[1024,128]{1,0:T(8,128)S(1)}, f32[1024,128]{1,0:T(8,128)}, u32[]{:S(2)}) copy-start(f32[1024,128]{1,0:T(8,128)} %g_ref.1) | copy-start | bytes 1572868
  46.7 16.9 %copy-start.2 = (f32[1024,128]{1,0:T(8,128)S(1)}, f32[1024,128]{1,0:T(8,128)}, u32[]{:S(2)}) copy-start(f32[1024,128]{1,0:T(8,128)} %c_ref.1) | copy-start | bytes 1572868
  46.7 1.4 %collective-permute-start.15 = (f32[128,128]{1,0:T(8,128)S(1)}, f32[128,128]{1,0:T(8,128)S(1)}, u32[]{:S(2)}, u32[]{:S(2)}) collective-permute-start(f32[128,128]{1,0:T(8,128)S(1)} %slice_select_fusion), channel_id=1, source_target_pairs={{0,1},{1,0},{2,3},{3,2},{4,5},{5,4},{6,7},{7,6},{8,9},{9,8},{10,11... | collective-permute-start | bytes 196616 | tf_op jit(solution)/shard_map/ppermute | solution.py:179
  48.2 4.4 %collective-permute-start.16 = (f32[128,128]{1,0:T(8,128)S(1)}, f32[128,128]{1,0:T(8,128)S(1)}, u32[]{:S(2)}, u32[]{:S(2)}) collective-permute-start(f32[128,128]{1,0:T(8,128)S(1)} %select_add_fusion), channel_id=1, source_target_pairs={{0,2},{1,3},{2,0},{3,1},{4,6},{5,7},{6,4},{7,5},{8,10},{9,11},{10,... | collective-permute-start | bytes 196616 | tf_op jit(solution)/shard_map/ppermute | solution.py:166
  49.5 5.0 %collective-permute-start.17 = (f32[128,128]{1,0:T(8,128)S(1)}, f32[128,128]{1,0:T(8,128)S(1)}, u32[]{:S(2)}, u32[]{:S(2)}) collective-permute-start(f32[128,128]{1,0:T(8,128)S(1)} %select_add_fusion), channel_id=1, source_target_pairs={{0,4},{1,5},{2,6},{3,7},{4,0},{5,1},{6,2},{7,3},{8,12},{9,13},{10,... | collective-permute-start | bytes 196616 | tf_op jit(solution)/shard_map/ppermute | solution.py:166
  50.0 5.2 %collective-permute-start.18 = (f32[128,128]{1,0:T(8,128)S(1)}, f32[128,128]{1,0:T(8,128)S(1)}, u32[]{:S(2)}, u32[]{:S(2)}) collective-permute-start(f32[128,128]{1,0:T(8,128)S(1)} %select_add_fusion), channel_id=1, source_target_pairs={{0,6},{1,7},{2,4},{3,5},{4,2},{5,3},{6,0},{7,1},{8,14},{9,15},{10,... | collective-permute-start | bytes 196616 | tf_op jit(solution)/shard_map/ppermute | solution.py:166
  55.2 8.3 %copy-start.9 = (s32[2,4]{1,0:T(2,128)S(1)}, s32[2,4]{1,0:T(2,128)}, u32[]{:S(2)}) copy-start(s32[2,4]{1,0:T(2,128)} %cols_ref.1) | copy-start | bytes 100
  55.2 4.5 %collective-permute-start.19 = (f32[128,128]{1,0:T(8,128)S(1)}, f32[128,128]{1,0:T(8,128)S(1)}, u32[]{:S(2)}, u32[]{:S(2)}) collective-permute-start(f32[128,128]{1,0:T(8,128)S(1)} %add_add_fusion), channel_id=1, source_target_pairs={{0,8},{1,9},{2,10},{3,11},{4,12},{5,13},{6,14},{7,15},{8,0},{9,1},... | collective-permute-start | bytes 196616 | tf_op jit(solution)/shard_map/ppermute | solution.py:166
  55.3 5.9 %collective-permute-start.20 = (f32[128,128]{1,0:T(8,128)S(1)}, f32[128,128]{1,0:T(8,128)S(1)}, u32[]{:S(2)}, u32[]{:S(2)}) collective-permute-start(f32[128,128]{1,0:T(8,128)S(1)} %add_add_fusion), channel_id=1, source_target_pairs={{0,16},{1,17},{2,18},{3,19},{4,20},{5,21},{6,22},{7,23},{8,24},{9,... | collective-permute-start | bytes 196616 | tf_op jit(solution)/shard_map/ppermute | solution.py:166
  57.4 6.1 %collective-permute-start.21 = (f32[128,128]{1,0:T(8,128)S(1)}, f32[128,128]{1,0:T(8,128)S(1)}, u32[]{:S(2)}, u32[]{:S(2)}) collective-permute-start(f32[128,128]{1,0:T(8,128)S(1)} %add_add_fusion), channel_id=1, source_target_pairs={{0,24},{1,25},{2,26},{3,27},{4,28},{5,29},{6,30},{7,31},{8,16},{9,... | collective-permute-start | bytes 196616 | tf_op jit(solution)/shard_map/ppermute | solution.py:166
  63.4 1.3 %collective-permute-start.22 = (f32[128,128]{1,0:T(8,128)S(1)}, f32[128,128]{1,0:T(8,128)S(1)}, u32[]{:S(2)}, u32[]{:S(2)}) collective-permute-start(f32[128,128]{1,0:T(8,128)S(1)} %add_multiply_fusion), channel_id=1, source_target_pairs={{0,1},{1,0},{2,3},{3,2},{4,5},{5,4},{6,7},{7,6},{8,9},{9,8},{10,11... | collective-permute-start | bytes 196616 | tf_op jit(solution)/shard_map/ppermute | solution.py:179
  66.2 1.3 %collective-permute-start.23 = (f32[64,128]{1,0:T(8,128)S(1)}, f32[64,128]{1,0:T(8,128)S(1)}, u32[]{:S(2)}, u32[]{:S(2)}) collective-permute-start(f32[64,128]{1,0:T(8,128)S(1)} %slice_select_fusion.1), channel_id=1, source_target_pairs={{0,1},{1,0},{2,3},{3,2},{4,5},{5,4},{6,7},{7,6},{8,9},{9,8},{10,11... | collective-permute-start | bytes 98312 | tf_op jit(solution)/shard_map/ppermute | solution.py:179
  67.5 4.4 %collective-permute-start.24 = (f32[64,128]{1,0:T(8,128)S(1)}, f32[64,128]{1,0:T(8,128)S(1)}, u32[]{:S(2)}, u32[]{:S(2)}) collective-permute-start(f32[64,128]{1,0:T(8,128)S(1)} %select_add_fusion.1), channel_id=1, source_target_pairs={{0,8},{1,9},{2,10},{3,11},{4,12},{5,13},{6,14},{7,15},{8,0},{9,1},... | collective-permute-start | bytes 98312 | tf_op jit(solution)/shard_map/ppermute | solution.py:166
  67.5 4.9 %collective-permute-start.25 = (f32[64,128]{1,0:T(8,128)S(1)}, f32[64,128]{1,0:T(8,128)S(1)}, u32[]{:S(2)}, u32[]{:S(2)}) collective-permute-start(f32[64,128]{1,0:T(8,128)S(1)} %select_add_fusion.1), channel_id=1, source_target_pairs={{0,16},{1,17},{2,18},{3,19},{4,20},{5,21},{6,22},{7,23},{8,24},{9,... | collective-permute-start | bytes 98312 | tf_op jit(solution)/shard_map/ppermute | solution.py:166
  70.3 5.7 %collective-permute-start.26 = (f32[64,128]{1,0:T(8,128)S(1)}, f32[64,128]{1,0:T(8,128)S(1)}, u32[]{:S(2)}, u32[]{:S(2)}) collective-permute-start(f32[64,128]{1,0:T(8,128)S(1)} %select_add_fusion.1), channel_id=1, source_target_pairs={{0,24},{1,25},{2,26},{3,27},{4,28},{5,29},{6,30},{7,31},{8,16},{9,... | collective-permute-start | bytes 98312 | tf_op jit(solution)/shard_map/ppermute | solution.py:166
  76.1 4.3 %collective-permute-start.27 = (f32[64,128]{1,0:T(8,128)S(1)}, f32[64,128]{1,0:T(8,128)S(1)}, u32[]{:S(2)}, u32[]{:S(2)}) collective-permute-start(f32[64,128]{1,0:T(8,128)S(1)} %add_add_fusion.1), channel_id=1, source_target_pairs={{0,2},{1,3},{2,0},{3,1},{4,6},{5,7},{6,4},{7,5},{8,10},{9,11},{10,... | collective-permute-start | bytes 98312 | tf_op jit(solution)/shard_map/ppermute | solution.py:166
  77.7 3.9 %collective-permute-start.28 = (f32[64,128]{1,0:T(8,128)S(1)}, f32[64,128]{1,0:T(8,128)S(1)}, u32[]{:S(2)}, u32[]{:S(2)}) collective-permute-start(f32[64,128]{1,0:T(8,128)S(1)} %add_add_fusion.1), channel_id=1, source_target_pairs={{0,4},{1,5},{2,6},{3,7},{4,0},{5,1},{6,2},{7,3},{8,12},{9,13},{10,... | collective-permute-start | bytes 98312 | tf_op jit(solution)/shard_map/ppermute | solution.py:166
  78.4 4.8 %collective-permute-start.29 = (f32[64,128]{1,0:T(8,128)S(1)}, f32[64,128]{1,0:T(8,128)S(1)}, u32[]{:S(2)}, u32[]{:S(2)}) collective-permute-start(f32[64,128]{1,0:T(8,128)S(1)} %add_add_fusion.1), channel_id=1, source_target_pairs={{0,6},{1,7},{2,4},{3,5},{4,2},{5,3},{6,0},{7,1},{8,14},{9,15},{10,... | collective-permute-start | bytes 98312 | tf_op jit(solution)/shard_map/ppermute | solution.py:166
  83.2 2.3 %collective-permute-start.30 = (f32[64,128]{1,0:T(8,128)S(1)}, f32[64,128]{1,0:T(8,128)S(1)}, u32[]{:S(2)}, u32[]{:S(2)}) collective-permute-start(f32[64,128]{1,0:T(8,128)S(1)} %add_multiply_fusion.1.half_ref), channel_id=1, source_target_pairs={{0,1},{1,0},{2,3},{3,2},{4,5},{5,4},{6,7},{7,6},{8,9},{9,8},{10,11... | collective-permute-start | bytes 98312 | tf_op jit(solution)/shard_map/ppermute | solution.py:179

commit v5 on v4

--- a/solution.py
+++ b/solution.py
@@ -34,20 +34,16 @@
 
 def parts_of(value):
     high = value.astype(jnp.bfloat16)
-    rest = value - high.astype(jnp.float32)
-    middle = rest.astype(jnp.bfloat16)
-    return high, middle, (rest - middle.astype(jnp.float32)).astype(jnp.bfloat16)
+    return high, (value - high.astype(jnp.float32)).astype(jnp.bfloat16)
 
 
 def dot_parts(left, right, right_dim):
     rows = left.shape[0]
-    high, middle, low = parts_of(left)
-    first, second, third = parts_of(right)
-    three = contract(jnp.concatenate([high, middle, low], axis=0), first, 1, right_dim, None)
-    two = contract(jnp.concatenate([high, middle], axis=0), second, 1, right_dim, None)
-    one = contract(high, third, 1, right_dim, None)
-    small = three[2 * rows :] + two[rows:] + one
-    return three[:rows] + ((three[rows : 2 * rows] + two[:rows]) + small)
+    high, middle = parts_of(left)
+    first, second = parts_of(right)
+    two = contract(jnp.concatenate([high, middle], axis=0), first, 1, right_dim, None)
+    one = contract(high, second, 1, right_dim, None)
+    return two[:rows] + (two[rows:] + one)
 
 
 def dot_nn(left, right):

time: 87 us -> 85.1 us (0.978)
  Pallas kernels: 12.1 us -> 10.3 us
    pallas_call x7, Pallas kernels: 12.1 us -> 10.3 us  [call(): pl.pallas_call(body, out_shape=outs, in_specs=specs, out_specs=[WHOLE] *...]
where the time goes in v5:
time: 85.1 us; the launch traced here: 84.8 us
  waiting for transfers between devices  37 us (43%)
  starting transfers between devices  34.2 us (40%)
  Pallas kernels  10.3 us (12%)
  local copies, waits for them, and re-layouts  1.27 us (1%)
  other arithmetic  1.08 us (1%)
  between operations  1 us (1%)
    ppermute x18, starting transfers between devices, hop(): total = total + lax.ppermute(value, axes, pairs)  23.9 us
    ppermute x18, waiting for transfers between devices, hop(): total = total + lax.ppermute(value, axes, pairs)  22.8 us
    pallas_call x7, Pallas kernels, call(): pl.pallas_call(body, out_shape=outs, in_specs=specs, out_specs=[WHOLE] *...  10.3 us
    ppermute x6, waiting for transfers between devices, gather_rows(): blocks.append(lax.ppermute(held, axes, pairs))  10.3 us
    ppermute x6, starting transfers between devices, gather_rows(): blocks.append(lax.ppermute(held, axes, pairs))  9.26 us
    ppermute x7, waiting for transfers between devices, swap_pair(): lax.ppermute(value, axes, [(source, source ^ 1) for source in range(count)])  3.94 us
  transfers between devices with their start and end apart: 31, of which 23 were waited for; matrix products, arithmetic and copies ran while one was open for 0% of the time, Pallas kernels for 5%

profile of v5, /device:TPU:0, one launch (start us, length us, event | category | flops | bytes accessed | tf_op | source)
XLA Modules:
  0.0 84.8 jit_solution(10588267953754094238)
XLA Ops:
  0.6 2.7 %shard_map.235 = (f32[64,256]{1,0:T(8,128)}, f32[64,128]{1,0:T(8,128)}, f32[64,128]{1,0:T(8,128)}, f32[72,128]{1,0:T(8,128)}) custom-call(s32[1]{0:T(128)} %bitcast.1.at_ref, f32[64,256]{1,0:T(8,128)} %bitcast.6, f32[256,256]{1,0:T(8,128)} %refs_1_.1, f32[256,256]{1,0:T(8,128)} %refs_2_.1, s32[1,256]{1,0:T(1,128)} %rows_ref.1, f32[8,64]{1,0:T(8,128)} %refs_4_.1, ...), custom_call_target="tpu_custom_call" | custom-call | flops 25165824 | bytes 812036 | tf_op jit(solution)/shard_map/pallas_call | solution.py:79
  3.3 3.1 %collective-permute-start.10 = (f32[72,128]{1,0:T(8,128)}, f32[72,128]{1,0:T(8,128)S(1)}, u32[]{:S(2)}, u32[]{:S(2)}) collective-permute-start(f32[72,128]{1,0:T(8,128)} %get-tuple-element.26), channel_id=1, source_target_pairs={{0,8},{1,9},{2,10},{3,11},{4,12},{5,13},{6,14},{7,15},{8,0},{9,1},... | collective-permute-start | bytes 110600 | tf_op jit(solution)/shard_map/ppermute | solution.py:238
  6.4 2.5 %collective-permute-start.8 = (f32[72,128]{1,0:T(8,128)}, f32[72,128]{1,0:T(8,128)S(1)}, u32[]{:S(2)}, u32[]{:S(2)}) collective-permute-start(f32[72,128]{1,0:T(8,128)} %get-tuple-element.26), channel_id=1, source_target_pairs={{0,24},{1,25},{2,26},{3,27},{4,28},{5,29},{6,30},{7,31},{8,16},{9,... | collective-permute-start | bytes 110600 | tf_op jit(solution)/shard_map/ppermute | solution.py:238
  9.0 3.9 %collective-permute-done.8 = f32[72,128]{1,0:T(8,128)S(1)} collective-permute-done((f32[72,128]{1,0:T(8,128)}, f32[72,128]{1,0:T(8,128)S(1)}, u32[]{:S(2)}, u32[]{:S(2)}) %collective-permute-start.8) | collective-permute-done | bytes 36896 | tf_op jit(solution)/shard_map/ppermute | solution.py:238
  12.9 1.5 %collective-permute-done.9 = f32[72,128]{1,0:T(8,128)S(1)} collective-permute-done((f32[72,128]{1,0:T(8,128)}, f32[72,128]{1,0:T(8,128)S(1)}, u32[]{:S(2)}, u32[]{:S(2)}) %collective-permute-start.9) | collective-permute-done | bytes 36896 | tf_op jit(solution)/shard_map/ppermute | solution.py:238
  14.4 0.8 broadcast_select_fusion.17
  15.2 2.5 %collective-permute-start.11 = (f32[288,128]{1,0:T(8,128)S(1)}, f32[288,128]{1,0:T(8,128)S(1)}, u32[]{:S(2)}, u32[]{:S(2)}) collective-permute-start(f32[288,128]{1,0:T(8,128)S(1)} %pad_maximum_fusion.1), channel_id=1, source_target_pairs={{0,6},{1,7},{2,4},{3,5},{4,2},{5,3},{6,0},{7,1},{8,14},{9,15},{10,... | collective-permute-start | bytes 442376 | tf_op jit(solution)/shard_map/ppermute | solution.py:238
  18.7 4.1 %collective-permute-done.11 = f32[288,128]{1,0:T(8,128)S(1)} collective-permute-done((f32[288,128]{1,0:T(8,128)S(1)}, f32[288,128]{1,0:T(8,128)S(1)}, u32[]{:S(2)}, u32[]{:S(2)}) %collective-permute-start.11) | collective-permute-done | bytes 147488 | tf_op jit(solution)/shard_map/ppermute | solution.py:238
  22.8 0.8 collective-permute-done.12
  23.9 0.6 copy-done.11
  24.5 1.5 %collective-permute-done = f32[64,128]{1,0:T(8,128)S(1)} collective-permute-done((f32[64,128]{1,0:T(8,128)S(1)}, f32[64,128]{1,0:T(8,128)S(1)}, u32[]{:S(2)}, u32[]{:S(2)}) %collective-permute-start) | collective-permute-done | bytes 32800 | tf_op jit(solution)/shard_map/ppermute | solution.py:175
  26.0 1.6 %collective-permute-start.1 = (f32[64,128]{1,0:T(8,128)S(1)}, f32[64,128]{1,0:T(8,128)S(1)}, u32[]{:S(2)}, u32[]{:S(2)}) collective-permute-start(f32[64,128]{1,0:T(8,128)S(1)} %add.75), channel_id=1, source_target_pairs={{0,2},{1,3},{2,0},{3,1},{4,6},{5,7},{6,4},{7,5},{8,10},{9,11},{10,... | collective-permute-start | bytes 98312 | tf_op jit(solution)/shard_map/ppermute | solution.py:162
  27.6 0.7 collective-permute-start.2
  28.3 1.2 %collective-permute-start.3 = (f32[64,128]{1,0:T(8,128)S(1)}, f32[64,128]{1,0:T(8,128)S(1)}, u32[]{:S(2)}, u32[]{:S(2)}) collective-permute-start(f32[64,128]{1,0:T(8,128)S(1)} %add.75), channel_id=1, source_target_pairs={{0,6},{1,7},{2,4},{3,5},{4,2},{5,3},{6,0},{7,1},{8,14},{9,15},{10,... | collective-permute-start | bytes 98312 | tf_op jit(solution)/shard_map/ppermute | solution.py:162
  30.0 1.9 %collective-permute-done.2 = f32[64,128]{1,0:T(8,128)S(1)} collective-permute-done((f32[64,128]{1,0:T(8,128)S(1)}, f32[64,128]{1,0:T(8,128)S(1)}, u32[]{:S(2)}, u32[]{:S(2)}) %collective-permute-start.2) | collective-permute-done | bytes 32800 | tf_op jit(solution)/shard_map/ppermute | solution.py:162
  31.8 1.3 %collective-permute-done.3 = f32[64,128]{1,0:T(8,128)S(1)} collective-permute-done((f32[64,128]{1,0:T(8,128)S(1)}, f32[64,128]{1,0:T(8,128)S(1)}, u32[]{:S(2)}, u32[]{:S(2)}) %collective-permute-start.3) | collective-permute-done | bytes 32800 | tf_op jit(solution)/shard_map/ppermute | solution.py:162
  33.6 2.5 %collective-permute-start.5 = (f32[64,128]{1,0:T(8,128)S(1)}, f32[64,128]{1,0:T(8,128)S(1)}, u32[]{:S(2)}, u32[]{:S(2)}) collective-permute-start(f32[64,128]{1,0:T(8,128)S(1)} %add_add_fusion.3), channel_id=1, source_target_pairs={{0,16},{1,17},{2,18},{3,19},{4,20},{5,21},{6,22},{7,23},{8,24},{9,... | collective-permute-start | bytes 98312 | tf_op jit(solution)/shard_map/ppermute | solution.py:162
  36.1 1.5 %collective-permute-start.6 = (f32[64,128]{1,0:T(8,128)S(1)}, f32[64,128]{1,0:T(8,128)S(1)}, u32[]{:S(2)}, u32[]{:S(2)}) collective-permute-start(f32[64,128]{1,0:T(8,128)S(1)} %add_add_fusion.3), channel_id=1, source_target_pairs={{0,24},{1,25},{2,26},{3,27},{4,28},{5,29},{6,30},{7,31},{8,16},{9,... | collective-permute-start | bytes 98312 | tf_op jit(solution)/shard_map/ppermute | solution.py:162
  37.6 0.8 collective-permute-done.5
  38.4 3.4 %collective-permute-done.6 = f32[64,128]{1,0:T(8,128)S(1)} collective-permute-done((f32[64,128]{1,0:T(8,128)S(1)}, f32[64,128]{1,0:T(8,128)S(1)}, u32[]{:S(2)}, u32[]{:S(2)}) %collective-permute-start.6) | collective-permute-done | bytes 32800 | tf_op jit(solution)/shard_map/ppermute | solution.py:162
  42.0 0.6 copy-done.5
  42.6 1.0 %shard_map.236 = (f32[64,768]{1,0:T(8,128)S(1)}, f32[256,768]{1,0:T(8,128)S(1)}) custom-call(s32[1]{0:T(128)} %bitcast.1.at_ref, f32[64,256]{1,0:T(8,128)S(1)} %copy-done.7, s32[1,256]{1,0:T(1,128)S(1)} %copy-done.8, f32[256,256]{1,0:T(8,128)S(1)} %copy-done.3, f32[256,256]{1,0:T(8,128)S(1)} %copy-done.4, f32[256,512]{1,0:T(8,128)S(1)} %copy-done, ...), custom_call_target="tpu_custom_call" | custom-call | flops 125829120 | bytes 2114564 | tf_op jit(solution)/shard_map/pallas_call | solution.py:79
  43.6 1.6 %shard_map.237 = (f32[64,384]{1,0:T(8,128)S(1)}, f32[256,128]{1,0:T(8,128)S(1)}) custom-call(s32[1]{0:T(128)} %bitcast.1.at_ref, f32[64,128]{1,0:T(8,128)S(1)} %add_add_fusion.2.half_ref, f32[64,128]{1,0:T(8,128)S(1)} %collective-permute-done.7.pair_ref, f32[1152,128]{1,0:T(8,128)S(1)} %pad_maximum_fusion.mine_ref, ...), custom_call_target="tpu_custom_call" | custom-call | flops 92274688 | bytes 2473988 | tf_op jit(solution)/shard_map/pallas_call | solution.py:79
  45.8 0.9 %collective-permute-done.15 = f32[128,128]{1,0:T(8,128)S(1)} collective-permute-done((f32[128,128]{1,0:T(8,128)S(1)}, f32[128,128]{1,0:T(8,128)S(1)}, u32[]{:S(2)}, u32[]{:S(2)}) %collective-permute-start.15) | collective-permute-done | bytes 65568 | tf_op jit(solution)/shard_map/ppermute | solution.py:175
  46.7 1.3 %collective-permute-start.16 = (f32[128,128]{1,0:T(8,128)S(1)}, f32[128,128]{1,0:T(8,128)S(1)}, u32[]{:S(2)}, u32[]{:S(2)}) collective-permute-start(f32[128,128]{1,0:T(8,128)S(1)} %select_add_fusion), channel_id=1, source_target_pairs={{0,2},{1,3},{2,0},{3,1},{4,6},{5,7},{6,4},{7,5},{8,10},{9,11},{10,... | collective-permute-start | bytes 196616 | tf_op jit(solution)/shard_map/ppermute | solution.py:162
  48.0 0.6 collective-permute-start.17
  48.6 1.7 %collective-permute-start.18 = (f32[128,128]{1,0:T(8,128)S(1)}, f32[128,128]{1,0:T(8,128)S(1)}, u32[]{:S(2)}, u32[]{:S(2)}) collective-permute-start(f32[128,128]{1,0:T(8,128)S(1)} %select_add_fusion), channel_id=1, source_target_pairs={{0,6},{1,7},{2,4},{3,5},{4,2},{5,3},{6,0},{7,1},{8,14},{9,15},{10,... | collective-permute-start | bytes 196616 | tf_op jit(solution)/shard_map/ppermute | solution.py:162
  50.3 0.9 %collective-permute-done.16 = f32[128,128]{1,0:T(8,128)S(1)} collective-permute-done((f32[128,128]{1,0:T(8,128)S(1)}, f32[128,128]{1,0:T(8,128)S(1)}, u32[]{:S(2)}, u32[]{:S(2)}) %collective-permute-start.16) | collective-permute-done | bytes 65568 | tf_op jit(solution)/shard_map/ppermute | solution.py:162
  51.2 1.9 %collective-permute-done.17 = f32[128,128]{1,0:T(8,128)S(1)} collective-permute-done((f32[128,128]{1,0:T(8,128)S(1)}, f32[128,128]{1,0:T(8,128)S(1)}, u32[]{:S(2)}, u32[]{:S(2)}) %collective-permute-start.17) | collective-permute-done | bytes 65568 | tf_op jit(solution)/shard_map/ppermute | solution.py:162
  53.0 0.8 collective-permute-done.18
  53.9 2.1 %collective-permute-start.20 = (f32[128,128]{1,0:T(8,128)S(1)}, f32[128,128]{1,0:T(8,128)S(1)}, u32[]{:S(2)}, u32[]{:S(2)}) collective-permute-start(f32[128,128]{1,0:T(8,128)S(1)} %add_add_fusion), channel_id=1, source_target_pairs={{0,16},{1,17},{2,18},{3,19},{4,20},{5,21},{6,22},{7,23},{8,24},{9,... | collective-permute-start | bytes 196616 | tf_op jit(solution)/shard_map/ppermute | solution.py:162
  56.0 2.3 %collective-permute-start.21 = (f32[128,128]{1,0:T(8,128)S(1)}, f32[128,128]{1,0:T(8,128)S(1)}, u32[]{:S(2)}, u32[]{:S(2)}) collective-permute-start(f32[128,128]{1,0:T(8,128)S(1)} %add_add_fusion), channel_id=1, source_target_pairs={{0,24},{1,25},{2,26},{3,27},{4,28},{5,29},{6,30},{7,31},{8,16},{9,... | collective-permute-start | bytes 196616 | tf_op jit(solution)/shard_map/ppermute | solution.py:162
  58.3 1.6 %collective-permute-done.20 = f32[128,128]{1,0:T(8,128)S(1)} collective-permute-done((f32[128,128]{1,0:T(8,128)S(1)}, f32[128,128]{1,0:T(8,128)S(1)}, u32[]{:S(2)}, u32[]{:S(2)}) %collective-permute-start.20) | collective-permute-done | bytes 65568 | tf_op jit(solution)/shard_map/ppermute | solution.py:162
  59.8 2.2 %collective-permute-done.21 = f32[128,128]{1,0:T(8,128)S(1)} collective-permute-done((f32[128,128]{1,0:T(8,128)S(1)}, f32[128,128]{1,0:T(8,128)S(1)}, u32[]{:S(2)}, u32[]{:S(2)}) %collective-permute-start.21) | collective-permute-done | bytes 65568 | tf_op jit(solution)/shard_map/ppermute | solution.py:162
  62.1 0.7 shard_map.238
  63.4 1.1 %shard_map.239 = (f32[64,512]{1,0:T(8,128)}, f32[64,384]{1,0:T(8,128)S(1)}, f32[128,128]{1,0:T(8,128)S(1)}) custom-call(f32[256,128]{1,0:T(8,128)S(1)} %pad_maximum_fusion.2.coef_ref, f32[64,384]{1,0:T(8,128)S(1)} %get-tuple-element.31.x_ref, f32[256,512]{1,0:T(8,128)S(1)} %copy-done, f32[8,512]{1,0:T(8,128)S(1)} %copy-done.5, f32[8,512]{1,0:T(8,128)S(1)} %copy-done.6, ...), custom_call_target="tpu_custom_call" | custom-call | flops 58720256 | bytes 1605632 | tf_op jit(solution)/shard_map/pallas_call | solution.py:79
  64.6 1.1 %collective-permute-done.23 = f32[64,128]{1,0:T(8,128)S(1)} collective-permute-done((f32[64,128]{1,0:T(8,128)S(1)}, f32[64,128]{1,0:T(8,128)S(1)}, u32[]{:S(2)}, u32[]{:S(2)}) %collective-permute-start.23) | collective-permute-done | bytes 32800 | tf_op jit(solution)/shard_map/ppermute | solution.py:175
  65.7 2.9 %collective-permute-start.25 = (f32[64,128]{1,0:T(8,128)S(1)}, f32[64,128]{1,0:T(8,128)S(1)}, u32[]{:S(2)}, u32[]{:S(2)}) collective-permute-start(f32[64,128]{1,0:T(8,128)S(1)} %select_add_fusion.1), channel_id=1, source_target_pairs={{0,16},{1,17},{2,18},{3,19},{4,20},{5,21},{6,22},{7,23},{8,24},{9,... | collective-permute-start | bytes 98312 | tf_op jit(solution)/shard_map/ppermute | solution.py:162
  68.6 1.5 %collective-permute-start.26 = (f32[64,128]{1,0:T(8,128)S(1)}, f32[64,128]{1,0:T(8,128)S(1)}, u32[]{:S(2)}, u32[]{:S(2)}) collective-permute-start(f32[64,128]{1,0:T(8,128)S(1)} %select_add_fusion.1), channel_id=1, source_target_pairs={{0,24},{1,25},{2,26},{3,27},{4,28},{5,29},{6,30},{7,31},{8,16},{9,... | collective-permute-start | bytes 98312 | tf_op jit(solution)/shard_map/ppermute | solution.py:162
  70.6 3.6 %collective-permute-done.26 = f32[64,128]{1,0:T(8,128)S(1)} collective-permute-done((f32[64,128]{1,0:T(8,128)S(1)}, f32[64,128]{1,0:T(8,128)S(1)}, u32[]{:S(2)}, u32[]{:S(2)}) %collective-permute-start.26) | collective-permute-done | bytes 32800 | tf_op jit(solution)/shard_map/ppermute | solution.py:162
  74.3 1.6 %collective-permute-start.27 = (f32[64,128]{1,0:T(8,128)S(1)}, f32[64,128]{1,0:T(8,128)S(1)}, u32[]{:S(2)}, u32[]{:S(2)}) collective-permute-start(f32[64,128]{1,0:T(8,128)S(1)} %add_add_fusion.1), channel_id=1, source_target_pairs={{0,2},{1,3},{2,0},{3,1},{4,6},{5,7},{6,4},{7,5},{8,10},{9,11},{10,... | collective-permute-start | bytes 98312 | tf_op jit(solution)/shard_map/ppermute | solution.py:162
  75.9 0.7 collective-permute-start.28
  76.6 1.2 %collective-permute-start.29 = (f32[64,128]{1,0:T(8,128)S(1)}, f32[64,128]{1,0:T(8,128)S(1)}, u32[]{:S(2)}, u32[]{:S(2)}) collective-permute-start(f32[64,128]{1,0:T(8,128)S(1)} %add_add_fusion.1), channel_id=1, source_target_pairs={{0,6},{1,7},{2,4},{3,5},{4,2},{5,3},{6,0},{7,1},{8,14},{9,15},{10,... | collective-permute-start | bytes 98312 | tf_op jit(solution)/shard_map/ppermute | solution.py:162
  77.8 0.7 collective-permute-done.27
  78.5 1.3 %collective-permute-done.28 = f32[64,128]{1,0:T(8,128)S(1)} collective-permute-done((f32[64,128]{1,0:T(8,128)S(1)}, f32[64,128]{1,0:T(8,128)S(1)}, u32[]{:S(2)}, u32[]{:S(2)}) %collective-permute-start.28) | collective-permute-done | bytes 32800 | tf_op jit(solution)/shard_map/ppermute | solution.py:162
  79.8 1.6 %collective-permute-done.29 = f32[64,128]{1,0:T(8,128)S(1)} collective-permute-done((f32[64,128]{1,0:T(8,128)S(1)}, f32[64,128]{1,0:T(8,128)S(1)}, u32[]{:S(2)}, u32[]{:S(2)}) %collective-permute-start.29) | collective-permute-done | bytes 32800 | tf_op jit(solution)/shard_map/ppermute | solution.py:162
  81.5 2.2 %shard_map.240.inverse_ref = f32[64,64]{1,0:T(8,128)S(1)} custom-call(f32[64,128]{1,0:T(8,128)S(1)} %add_multiply_fusion.1.half_ref), custom_call_target="tpu_custom_call" | custom-call | bytes 49152 | tf_op jit(solution)/shard_map/pallas_call | solution.py:79
  83.8 1.1 %shard_map.241 = (f32[64,256]{1,0:T(8,128)}, f32[8,64]{1,0:T(8,128)}, f32[8,64]{1,0:T(8,128)}, f32[64,64]{1,0:T(8,128)}, f32[64,64]{1,0:T(8,128)}) custom-call(s32[1]{0:T(128)} %bitcast.at_ref, f32[64,128]{1,0:T(8,128)S(1)} %add_multiply_fusion.1.half_ref, f32[64,128]{1,0:T(8,128)S(1)} %collective-permute-done.30.pair_ref, ...), custom_call_target="tpu_custom_call" | custom-call | flops 16777216 | bytes 282628 | tf_op jit(solution)/shard_map/pallas_call | solution.py:79
  (63 shorter events, 4.6 us)
Async XLA Ops:
  3.3 5.7 %collective-permute-start.10 = (f32[72,128]{1,0:T(8,128)}, f32[72,128]{1,0:T(8,128)S(1)}, u32[]{:S(2)}, u32[]{:S(2)}) collective-permute-start(f32[72,128]{1,0:T(8,128)} %get-tuple-element.26), channel_id=1, source_target_pairs={{0,8},{1,9},{2,10},{3,11},{4,12},{5,13},{6,14},{7,15},{8,0},{9,1},... | collective-permute-start | bytes 110600 | tf_op jit(solution)/shard_map/ppermute | solution.py:238
  6.4 6.5 %collective-permute-start.8 = (f32[72,128]{1,0:T(8,128)}, f32[72,128]{1,0:T(8,128)S(1)}, u32[]{:S(2)}, u32[]{:S(2)}) collective-permute-start(f32[72,128]{1,0:T(8,128)} %get-tuple-element.26), channel_id=1, source_target_pairs={{0,24},{1,25},{2,26},{3,27},{4,28},{5,29},{6,30},{7,31},{8,16},{9,... | collective-permute-start | bytes 110600 | tf_op jit(solution)/shard_map/ppermute | solution.py:238
  8.9 5.5 %collective-permute-start.9 = (f32[72,128]{1,0:T(8,128)}, f32[72,128]{1,0:T(8,128)S(1)}, u32[]{:S(2)}, u32[]{:S(2)}) collective-permute-start(f32[72,128]{1,0:T(8,128)} %get-tuple-element.26), channel_id=1, source_target_pairs={{0,16},{1,17},{2,18},{3,19},{4,20},{5,21},{6,22},{7,23},{8,24},{9,... | collective-permute-start | bytes 110600 | tf_op jit(solution)/shard_map/ppermute | solution.py:238
  15.2 7.7 %collective-permute-start.11 = (f32[288,128]{1,0:T(8,128)S(1)}, f32[288,128]{1,0:T(8,128)S(1)}, u32[]{:S(2)}, u32[]{:S(2)}) collective-permute-start(f32[288,128]{1,0:T(8,128)S(1)} %pad_maximum_fusion.1), channel_id=1, source_target_pairs={{0,6},{1,7},{2,4},{3,5},{4,2},{5,3},{6,0},{7,1},{8,14},{9,15},{10,... | collective-permute-start | bytes 442376 | tf_op jit(solution)/shard_map/ppermute | solution.py:238
  17.7 5.9 %collective-permute-start.12 = (f32[288,128]{1,0:T(8,128)S(1)}, f32[288,128]{1,0:T(8,128)S(1)}, u32[]{:S(2)}, u32[]{:S(2)}) collective-permute-start(f32[288,128]{1,0:T(8,128)S(1)} %pad_maximum_fusion.1), channel_id=1, source_target_pairs={{0,4},{1,5},{2,6},{3,7},{4,0},{5,1},{6,2},{7,3},{8,12},{9,13},{10,... | collective-permute-start | bytes 442376 | tf_op jit(solution)/shard_map/ppermute | solution.py:238
  18.2 5.5 %collective-permute-start.13 = (f32[288,128]{1,0:T(8,128)S(1)}, f32[288,128]{1,0:T(8,128)S(1)}, u32[]{:S(2)}, u32[]{:S(2)}) collective-permute-start(f32[288,128]{1,0:T(8,128)S(1)} %pad_maximum_fusion.1), channel_id=1, source_target_pairs={{0,2},{1,3},{2,0},{3,1},{4,6},{5,7},{6,4},{7,5},{8,10},{9,11},{10,... | collective-permute-start | bytes 442376 | tf_op jit(solution)/shard_map/ppermute | solution.py:238
  23.7 0.8 copy-start.11
  23.8 2.2 %copy-start.10 = (f32[64,128]{1,0:T(8,128)S(1)}, f32[64,128]{1,0:T(8,128)}, u32[]{:S(2)}) copy-start(f32[64,128]{1,0:T(8,128)} %get-tuple-element.24) | copy-start | bytes 98308
  23.8 18.2 %copy-start = (f32[256,512]{1,0:T(8,128)S(1)}, f32[256,512]{1,0:T(8,128)}, u32[]{:S(2)}) copy-start(f32[256,512]{1,0:T(8,128)} %q_leaf_ref.1) | copy-start | bytes 1572868
  23.8 18.2 %copy-start.4 = (f32[256,256]{1,0:T(8,128)S(1)}, f32[256,256]{1,0:T(8,128)}, u32[]{:S(2)}) copy-start(f32[256,256]{1,0:T(8,128)} %uinv_ref.1) | copy-start | bytes 786436
  23.8 18.1 %copy-start.3 = (f32[256,256]{1,0:T(8,128)S(1)}, f32[256,256]{1,0:T(8,128)}, u32[]{:S(2)}) copy-start(f32[256,256]{1,0:T(8,128)} %upper_ref.1) | copy-start | bytes 786436
  23.8 19.8 %collective-permute-start.14 = (f32[1152,128]{1,0:T(8,128)S(1)}, f32[1152,128]{1,0:T(8,128)S(1)}, u32[]{:S(2)}, u32[]{:S(2)}) collective-permute-start(f32[1152,128]{1,0:T(8,128)S(1)} %pad_maximum_fusion.mine_ref), channel_id=1, source_target_pairs={{0,1},{1,0},{2,3},{3,2},{4,5},{5,4},{6,7},{7,6},{8,9},{9,8},{10,11... | collective-permute-start | bytes 1769480 | tf_op jit(solution)/shard_map/ppermute | solution.py:175
  24.5 1.5 %collective-permute-start = (f32[64,128]{1,0:T(8,128)S(1)}, f32[64,128]{1,0:T(8,128)S(1)}, u32[]{:S(2)}, u32[]{:S(2)}) collective-permute-start(f32[64,128]{1,0:T(8,128)S(1)} %copy-done.11), channel_id=1, source_target_pairs={{0,1},{1,0},{2,3},{3,2},{4,5},{5,4},{6,7},{7,6},{8,9},{9,8},{10,11... | collective-permute-start | bytes 98312 | tf_op jit(solution)/shard_map/ppermute | solution.py:175
  26.0 4.0 %collective-permute-start.1 = (f32[64,128]{1,0:T(8,128)S(1)}, f32[64,128]{1,0:T(8,128)S(1)}, u32[]{:S(2)}, u32[]{:S(2)}) collective-permute-start(f32[64,128]{1,0:T(8,128)S(1)} %add.75), channel_id=1, source_target_pairs={{0,2},{1,3},{2,0},{3,1},{4,6},{5,7},{6,4},{7,5},{8,10},{9,11},{10,... | collective-permute-start | bytes 98312 | tf_op jit(solution)/shard_map/ppermute | solution.py:162
  27.6 4.3 %collective-permute-start.2 = (f32[64,128]{1,0:T(8,128)S(1)}, f32[64,128]{1,0:T(8,128)S(1)}, u32[]{:S(2)}, u32[]{:S(2)}) collective-permute-start(f32[64,128]{1,0:T(8,128)S(1)} %add.75), channel_id=1, source_target_pairs={{0,4},{1,5},{2,6},{3,7},{4,0},{5,1},{6,2},{7,3},{8,12},{9,13},{10,... | collective-permute-start | bytes 98312 | tf_op jit(solution)/shard_map/ppermute | solution.py:162
  28.3 4.8 %collective-permute-start.3 = (f32[64,128]{1,0:T(8,128)S(1)}, f32[64,128]{1,0:T(8,128)S(1)}, u32[]{:S(2)}, u32[]{:S(2)}) collective-permute-start(f32[64,128]{1,0:T(8,128)S(1)} %add.75), channel_id=1, source_target_pairs={{0,6},{1,7},{2,4},{3,5},{4,2},{5,3},{6,0},{7,1},{8,14},{9,15},{10,... | collective-permute-start | bytes 98312 | tf_op jit(solution)/shard_map/ppermute | solution.py:162
  33.1 8.8 %copy-start.7 = (f32[64,256]{1,0:T(8,128)S(1)}, f32[64,256]{1,0:T(8,128)}, u32[]{:S(2)}) copy-start(f32[64,256]{1,0:T(8,128)} %get-tuple-element.27.y_ref) | copy-start | bytes 196612
  33.1 4.5 %collective-permute-start.4 = (f32[64,128]{1,0:T(8,128)S(1)}, f32[64,128]{1,0:T(8,128)S(1)}, u32[]{:S(2)}, u32[]{:S(2)}) collective-permute-start(f32[64,128]{1,0:T(8,128)S(1)} %add_add_fusion.3), channel_id=1, source_target_pairs={{0,8},{1,9},{2,10},{3,11},{4,12},{5,13},{6,14},{7,15},{8,0},{9,1},... | collective-permute-start | bytes 98312 | tf_op jit(solution)/shard_map/ppermute | solution.py:162
  33.6 4.8 %collective-permute-start.5 = (f32[64,128]{1,0:T(8,128)S(1)}, f32[64,128]{1,0:T(8,128)S(1)}, u32[]{:S(2)}, u32[]{:S(2)}) collective-permute-start(f32[64,128]{1,0:T(8,128)S(1)} %add_add_fusion.3), channel_id=1, source_target_pairs={{0,16},{1,17},{2,18},{3,19},{4,20},{5,21},{6,22},{7,23},{8,24},{9,... | collective-permute-start | bytes 98312 | tf_op jit(solution)/shard_map/ppermute | solution.py:162
  36.1 5.7 %collective-permute-start.6 = (f32[64,128]{1,0:T(8,128)S(1)}, f32[64,128]{1,0:T(8,128)S(1)}, u32[]{:S(2)}, u32[]{:S(2)}) collective-permute-start(f32[64,128]{1,0:T(8,128)S(1)} %add_add_fusion.3), channel_id=1, source_target_pairs={{0,24},{1,25},{2,26},{3,27},{4,28},{5,29},{6,30},{7,31},{8,16},{9,... | collective-permute-start | bytes 98312 | tf_op jit(solution)/shard_map/ppermute | solution.py:162
  41.8 0.7 copy-start.5
  41.8 1.8 %collective-permute-start.7 = (f32[64,128]{1,0:T(8,128)S(1)}, f32[64,128]{1,0:T(8,128)S(1)}, u32[]{:S(2)}, u32[]{:S(2)}) collective-permute-start(f32[64,128]{1,0:T(8,128)S(1)} %add_add_fusion.2.half_ref), channel_id=1, source_target_pairs={{0,1},{1,0},{2,3},{3,2},{4,5},{5,4},{6,7},{7,6},{8,9},{9,8},{10,11... | collective-permute-start | bytes 98312 | tf_op jit(solution)/shard_map/ppermute | solution.py:175
  41.9 0.7 copy-start.8
  42.6 1.1 %copy-start.6 = (f32[8,512]{1,0:T(8,128)S(1)}, f32[8,512]{1,0:T(8,128)}, u32[]{:S(2)}) copy-start(f32[8,512]{1,0:T(8,128)} %q_root_ref.3) | copy-start | bytes 49156
  45.2 16.9 %copy-start.1 = (f32[1024,128]{1,0:T(8,128)S(1)}, f32[1024,128]{1,0:T(8,128)}, u32[]{:S(2)}) copy-start(f32[1024,128]{1,0:T(8,128)} %g_ref.1) | copy-start | bytes 1572868
  45.3 16.9 %copy-start.2 = (f32[1024,128]{1,0:T(8,128)S(1)}, f32[1024,128]{1,0:T(8,128)}, u32[]{:S(2)}) copy-start(f32[1024,128]{1,0:T(8,128)} %c_ref.1) | copy-start | bytes 1572868
  45.3 1.5 %collective-permute-start.15 = (f32[128,128]{1,0:T(8,128)S(1)}, f32[128,128]{1,0:T(8,128)S(1)}, u32[]{:S(2)}, u32[]{:S(2)}) collective-permute-start(f32[128,128]{1,0:T(8,128)S(1)} %slice_select_fusion), channel_id=1, source_target_pairs={{0,1},{1,0},{2,3},{3,2},{4,5},{5,4},{6,7},{7,6},{8,9},{9,8},{10,11... | collective-permute-start | bytes 196616 | tf_op jit(solution)/shard_map/ppermute | solution.py:175
  46.7 4.4 %collective-permute-start.16 = (f32[128,128]{1,0:T(8,128)S(1)}, f32[128,128]{1,0:T(8,128)S(1)}, u32[]{:S(2)}, u32[]{:S(2)}) collective-permute-start(f32[128,128]{1,0:T(8,128)S(1)} %select_add_fusion), channel_id=1, source_target_pairs={{0,2},{1,3},{2,0},{3,1},{4,6},{5,7},{6,4},{7,5},{8,10},{9,11},{10,... | collective-permute-start | bytes 196616 | tf_op jit(solution)/shard_map/ppermute | solution.py:162
  48.0 5.0 %collective-permute-start.17 = (f32[128,128]{1,0:T(8,128)S(1)}, f32[128,128]{1,0:T(8,128)S(1)}, u32[]{:S(2)}, u32[]{:S(2)}) collective-permute-start(f32[128,128]{1,0:T(8,128)S(1)} %select_add_fusion), channel_id=1, source_target_pairs={{0,4},{1,5},{2,6},{3,7},{4,0},{5,1},{6,2},{7,3},{8,12},{9,13},{10,... | collective-permute-start | bytes 196616 | tf_op jit(solution)/shard_map/ppermute | solution.py:162
  48.6 5.2 %collective-permute-start.18 = (f32[128,128]{1,0:T(8,128)S(1)}, f32[128,128]{1,0:T(8,128)S(1)}, u32[]{:S(2)}, u32[]{:S(2)}) collective-permute-start(f32[128,128]{1,0:T(8,128)S(1)} %select_add_fusion), channel_id=1, source_target_pairs={{0,6},{1,7},{2,4},{3,5},{4,2},{5,3},{6,0},{7,1},{8,14},{9,15},{10,... | collective-permute-start | bytes 196616 | tf_op jit(solution)/shard_map/ppermute | solution.py:162
  53.8 8.3 %copy-start.9 = (s32[2,4]{1,0:T(2,128)S(1)}, s32[2,4]{1,0:T(2,128)}, u32[]{:S(2)}) copy-start(s32[2,4]{1,0:T(2,128)} %cols_ref.1) | copy-start | bytes 100
  53.8 4.5 %collective-permute-start.19 = (f32[128,128]{1,0:T(8,128)S(1)}, f32[128,128]{1,0:T(8,128)S(1)}, u32[]{:S(2)}, u32[]{:S(2)}) collective-permute-start(f32[128,128]{1,0:T(8,128)S(1)} %add_add_fusion), channel_id=1, source_target_pairs={{0,8},{1,9},{2,10},{3,11},{4,12},{5,13},{6,14},{7,15},{8,0},{9,1},... | collective-permute-start | bytes 196616 | tf_op jit(solution)/shard_map/ppermute | solution.py:162
  53.9 5.9 %collective-permute-start.20 = (f32[128,128]{1,0:T(8,128)S(1)}, f32[128,128]{1,0:T(8,128)S(1)}, u32[]{:S(2)}, u32[]{:S(2)}) collective-permute-start(f32[128,128]{1,0:T(8,128)S(1)} %add_add_fusion), channel_id=1, source_target_pairs={{0,16},{1,17},{2,18},{3,19},{4,20},{5,21},{6,22},{7,23},{8,24},{9,... | collective-permute-start | bytes 196616 | tf_op jit(solution)/shard_map/ppermute | solution.py:162
  56.0 6.1 %collective-permute-start.21 = (f32[128,128]{1,0:T(8,128)S(1)}, f32[128,128]{1,0:T(8,128)S(1)}, u32[]{:S(2)}, u32[]{:S(2)}) collective-permute-start(f32[128,128]{1,0:T(8,128)S(1)} %add_add_fusion), channel_id=1, source_target_pairs={{0,24},{1,25},{2,26},{3,27},{4,28},{5,29},{6,30},{7,31},{8,16},{9,... | collective-permute-start | bytes 196616 | tf_op jit(solution)/shard_map/ppermute | solution.py:162
  62.0 1.3 %collective-permute-start.22 = (f32[128,128]{1,0:T(8,128)S(1)}, f32[128,128]{1,0:T(8,128)S(1)}, u32[]{:S(2)}, u32[]{:S(2)}) collective-permute-start(f32[128,128]{1,0:T(8,128)S(1)} %add_multiply_fusion), channel_id=1, source_target_pairs={{0,1},{1,0},{2,3},{3,2},{4,5},{5,4},{6,7},{7,6},{8,9},{9,8},{10,11... | collective-permute-start | bytes 196616 | tf_op jit(solution)/shard_map/ppermute | solution.py:175
  64.5 1.2 %collective-permute-start.23 = (f32[64,128]{1,0:T(8,128)S(1)}, f32[64,128]{1,0:T(8,128)S(1)}, u32[]{:S(2)}, u32[]{:S(2)}) collective-permute-start(f32[64,128]{1,0:T(8,128)S(1)} %slice_select_fusion.1), channel_id=1, source_target_pairs={{0,1},{1,0},{2,3},{3,2},{4,5},{5,4},{6,7},{7,6},{8,9},{9,8},{10,11... | collective-permute-start | bytes 98312 | tf_op jit(solution)/shard_map/ppermute | solution.py:175
  65.7 4.4 %collective-permute-start.24 = (f32[64,128]{1,0:T(8,128)S(1)}, f32[64,128]{1,0:T(8,128)S(1)}, u32[]{:S(2)}, u32[]{:S(2)}) collective-permute-start(f32[64,128]{1,0:T(8,128)S(1)} %select_add_fusion.1), channel_id=1, source_target_pairs={{0,8},{1,9},{2,10},{3,11},{4,12},{5,13},{6,14},{7,15},{8,0},{9,1},... | collective-permute-start | bytes 98312 | tf_op jit(solution)/shard_map/ppermute | solution.py:162
  65.7 4.9 %collective-permute-start.25 = (f32[64,128]{1,0:T(8,128)S(1)}, f32[64,128]{1,0:T(8,128)S(1)}, u32[]{:S(2)}, u32[]{:S(2)}) collective-permute-start(f32[64,128]{1,0:T(8,128)S(1)} %select_add_fusion.1), channel_id=1, source_target_pairs={{0,16},{1,17},{2,18},{3,19},{4,20},{5,21},{6,22},{7,23},{8,24},{9,... | collective-permute-start | bytes 98312 | tf_op jit(solution)/shard_map/ppermute | solution.py:162
  68.6 5.7 %collective-permute-start.26 = (f32[64,128]{1,0:T(8,128)S(1)}, f32[64,128]{1,0:T(8,128)S(1)}, u32[]{:S(2)}, u32[]{:S(2)}) collective-permute-start(f32[64,128]{1,0:T(8,128)S(1)} %select_add_fusion.1), channel_id=1, source_target_pairs={{0,24},{1,25},{2,26},{3,27},{4,28},{5,29},{6,30},{7,31},{8,16},{9,... | collective-permute-start | bytes 98312 | tf_op jit(solution)/shard_map/ppermute | solution.py:162
  74.3 4.2 %collective-permute-start.27 = (f32[64,128]{1,0:T(8,128)S(1)}, f32[64,128]{1,0:T(8,128)S(1)}, u32[]{:S(2)}, u32[]{:S(2)}) collective-permute-start(f32[64,128]{1,0:T(8,128)S(1)} %add_add_fusion.1), channel_id=1, source_target_pairs={{0,2},{1,3},{2,0},{3,1},{4,6},{5,7},{6,4},{7,5},{8,10},{9,11},{10,... | collective-permute-start | bytes 98312 | tf_op jit(solution)/shard_map/ppermute | solution.py:162
  75.9 3.9 %collective-permute-start.28 = (f32[64,128]{1,0:T(8,128)S(1)}, f32[64,128]{1,0:T(8,128)S(1)}, u32[]{:S(2)}, u32[]{:S(2)}) collective-permute-start(f32[64,128]{1,0:T(8,128)S(1)} %add_add_fusion.1), channel_id=1, source_target_pairs={{0,4},{1,5},{2,6},{3,7},{4,0},{5,1},{6,2},{7,3},{8,12},{9,13},{10,... | collective-permute-start | bytes 98312 | tf_op jit(solution)/shard_map/ppermute | solution.py:162
  76.6 4.8 %collective-permute-start.29 = (f32[64,128]{1,0:T(8,128)S(1)}, f32[64,128]{1,0:T(8,128)S(1)}, u32[]{:S(2)}, u32[]{:S(2)}) collective-permute-start(f32[64,128]{1,0:T(8,128)S(1)} %add_add_fusion.1), channel_id=1, source_target_pairs={{0,6},{1,7},{2,4},{3,5},{4,2},{5,3},{6,0},{7,1},{8,14},{9,15},{10,... | collective-permute-start | bytes 98312 | tf_op jit(solution)/shard_map/ppermute | solution.py:162
  81.4 2.3 %collective-permute-start.30 = (f32[64,128]{1,0:T(8,128)S(1)}, f32[64,128]{1,0:T(8,128)S(1)}, u32[]{:S(2)}, u32[]{:S(2)}) collective-permute-start(f32[64,128]{1,0:T(8,128)S(1)} %add_multiply_fusion.1.half_ref), channel_id=1, source_target_pairs={{0,1},{1,0},{2,3},{3,2},{4,5},{5,4},{6,7},{7,6},{8,9},{9,8},{10,11... | collective-permute-start | bytes 98312 | tf_op jit(solution)/shard_map/ppermute | solution.py:175
